TPU v7x, 256 devices: a whole 4x4x8 slice. The times are simulated.
256 devices in a mesh: grid: 16 (over y, x), mic: 4 (over z_hi), bin: 4 (over z_lo, core).
Axes of the slice: x: 4, y: 4, z: 8 (z_hi: 4, z_lo: 2; z = z_hi * 2 + z_lo), core: 2. Of those that a mesh axis runs over, the one named last changes fastest.
Arguments:
- grid_points: float32 [3, 16384], P(None, 'grid'), may hold values from -1 to 3, as said below
- mic_coords: float32 [3, 4096], P(None, 'mic'), may hold values from -1 to 1, as said below
- wavenumbers: float32 [16], P('bin'), may hold values from 20 to 150
- pressures: float32 [16, 2, 16, 4096], P('bin', None, None, 'mic'), may hold values from -6 to 6
Outputs:
- solution: float32 [16, 2, 16, 16384], P('bin', None, None, 'grid')
- residual: float32 [16, 2, 16, 4096], P('bin', None, None, 'mic')
Inputs may be any that keep to these rules, and one draw needn't show every extreme that they name: `grid_points`: rows 0 and 1 lie in -1 to 1, row 2 in 1 to 3. `mic_coords`: rows 0 and 1 lie in -1 to 1, row 2 in -0.05 to 0.05.
All inputs are finite; a program needn't handle non-finite values.
Results may differ from a plain program's by a relative error of at most 0.0055.
Values may be sent and summed in bfloat16 or wider, within the bound.
No kernel may reach another device: no remote copies, remote signals or barrier semaphores. Data moves between devices by JAX's collectives and lax.ppermute only.
A program may use at most 64 MiB of HBM per device.

v0:
```python
import math

import jax
import jax.numpy as jnp
from jax import lax
from jax.sharding import PartitionSpec as P

ITERS = 2


def steering_tiles(grid_points, mic_coords, wavenumbers, norm_scale):
    dist_x = grid_points[0][:, None] - mic_coords[0][None, :]
    dist_y = grid_points[1][:, None] - mic_coords[1][None, :]
    dist_z = grid_points[2][:, None] - mic_coords[2][None, :]
    radius = jnp.sqrt(dist_x * dist_x + dist_y * dist_y + dist_z * dist_z)
    amplitude = norm_scale / radius
    cos_list = []
    sin_list = []
    for bin_index in range(wavenumbers.shape[0]):
        phase_angle = wavenumbers[bin_index] * radius
        cos_list.append((jnp.cos(phase_angle) * amplitude).astype(jnp.bfloat16))
        sin_list.append((jnp.sin(phase_angle) * amplitude).astype(jnp.bfloat16))
    return (jnp.stack(cos_list), jnp.stack(sin_list))


def body(grid_points, mic_coords, wavenumbers, pressures):
    bin_count = pressures.shape[0]
    snap_count = pressures.shape[2]
    grid_local = grid_points.shape[1]
    norm_scale = 1.0 / math.sqrt(grid_local * lax.axis_size("grid"))
    cos_tiles, sin_tiles = steering_tiles(grid_points, mic_coords, wavenumbers, norm_scale)

    def combine_adjoint(cos_sum, sin_sum):
        real_part = cos_sum[:, :snap_count] - sin_sum[:, snap_count:]
        imag_part = cos_sum[:, snap_count:] + sin_sum[:, :snap_count]
        return jnp.stack([real_part, imag_part], axis=1)

    def apply_adjoint(residual):
        rounded = residual.astype(jnp.bfloat16).reshape(
            bin_count, 2 * snap_count, residual.shape[3]
        )
        cos_sum = jnp.einsum("fkm,fgm->fkg", rounded, cos_tiles, preferred_element_type=jnp.float32)
        sin_sum = jnp.einsum("fkm,fgm->fkg", rounded, sin_tiles, preferred_element_type=jnp.float32)
        partial_terms = combine_adjoint(cos_sum, sin_sum)
        summed = lax.psum(partial_terms, "mic")
        grad_norm = lax.psum(jnp.sum(summed * summed), ("grid", "bin"))
        return (summed, grad_norm)

    residual = pressures
    gradient, grad_norm = apply_adjoint(residual)
    direction = gradient
    solution = jnp.zeros_like(gradient)
    for iteration in range(ITERS):
        apply_rounded = direction.astype(jnp.bfloat16).reshape(
            bin_count, 2 * snap_count, direction.shape[3]
        )
        apply_cos_sum = jnp.einsum(
            "fkg,fgm->fkm", apply_rounded, cos_tiles, preferred_element_type=jnp.float32
        )
        apply_sin_sum = jnp.einsum(
            "fkg,fgm->fkm", apply_rounded, sin_tiles, preferred_element_type=jnp.float32
        )
        combine_real_part = apply_cos_sum[:, :snap_count] + apply_sin_sum[:, snap_count:]
        combine_imag_part = apply_cos_sum[:, snap_count:] - apply_sin_sum[:, :snap_count]
        apply_partial_terms = jnp.stack([combine_real_part, combine_imag_part], axis=1)
        apply_summed = lax.psum(apply_partial_terms, "grid")
        image_norm = lax.psum(jnp.sum(apply_summed * apply_summed), ("mic", "bin"))
        image, image_norm = (apply_summed, image_norm)
        step_size = grad_norm / image_norm
        solution = solution + step_size * direction
        residual = residual - step_size * image
        if iteration + 1 < ITERS:
            gradient, next_norm = apply_adjoint(residual)
            direction = gradient + next_norm / grad_norm * direction
            grad_norm = next_norm
    return (solution, residual)


def solution(mesh):
    placed = (P(None, "grid"), P(None, "mic"), P("bin"), P("bin", None, None, "mic"))
    return jax.shard_map(
        body,
        mesh=mesh,
        in_specs=placed,
        out_specs=(P("bin", None, None, "grid"), P("bin", None, None, "mic")),
        check_vma=False,
    )
```

profile of v0, /device:TPU:1, one launch (start us, length us, event | category | flops | bytes accessed | tf_op | source)
XLA Modules:
  0.0 768.9 jit_solution(6533060130410521625)
XLA Ops:
  7.2 0.0 all-reduce.5.cloned.1.call-start
  7.2 1.5 fusion.13
  8.7 0.8 fusion.11
  9.5 0.8 fusion.12
  10.4 1.1 convert_element_type.96
  11.5 67.4 %multiply_convert_fusion.7 = (bf16[1,1024,1024]{2,1,0:T(8,128)(2,1)S(1)}, bf16[1,1024,1024]{2,1,0:T(8,128)(2,1)S(1)}, bf16[1,1024,1024]{2,1,0:T(8,128)(2,1)S(1)}...) fusion(f32[1024]{0:T(1024)S(1)} %bitcast.62, ...), kind=kLoop, calls=%fused_computation.9 | loop fusion | flops 30408704 | bytes 16801808 | tf_op jit(solution)/shard_map/convert_element_type | solution.py:21
  78.9 2.4 pad_maximum_fusion
  81.3 2.6 convolution_bitcast_fusion
  83.9 0.6 copy-done
  84.5 2.5 copy-done.2
  87.0 2.6 convolution_bitcast_fusion.1
  89.6 0.1 fusion.8
  89.6 0.8 pad_maximum_fusion.2
  90.5 0.0 all-reduce.5.cloned.1.call-update
  90.5 0.0 all-reduce.7.cloned.1.call-start
  90.6 56.2 %all-reduce.5.cloned.1.call-done = f32[4,2,16,1024]{3,2,0,1:T(8,128)} async-done(((f32[4,2,16,1024]{3,2,0,1:T(8,128)}), f32[4,2,16,1024]{3,2,0,1:T(8,128)}) %all-reduce.5.cloned.1.call-update) | async-done | bytes 524304 | tf_op jit(solution)/shard_map/psum | solution.py:45
  146.7 1.9 multiply_reduce_fusion.3
  148.7 5.1 fusion.14
  153.8 0.7 copy-done.1
  154.5 1.5 fusion.15
  156.0 0.1 fusion.6
  156.1 0.8 pad_maximum_fusion.3
  156.9 0.0 all-reduce.9.cloned.1.call-start
  157.0 94.4 %all-reduce.7.cloned.1.call-done = f32[4,2,16,1024]{3,2,0,1:T(8,128)} async-done(((f32[4,2,16,1024]{3,2,0,1:T(8,128)}), f32[4,2,16,1024]{3,2,0,1:T(8,128)}) %all-reduce.7.cloned.1.call-update) | async-done | bytes 524304 | tf_op jit(solution)/shard_map/psum | solution.py:66
  251.4 1.8 multiply_reduce_fusion.2
  253.2 140.4 %psum.57 = f32[]{:T(128)} all-reduce(f32[]{:T(128)} %get-tuple-element.14), channel_id=1, replica_groups=mesh['grid'=16,'mic'=4,'bin'=4] {'grid','bin'}, use_global_device_ids=true, to_apply=%region_2.0 | all-reduce | flops 1 | bytes 8 | tf_op jit(solution)/shard_map/psum | solution.py:46
  393.6 25.9 %psum.59 = f32[]{:T(128)} all-reduce(f32[]{:T(128)} %multiply_reduce_fusion.2), channel_id=1, replica_groups=mesh['grid'=16,'mic'=4,'bin'=4] {'mic','bin'}, use_global_device_ids=true, to_apply=%region_5.0 | all-reduce | flops 1 | bytes 8 | tf_op jit(solution)/shard_map/psum | solution.py:67
  420.8 1.1 fusion.10
  422.0 5.9 fusion.16
  427.9 6.0 fusion.17
  434.0 0.1 fusion.4
  434.0 0.8 pad_maximum_fusion.4
  434.9 0.0 all-reduce.11.cloned.1.call-start
  434.9 47.9 %all-reduce.9.cloned.1.call-done = f32[4,2,16,1024]{3,2,0,1:T(8,128)} async-done(((f32[4,2,16,1024]{3,2,0,1:T(8,128)}), f32[4,2,16,1024]{3,2,0,1:T(8,128)}) %all-reduce.9.cloned.1.call-update) | async-done | bytes 524304 | tf_op jit(solution)/shard_map/psum | solution.py:45
  482.8 1.8 multiply_reduce_fusion.1
  484.6 140.7 %psum.61 = f32[]{:T(128)} all-reduce(f32[]{:T(128)} %multiply_reduce_fusion.1), channel_id=1, replica_groups=mesh['grid'=16,'mic'=4,'bin'=4] {'grid','bin'}, use_global_device_ids=true, to_apply=%region_8.0 | all-reduce | flops 1 | bytes 8 | tf_op jit(solution)/shard_map/psum | solution.py:46
  626.6 1.1 fusion.9
  627.8 4.9 fusion.18
  632.7 5.0 fusion.19
  637.7 0.1 fusion.2
  637.8 0.8 pad_maximum_fusion.5
  638.6 91.7 %all-reduce.11.cloned.1.call-done = f32[4,2,16,1024]{3,2,0,1:T(8,128)} async-done(((f32[4,2,16,1024]{3,2,0,1:T(8,128)}), f32[4,2,16,1024]{3,2,0,1:T(8,128)}) %all-reduce.11.cloned.1.call-update) | async-done | bytes 524304 | tf_op jit(solution)/shard_map/psum | solution.py:66
  730.4 1.8 multiply_reduce_fusion
  732.1 26.0 %psum.63 = f32[]{:T(128)} all-reduce(f32[]{:T(128)} %multiply_reduce_fusion), channel_id=1, replica_groups=mesh['grid'=16,'mic'=4,'bin'=4] {'mic','bin'}, use_global_device_ids=true, to_apply=%region_11.0 | all-reduce | flops 1 | bytes 8 | tf_op jit(solution)/shard_map/psum | solution.py:67
  759.4 1.2 multiply_subtract_fusion
  760.6 0.8 copy.14
  761.5 0.1 multiply_add_fusion
  761.6 0.8 copy.13
  (17 shorter events, 0.1 us)
Async XLA Ops:
  7.2 139.6 %all-reduce.5.cloned.1.call-start = ((), (), s32[]{:S(2)}) async-start(), calls=%async_computation | async-start | bytes 1048576 | tf_op jit(solution)/shard_map/psum | solution.py:45
  81.3 3.2 copy-start
  81.3 5.7 copy-start.2
  90.5 160.9 %all-reduce.7.cloned.1.call-start = ((), (), s32[]{:S(2)}) async-start(), calls=%async_computation.1 | async-start | bytes 1048576 | tf_op jit(solution)/shard_map/psum | solution.py:66
  148.7 5.8 copy-start.1
  154.5 266.4 %copy-start.5 = (f32[4,2,16,1024]{3,2,1,0:T(8,128)S(1)}, f32[4,2,16,1024]{3,2,1,0:T(8,128)}, u32[]{:S(2)}) copy-start(f32[4,2,16,1024]{3,2,1,0:T(8,128)} %param.7) | copy-start | bytes 1572868
  156.9 325.9 %all-reduce.9.cloned.1.call-start = ((), (), s32[]{:S(2)}) async-start(), calls=%async_computation.2 | async-start | bytes 1048576 | tf_op jit(solution)/shard_map/psum | solution.py:45
  427.9 198.7 %copy-start.3 = (f32[4,2,16,1024]{3,2,0,1:T(8,128)S(1)}, f32[4,2,16,1024]{3,2,0,1:T(8,128)}, u32[]{:S(2)}) copy-start(f32[4,2,16,1024]{3,2,0,1:T(8,128)} %all-reduce.5.cloned.1.call-done) | copy-start | bytes 1572868
  434.9 295.5 %all-reduce.11.cloned.1.call-start = ((), (), s32[]{:S(2)}) async-start(), calls=%async_computation.3 | async-start | bytes 1048576 | tf_op jit(solution)/shard_map/psum | solution.py:66
  632.7 126.7 %copy-start.6 = (f32[4,2,16,1024]{3,2,0,1:T(8,128)S(1)}, f32[4,2,16,1024]{3,2,0,1:T(8,128)}, u32[]{:S(2)}) copy-start(f32[4,2,16,1024]{3,2,0,1:T(8,128)} %all-reduce.7.cloned.1.call-done) | copy-start | bytes 1572868
  637.7 123.8 %copy-start.4 = (f32[4,2,16,1024]{3,2,0,1:T(8,128)S(1)}, f32[4,2,16,1024]{3,2,0,1:T(8,128)}, u32[]{:S(2)}) copy-start(f32[4,2,16,1024]{3,2,0,1:T(8,128)} %all-reduce.9.cloned.1.call-done) | copy-start | bytes 1572868
Sparse Core Ops, SparseCore 0:
  90.6 56.0 all-reduce.4
  157.1 94.3 all-reduce.6
  435.0 47.7 all-reduce.8
  638.7 91.5 all-reduce.10
where the time goes:
time: 770 us; the launch traced here: 769 us
  blocking collectives  333 us (43%)
  waiting for transfers between devices  290 us (38%)
  other arithmetic  85.2 us (11%)
  matrix products  33.6 us (4%)
  between operations  17.9 us (2%)
  local copies, waits for them, and re-layouts  8.73 us (1%)
    psum x2, blocking collectives, apply_adjoint(): grad_norm = lax.psum(jnp.sum(summed * summed), ('grid', 'bin'))  281 us
    psum x2, waiting for transfers between devices, body(): apply_summed = lax.psum(apply_partial_terms, 'grid')  186 us
    psum x2, waiting for transfers between devices, apply_adjoint(): summed = lax.psum(partial_terms, 'mic')  104 us
    convert_element_type x1, other arithmetic, steering_tiles(): cos_list.append((jnp.cos(phase_angle) * amplitude).astype(jnp.bfloat16))  67.4 us
    psum x2, blocking collectives, body(): image_norm = lax.psum(jnp.sum(apply_summed * apply_summed), ('mic', 'bin'))  51.9 us
  transfers between devices with their start and end apart: 4, of which 4 were waited for; matrix products, arithmetic and copies ran while one was open for 0% of the time, Pallas kernels for 0%

commit v1 on v0

v1 whole, which is shorter than its diff:
```python
import functools
import math

import jax
import jax.numpy as jnp
from jax import lax
from jax.experimental import pallas as pl
from jax.experimental.pallas import tpu as pltpu
from jax.sharding import PartitionSpec as P

F32, BF16 = jnp.float32, jnp.bfloat16
SIN_POLY = (4.442883014678955, -7.308245658874512, 3.6063544750213623, -0.8461129069328308, 0.10982698947191238)
COS_POLY = (1.4142135381698608, -6.978850841522217, 5.7394609451293945, -1.8835630416870117, 0.31069818139076233)
ROUNDER = 12582912.0
ROWS, LANES, UNROLL = 32, 256, 2
STEP = 128


def steering(gx, gy, gz, mx, my, mz, turns):
    dx, dy, dz = gx - mx, gy - my, gz - mz
    square = dx * dx + dy * dy + dz * dz
    inverse = lax.rsqrt(square)
    cycles = (square * inverse) * turns
    part = cycles - ((cycles + ROUNDER) - ROUNDER)
    t = part * part
    s = SIN_POLY[4]
    c = COS_POLY[4]
    for k in (3, 2, 1, 0):
        s = s * t + SIN_POLY[k]
        c = c * t + COS_POLY[k]
    s = s * part
    scaled = s * inverse
    return (inverse - scaled * s).astype(BF16), (scaled * c).astype(BF16)


def dot_nt(a, b):
    return lax.dot_general(a, b, (((1,), (1,)), ((), ())), preferred_element_type=F32)


def dot_nn(a, b):
    return lax.dot_general(a, b, (((1,), (0,)), ((), ())), preferred_element_type=F32)


def store_image(out_ref, image, scale):
    for s in range(out_ref.shape[2]):
        for c in range(8):
            for h in range(2):
                lo = s * 1024 + c * 128
                out_ref[c, h, s] = image[h * 16 : h * 16 + 16, lo : lo + 128] * scale


def lane_sums(x):
    return jnp.sum(x, axis=0, keepdims=True)


def first_kernel(scale, turns_ref, grid_ref, p0, p1, p2, p3, cos_ref, sin_ref, grad_ref, image_ref, wc, ws, image):
    step = pl.program_id(0)
    packs = (p0, p1, p2, p3)

    @pl.when(step == 0)
    def _():
        for s in range(4):
            w = packs[s][0:32, :].astype(BF16)
            cols = slice(s * 1024, s * 1024 + 1024)
            wc[:, cols] = w
            ws[0:16, cols] = -w[16:32]
            ws[16:32, cols] = w[0:16]
        image[...] = jnp.zeros_like(image)

    turns = turns_ref[0]
    for s in range(4):

        def rows(i, carry, s=s):
            r0 = pl.multiple_of(i * ROWS, ROWS)
            g = [jnp.broadcast_to(grid_ref[pl.ds(r0, ROWS), d : d + 1], (ROWS, LANES)) for d in range(3)]

            def lanes(j, carry):
                for q in range(UNROLL):
                    l0 = pl.multiple_of((j * UNROLL + q) * LANES, LANES)
                    m = [packs[s][32 + d : 33 + d, pl.ds(l0, LANES)] for d in range(3)]
                    c, sn = steering(*g, *m, turns)
                    o0 = pl.multiple_of(l0 + s * 1024, LANES)
                    cos_ref[pl.ds(r0, ROWS), pl.ds(o0, LANES)] = c
                    sin_ref[pl.ds(r0, ROWS), pl.ds(o0, LANES)] = sn
                return carry

            return lax.fori_loop(0, 1024 // (LANES * UNROLL), lanes, carry)

        lax.fori_loop(0, STEP // ROWS, rows, 0)

    grad = (dot_nt(wc[...], cos_ref[...]) + dot_nt(ws[...], sin_ref[...])) * scale
    grad_ref[...] = grad
    v = grad.astype(BF16)
    v2 = jnp.concatenate([v[16:32], -v[0:16]], axis=0)
    image[...] += dot_nn(v, cos_ref[...]) + dot_nn(v2, sin_ref[...])

    @pl.when(step == pl.num_programs(0) - 1)
    def _():
        store_image(image_ref, image, scale)


def second_kernel(scale, q_ref, cos_ref, sin_ref, grad0_ref, grad_ref, image_ref, sums_ref, wc, ws, image):
    step = pl.program_id(0)

    @pl.when(step == 0)
    def _():
        for s in range(4):
            for c in range(8):
                cols = slice(s * 1024 + c * 128, s * 1024 + c * 128 + 128)
                real, imag = q_ref[2 * c, s], q_ref[2 * c + 1, s]
                wc[0:16, cols] = real
                wc[16:32, cols] = imag
                ws[0:16, cols] = -imag
                ws[16:32, cols] = real
        image[...] = jnp.zeros_like(image)
        sums_ref[...] = jnp.zeros_like(sums_ref)

    grad = (dot_nt(wc[...], cos_ref[...]) + dot_nt(ws[...], sin_ref[...])) * scale
    grad_ref[...] = grad
    g0 = grad0_ref[...]
    sums_ref[0:1] += lane_sums(g0 * g0)
    sums_ref[1:2] += lane_sums(g0 * grad)
    sums_ref[2:3] += lane_sums(grad * grad)
    v = grad.astype(BF16)
    v2 = jnp.concatenate([v[16:32], -v[0:16]], axis=0)
    image[...] += dot_nn(v, cos_ref[...]) + dot_nn(v2, sin_ref[...])

    @pl.when(step == pl.num_programs(0) - 1)
    def _():
        store_image(image_ref, image, scale)


def gather_kernel(parts_ref, shard_ref, copies_ref):
    total = parts_ref[0]
    for j in range(1, 16):
        total += parts_ref[j]
    shard_ref[...] = total
    low = total.astype(BF16)
    for j in range(16):
        copies_ref[j] = low


def spread_kernel(mic_ref, parts_ref, q_ref, sums_ref, out_ref, shard):
    total = parts_ref[0]
    for j in range(1, 16):
        total += parts_ref[j]
    shard[...] = total
    q = q_ref[...]
    flat = lambda x: lane_sums(x.reshape(64, 128))
    sums = jnp.concatenate(
        [sums_ref[0:3], flat(q * q), flat(q * total), flat(total * total), jnp.zeros((2, 128), F32)], axis=0
    )
    for t in range(4):
        s = lax.rem(t + 4 - mic_ref[0], 4)
        a, b = q_ref[s], shard[s]
        for j in range(16):
            out_ref[j * 4 + t, 0:16] = a
            out_ref[j * 4 + t, 16:32] = b
            out_ref[j * 4 + t, 32:40] = sums


def local_sums_kernel(recv_ref, out_ref):
    total = recv_ref[0, 32:40]
    for j in range(1, 64):
        total += recv_ref[j, 32:40]
    out_ref[...] = total


def last_kernel(mic_ref, sums_ref, recv_ref, press_ref, h0, h1, h2, h3, x_ref, r_ref):
    total = jnp.sum(sums_ref[...], axis=1, keepdims=True)
    gg, gh, hh, qq, qp, pp = [total[i : i + 1] for i in range(6)]
    step0 = gg / qq
    norm1 = gg - 2.0 * step0 * gh + step0 * step0 * hh
    ratio = norm1 / gg
    image1 = (1.0 + ratio) * (1.0 + ratio) * qq - 2.0 * (1.0 + ratio) * step0 * qp + step0 * step0 * pp
    step1 = norm1 / image1
    lead = jnp.broadcast_to(step0 + step1 * (1.0 + ratio), (16, 128))
    tail = jnp.broadcast_to(step0 * step1, (16, 128))
    for s, hop in enumerate((h0, h1, h2, h3)):
        bin_at = lax.rem(mic_ref[0] + s, 4)
        for h in range(2):
            for c in range(8):
                rows, cols = slice(h * 16, h * 16 + 16), slice(c * 128, c * 128 + 128)
                x_ref[bin_at, h, :, cols] = lead * hop[0, rows, cols] - tail * hop[1, rows, cols]
    for m in range(4):
        for h in range(2):
            for c in range(8):
                cols = slice(c * 128, c * 128 + 128)
                j = (2 * c + h) * 4 + m
                r_ref[m, h, :, cols] = (
                    press_ref[m, h, :, cols] - lead * recv_ref[j, 0:16] + tail * recv_ref[j, 16:32]
                )


VM = pl.BlockSpec(memory_space=pltpu.VMEM)
SM = pl.BlockSpec(memory_space=pltpu.SMEM)
PARAMS = pltpu.CompilerParams(vmem_limit_bytes=48 << 20)


def whole(shape):
    return pl.BlockSpec(shape, lambda i: (0,) * len(shape))


def ahead(x, shift):
    return lax.ppermute(x, "mic", [((t + shift) % 4, t) for t in range(4)])


def body(grid_points, mic_coords, wavenumbers, pressures):
    grid_total = grid_points.shape[1] * lax.axis_size("grid")
    scale = 1.0 / math.sqrt(grid_total)
    mic = lax.axis_index("mic")
    mic_one = jnp.reshape(mic, (1,)).astype(jnp.int32)
    turns = lax.dynamic_slice(wavenumbers, (mic,), (1,)) * (0.5 / math.pi)
    flat = pressures.reshape(4, 32, 1024)
    coords = jnp.pad(mic_coords, ((0, 5), (0, 0)))

    def pack(owner):
        return jnp.concatenate([lax.dynamic_index_in_dim(flat, owner, 0, False), coords], axis=0)

    packs = [pack(mic)] + [ahead(pack(lax.rem(mic + 4 - s, 4)), s) for s in (1, 2, 3)]

    tile = jax.ShapeDtypeStruct((1024, 4096), BF16)
    tile_spec = pl.BlockSpec((STEP, 4096), lambda i: (i, 0))
    grad_type = jax.ShapeDtypeStruct((32, 1024), F32)
    grad_spec = pl.BlockSpec((32, STEP), lambda i: (0, i))
    image_type = jax.ShapeDtypeStruct((8, 2, 4, 16, 128), F32)
    scratch = [pltpu.VMEM((32, 4096), BF16), pltpu.VMEM((32, 4096), BF16), pltpu.VMEM((32, 4096), F32)]
    cos_tile, sin_tile, grad0, part0 = pl.pallas_call(
        functools.partial(first_kernel, scale),
        grid=(1024 // STEP,),
        in_specs=[SM, pl.BlockSpec((STEP, 3), lambda i: (i, 0))] + [whole((40, 1024))] * 4,
        out_specs=[tile_spec, tile_spec, grad_spec, whole(image_type.shape)],
        out_shape=[tile, tile, grad_type, image_type],
        scratch_shapes=scratch,
        compiler_params=PARAMS,
        name="build",
    )(turns, grid_points.T, *packs)

    parts = lax.all_to_all(part0.reshape(16, 4, 16, 128), "grid", 0, 0)
    shard_type = jax.ShapeDtypeStruct((4, 16, 128), F32)
    image0, copies = pl.pallas_call(
        gather_kernel,
        in_specs=[VM],
        out_specs=[VM, VM],
        out_shape=[shard_type, jax.ShapeDtypeStruct((16, 4, 16, 128), BF16)],
        name="gather",
    )(parts)
    rounded = lax.all_to_all(copies, "grid", 0, 0)

    grad1, part1, sums = pl.pallas_call(
        functools.partial(second_kernel, scale),
        grid=(1024 // STEP,),
        in_specs=[whole((16, 4, 16, 128)), tile_spec, tile_spec, grad_spec],
        out_specs=[grad_spec, whole(image_type.shape), whole((8, 128))],
        out_shape=[grad_type, image_type, jax.ShapeDtypeStruct((8, 128), F32)],
        scratch_shapes=scratch,
        compiler_params=PARAMS,
        name="again",
    )(rounded, cos_tile, sin_tile, grad0)

    both = jnp.stack([grad0, grad1])
    hops = [both] + [ahead(both, s) for s in (1, 2, 3)]
    parts = lax.all_to_all(part1.reshape(16, 4, 16, 128), "grid", 0, 0)
    sent = pl.pallas_call(
        spread_kernel,
        in_specs=[SM, VM, VM, VM],
        out_specs=VM,
        out_shape=jax.ShapeDtypeStruct((64, 40, 128), F32),
        scratch_shapes=[pltpu.VMEM((4, 16, 128), F32)],
        name="spread",
    )(mic_one, parts, image0, sums)
    recv = lax.all_to_all(sent, ("grid", "mic"), 0, 0)
    local = pl.pallas_call(
        local_sums_kernel,
        in_specs=[VM],
        out_specs=VM,
        out_shape=jax.ShapeDtypeStruct((8, 128), F32),
        name="local_sums",
    )(recv)
    total = lax.psum(local, "bin")
    out_type = jax.ShapeDtypeStruct((4, 2, 16, 1024), F32)
    return pl.pallas_call(
        last_kernel,
        in_specs=[SM] + [VM] * 7,
        out_specs=[VM, VM],
        out_shape=[out_type, out_type],
        compiler_params=PARAMS,
        name="last",
    )(mic_one, total, recv, pressures, *hops)


def solution(mesh):
    placed = (P(None, "grid"), P(None, "mic"), P("bin"), P("bin", None, None, "mic"))
    return jax.shard_map(
        body,
        mesh=mesh,
        in_specs=placed,
        out_specs=(P("bin", None, None, "grid"), P("bin", None, None, "mic")),
        check_vma=False,
    )
```

time: 770 us -> 204 us (0.26)
  waiting for transfers between devices: 290 us -> 23 us
  blocking collectives: 333 us -> 72.4 us
  other arithmetic: 85.2 us -> 0.8 us
  Pallas kernels: 0 us -> 69.1 us
  matrix products: 33.6 us -> 0 us
  starting transfers between devices: 0.16 us -> 30.9 us
  between operations: 17.9 us -> 1.41 us
    psum x4 -> x1, blocking collectives: 333 us -> 33.4 us  [body(): total = lax.psum(local, 'bin')]
    psum x4 -> x0, waiting for transfers between devices: 290 us -> none  [the longest x2 186 us: body(): apply_summed = lax.psum(apply_partial_terms, 'grid')]
    convert_element_type x4 -> x0, other arithmetic: 70.7 us -> none  [the longest x1 67.4 us: steering_tiles(): cos_list.append((jnp.cos(phase_angle) * amplitude).astype(jnp.bfloat16))]
    pallas_call x0 -> x6, Pallas kernels: none -> 69.1 us  [the longest x1 47.1 us: body(): pl.pallas_call(functools.partial(first_kernel, scale), grid=(1024 // STEP...]
    all_to_all x0 -> x3, blocking collectives: none -> 39 us  [the longest x1 15.7 us: body(): parts = lax.all_to_all(part0.reshape(16, 4, 16, 128), 'grid', 0, 0)]
    dot_general x8 -> x0, matrix products: 33.6 us -> none  [the longest x2 10 us: body(): jnp.einsum('fkg,fgm->fkm', apply_rounded, cos_tiles, preferred_element_ty...]
    ppermute x0 -> x6, starting transfers between devices: none -> 20 us  [ahead(): return lax.ppermute(x, 'mic', [((t + shift) % 4, t) for t in range(4)])]
    all_to_all x0 -> x1, waiting for transfers between devices: none -> 17 us  [body(): recv = lax.all_to_all(sent, ('grid', 'mic'), 0, 0)]
  transfers between devices with their start and end apart: 4 -> 7, of which waited for: 4 -> 3; matrix products, arithmetic and copies ran while one was open for 0% -> 1% of each run, Pallas kernels for 0% -> 1%
where the time goes in v1:
time: 204 us; the launch traced here: 203 us
  blocking collectives  72.4 us (35%)
  Pallas kernels  69.1 us (34%)
  starting transfers between devices  30.9 us (15%)
  waiting for transfers between devices  23 us (11%)
  local copies, waits for them, and re-layouts  5.7 us (3%)
    pallas_call x1, Pallas kernels, body(): pl.pallas_call(functools.partial(first_kernel, scale), grid=(1024 // STEP...  47.1 us
    psum x1, blocking collectives, body(): total = lax.psum(local, 'bin')  33.4 us
    ppermute x6, starting transfers between devices, ahead(): return lax.ppermute(x, 'mic', [((t + shift) % 4, t) for t in range(4)])  20 us
    all_to_all x1, waiting for transfers between devices, body(): recv = lax.all_to_all(sent, ('grid', 'mic'), 0, 0)  17 us
    all_to_all x1, blocking collectives, body(): parts = lax.all_to_all(part0.reshape(16, 4, 16, 128), 'grid', 0, 0)  15.7 us
    pallas_call x1, Pallas kernels, body(): pl.pallas_call(functools.partial(second_kernel, scale), grid=(1024 // STE...  14.8 us
    all_to_all x1, blocking collectives, body(): parts = lax.all_to_all(part1.reshape(16, 4, 16, 128), 'grid', 0, 0)  12.3 us
    all_to_all x1, blocking collectives, body(): rounded = lax.all_to_all(copies, 'grid', 0, 0)  11 us
  transfers between devices with their start and end apart: 7, of which 3 were waited for; matrix products, arithmetic and copies ran while one was open for 1% of the time, Pallas kernels for 1%

profile of v1, /device:TPU:1, one launch (start us, length us, event | category | flops | bytes accessed | tf_op | source)
XLA Modules:
  0.0 203.3 jit_solution(9139567573484272428)
XLA Ops:
  0.6 1.1 dynamic-slice_bitcast_fusion
  1.8 0.8 fusion.3
  2.6 3.9 %collective-permute-start.2 = (f32[40,1024]{1,0:T(8,128)S(1)}, f32[40,1024]{1,0:T(8,128)S(1)}, u32[]{:S(2)}, u32[]{:S(2)}) collective-permute-start(f32[40,1024]{1,0:T(8,128)S(1)} %get-tuple-element.24), channel_id=1, source_target_pairs={{12,0},{0,4},{4,8},{8,12},{13,1},{1,5},{5,9},{9,13},{14,2},{2,6},{... | collective-permute-start | bytes 491528 | tf_op jit(solution)/shard_map/ppermute | solution.py:205
  6.5 3.1 %collective-permute-start = (f32[40,1024]{1,0:T(8,128)S(1)}, f32[40,1024]{1,0:T(8,128)S(1)}, u32[]{:S(2)}, u32[]{:S(2)}) collective-permute-start(f32[40,1024]{1,0:T(8,128)S(1)} %get-tuple-element.26), channel_id=1, source_target_pairs={{4,0},{8,4},{12,8},{0,12},{5,1},{9,5},{13,9},{1,13},{6,2},{10,6},{... | collective-permute-start | bytes 491528 | tf_op jit(solution)/shard_map/ppermute | solution.py:205
  9.6 4.4 %collective-permute-start.1 = (f32[40,1024]{1,0:T(8,128)S(1)}, f32[40,1024]{1,0:T(8,128)S(1)}, u32[]{:S(2)}, u32[]{:S(2)}) collective-permute-start(f32[40,1024]{1,0:T(8,128)S(1)} %get-tuple-element.27), channel_id=1, source_target_pairs={{8,0},{12,4},{0,8},{4,12},{9,1},{13,5},{1,9},{5,13},{10,2},{14,6},... | collective-permute-start | bytes 491528 | tf_op jit(solution)/shard_map/ppermute | solution.py:205
  14.0 1.2 dynamic_slice.16
  15.2 0.9 copy.6
  16.8 0.0 collective-permute-done.2.p3
  16.8 5.2 %collective-permute-done.p1 = f32[40,1024]{1,0:T(8,128)S(1)} collective-permute-done((f32[40,1024]{1,0:T(8,128)S(1)}, f32[40,1024]{1,0:T(8,128)S(1)}, u32[]{:S(2)}, u32[]{:S(2)}) %collective-permute-start) | collective-permute-done | bytes 163872 | tf_op jit(solution)/shard_map/ppermute | solution.py:205
  22.0 0.9 collective-permute-done.1.p2
  22.9 47.1 %build.1 = (bf16[1024,4096]{1,0:T(8,128)(2,1)}, bf16[1024,4096]{1,0:T(8,128)(2,1)}, f32[32,1024]{1,0:T(8,128)S(1)}, f32[8,2,4,16,128]{4,3,2,1,0:T(8,128)S(1)}) custom-call(f32[1]{0:T(128)S(6)} %mul.3.turns_ref, f32[1024,3]{1,0:T(8,128)S(1)} %bitcast.16, f32[40,1024]{1,0:T(8,128)S(1)} %get-tuple-element.25.p0, f32[40,1024]{1,0:T(8,128)S(1)} %collective-permute-done.p1, ...), custom_call_target="tpu_custom_call" | custom-call | tf_op jit(solution)/shard_map/build/pallas_call | solution.py:228
  69.9 15.7 %all_to_all.20.parts_ref = f32[16,4,16,128]{3,2,1,0:T(8,128)} all-to-all(f32[16,4,16,128]{3,2,1,0:T(8,128)S(1)} %bitcast.18), channel_id=1, replica_groups=mesh['grid'=16,'mic'=4,'bin'=4] {'grid'}, dimensions={0} | all-to-all | bytes 1048576 | tf_op jit(solution)/shard_map/all_to_all | solution.py:239
  85.7 1.8 gather.1
  87.4 11.0 %all_to_all.21.q_ref = bf16[16,4,16,128]{3,2,1,0:T(8,128)(2,1)S(1)} all-to-all(bf16[16,4,16,128]{3,2,1,0:T(8,128)(2,1)} %get-tuple-element.12), channel_id=1, replica_groups=mesh['grid'=16,'mic'=4,'bin'=4] {'grid'}, dimensions={0} | all-to-all | bytes 524288 | tf_op jit(solution)/shard_map/all_to_all | solution.py:248
  98.5 0.0 copy-start.2
  98.5 14.8 %again.1 = (f32[32,1024]{1,0:T(8,128)S(1)}, f32[8,2,4,16,128]{4,3,2,1,0:T(8,128)S(1)}, f32[8,128]{1,0:T(8,128)S(1)}) custom-call(bf16[16,4,16,128]{3,2,1,0:T(8,128)(2,1)S(1)} %all_to_all.21.q_ref, bf16[1024,4096]{1,0:T(8,128)(2,1)} %get-tuple-element.13.cos_ref, bf16[1024,4096]{1,0:T(8,128)(2,1)} %get-tuple-element.14.sin_ref, ...), custom_call_target="tpu_custom_call" | custom-call | tf_op jit(solution)/shard_map/again/pallas_call | solution.py:250
  113.3 0.0 copy-start.3
  113.3 12.3 %all_to_all.22.parts_ref = f32[16,4,16,128]{3,2,1,0:T(8,128)} all-to-all(f32[16,4,16,128]{3,2,1,0:T(8,128)S(1)} %bitcast.19), channel_id=1, replica_groups=mesh['grid'=16,'mic'=4,'bin'=4] {'grid'}, dimensions={0} | all-to-all | bytes 1048576 | tf_op jit(solution)/shard_map/all_to_all | solution.py:263
  125.6 0.0 copy-done.3
  125.6 2.3 %spread.1 = f32[64,40,128]{2,1,0:T(8,128)} custom-call(s32[1]{0:T(128)} %bitcast.mic_ref, f32[16,4,16,128]{3,2,1,0:T(8,128)} %all_to_all.22.parts_ref, f32[4,16,128]{2,1,0:T(8,128)} %get-tuple-element.17.q_ref, f32[8,128]{1,0:T(8,128)} %copy-done.3), custom_call_target="tpu_custom_call" | custom-call | tf_op jit(solution)/shard_map/spread/pallas_call | solution.py:264
  127.8 10.9 %all-to-all-start.3 = ((f32[64,40,128]{2,1,0:T(8,128)}), f32[64,40,128]{2,1,0:T(8,128)S(1)}, u32[]{:S(2)}, u32[]{:S(2)}) async-start(f32[64,40,128]{2,1,0:T(8,128)} %spread.1), calls=%async_computation.3 | async-start | bytes 2621440 | tf_op jit(solution)/shard_map/all_to_all | solution.py:272
  138.8 2.0 collective-permute-start.5
  140.7 3.3 %collective-permute-start.4 = (f32[2,32,1024]{2,1,0:T(8,128)S(1)}, f32[2,32,1024]{2,1,0:T(8,128)S(1)}, u32[]{:S(2)}, u32[]{:S(2)}) collective-permute-start(f32[2,32,1024]{2,1,0:T(8,128)S(1)} %pad_maximum_fusion.h0), channel_id=1, source_target_pairs={{8,0},{12,4},{0,8},{4,12},{9,1},{13,5},{1,9},{5,13},{10,2},{14,6},... | collective-permute-start | bytes 786440 | tf_op jit(solution)/shard_map/ppermute | solution.py:205
  144.0 3.3 %collective-permute-start.3 = (f32[2,32,1024]{2,1,0:T(8,128)S(1)}, f32[2,32,1024]{2,1,0:T(8,128)S(1)}, u32[]{:S(2)}, u32[]{:S(2)}) collective-permute-start(f32[2,32,1024]{2,1,0:T(8,128)S(1)} %pad_maximum_fusion.h0), channel_id=1, source_target_pairs={{4,0},{8,4},{12,8},{0,12},{5,1},{9,5},{13,9},{1,13},{6,2},{10,6},{... | collective-permute-start | bytes 786440 | tf_op jit(solution)/shard_map/ppermute | solution.py:205
  147.3 17.0 %all-to-all-done.3.recv_ref = f32[64,40,128]{2,1,0:T(8,128)S(1)} async-done(((f32[64,40,128]{2,1,0:T(8,128)}), f32[64,40,128]{2,1,0:T(8,128)S(1)}, u32[]{:S(2)}, u32[]{:S(2)}) %all-to-all-start.3) | async-done | bytes 1310752 | tf_op jit(solution)/shard_map/all_to_all | solution.py:272
  164.3 0.0 copy-start
  164.3 1.1 copy-done
  165.4 2.0 local_sums.1
  167.3 33.4 %psum.7.sums_ref = f32[8,128]{1,0:T(8,128)S(1)} all-reduce(f32[8,128]{1,0:T(8,128)} %local_sums.1), channel_id=1, replica_groups=mesh['grid'=16,'mic'=4,'bin'=4] {'bin'}, use_global_device_ids=true, to_apply=%region_0.1 | all-reduce | flops 1024 | bytes 8192 | tf_op jit(solution)/shard_map/psum | solution.py:280
  200.8 0.0 collective-permute-done.5.h3
  200.8 0.0 collective-permute-done.4.h2
  200.8 0.0 collective-permute-done.3.h1
  200.8 0.0 copy-done.2
  200.8 0.0 copy-start.1
  200.8 1.3 copy-done.1
  202.1 1.2 last.1
  (1 shorter events, 0.0 us)
Async XLA Ops:
  2.6 14.2 %collective-permute-start.2 = (f32[40,1024]{1,0:T(8,128)S(1)}, f32[40,1024]{1,0:T(8,128)S(1)}, u32[]{:S(2)}, u32[]{:S(2)}) collective-permute-start(f32[40,1024]{1,0:T(8,128)S(1)} %get-tuple-element.24), channel_id=1, source_target_pairs={{12,0},{0,4},{4,8},{8,12},{13,1},{1,5},{5,9},{9,13},{14,2},{2,6},{... | collective-permute-start | bytes 491528 | tf_op jit(solution)/shard_map/ppermute | solution.py:205
  6.5 15.5 %collective-permute-start = (f32[40,1024]{1,0:T(8,128)S(1)}, f32[40,1024]{1,0:T(8,128)S(1)}, u32[]{:S(2)}, u32[]{:S(2)}) collective-permute-start(f32[40,1024]{1,0:T(8,128)S(1)} %get-tuple-element.26), channel_id=1, source_target_pairs={{4,0},{8,4},{12,8},{0,12},{5,1},{9,5},{13,9},{1,13},{6,2},{10,6},{... | collective-permute-start | bytes 491528 | tf_op jit(solution)/shard_map/ppermute | solution.py:205
  9.6 13.3 %collective-permute-start.1 = (f32[40,1024]{1,0:T(8,128)S(1)}, f32[40,1024]{1,0:T(8,128)S(1)}, u32[]{:S(2)}, u32[]{:S(2)}) collective-permute-start(f32[40,1024]{1,0:T(8,128)S(1)} %get-tuple-element.27), channel_id=1, source_target_pairs={{8,0},{12,4},{0,8},{4,12},{9,1},{13,5},{1,9},{5,13},{10,2},{14,6},... | collective-permute-start | bytes 491528 | tf_op jit(solution)/shard_map/ppermute | solution.py:205
  98.5 102.3 %copy-start.2 = (f32[4,2,16,1024]{3,2,1,0:T(8,128)S(1)}, f32[4,2,16,1024]{3,2,1,0:T(8,128)}, u32[]{:S(2)}) copy-start(f32[4,2,16,1024]{3,2,1,0:T(8,128)} %press_ref.1) | copy-start | bytes 1572868
  113.3 12.3 %copy-start.3 = (f32[8,128]{1,0:T(8,128)}, f32[8,128]{1,0:T(8,128)S(1)}, u32[]{:S(2)}) copy-start(f32[8,128]{1,0:T(8,128)S(1)} %get-tuple-element.18.sums_ref) | copy-start | bytes 12292
  127.8 36.5 %all-to-all-start.3 = ((f32[64,40,128]{2,1,0:T(8,128)}), f32[64,40,128]{2,1,0:T(8,128)S(1)}, u32[]{:S(2)}, u32[]{:S(2)}) async-start(f32[64,40,128]{2,1,0:T(8,128)} %spread.1), calls=%async_computation.3 | async-start | bytes 2621440 | tf_op jit(solution)/shard_map/all_to_all | solution.py:272
  138.8 62.0 %collective-permute-start.5 = (f32[2,32,1024]{2,1,0:T(8,128)S(1)}, f32[2,32,1024]{2,1,0:T(8,128)S(1)}, u32[]{:S(2)}, u32[]{:S(2)}) collective-permute-start(f32[2,32,1024]{2,1,0:T(8,128)S(1)} %pad_maximum_fusion.h0), channel_id=1, source_target_pairs={{12,0},{0,4},{4,8},{8,12},{13,1},{1,5},{5,9},{9,13},{14,2},{2,6},{... | collective-permute-start | bytes 786440 | tf_op jit(solution)/shard_map/ppermute | solution.py:205
  140.7 60.0 %collective-permute-start.4 = (f32[2,32,1024]{2,1,0:T(8,128)S(1)}, f32[2,32,1024]{2,1,0:T(8,128)S(1)}, u32[]{:S(2)}, u32[]{:S(2)}) collective-permute-start(f32[2,32,1024]{2,1,0:T(8,128)S(1)} %pad_maximum_fusion.h0), channel_id=1, source_target_pairs={{8,0},{12,4},{0,8},{4,12},{9,1},{13,5},{1,9},{5,13},{10,2},{14,6},... | collective-permute-start | bytes 786440 | tf_op jit(solution)/shard_map/ppermute | solution.py:205
  144.0 56.7 %collective-permute-start.3 = (f32[2,32,1024]{2,1,0:T(8,128)S(1)}, f32[2,32,1024]{2,1,0:T(8,128)S(1)}, u32[]{:S(2)}, u32[]{:S(2)}) collective-permute-start(f32[2,32,1024]{2,1,0:T(8,128)S(1)} %pad_maximum_fusion.h0), channel_id=1, source_target_pairs={{4,0},{8,4},{12,8},{0,12},{5,1},{9,5},{13,9},{1,13},{6,2},{10,6},{... | collective-permute-start | bytes 786440 | tf_op jit(solution)/shard_map/ppermute | solution.py:205
  164.3 1.1 copy-start
  200.8 1.3 copy-start.1

commit v2 on v0

v2 whole, which is shorter than its diff:
```python
import functools
import math

import jax
import jax.numpy as jnp
from jax import lax
from jax.experimental import pallas as pl
from jax.experimental.pallas import tpu as pltpu
from jax.sharding import PartitionSpec as P

F32, BF16 = jnp.float32, jnp.bfloat16
QUARTER = (2.641753911972046, -1.0863767862319946, 0.13400563597679138, -0.0077399080619215965)
SQUARE = 2.0 * math.sqrt(2.0)
ROOT = math.sqrt(2.0)
ROWS, LANES, EDGE = 16, 256, 256
VM = pl.BlockSpec(memory_space=pltpu.VMEM)
SM = pl.BlockSpec(memory_space=pltpu.SMEM)


def steering(gx, gy, gz, mx, my, mz, turns):
    dx, dy, dz = gx - mx, gy - my, gz - mz
    square = dx * dx + dy * dy + dz * dz
    inverse = lax.rsqrt(square)
    cycles = (square * inverse) * turns
    part = cycles - jnp.round(cycles)
    t = part * part
    s = QUARTER[3]
    for k in (2, 1, 0):
        s = s * t + QUARTER[k]
    s = s * part
    q = s * s
    w = SQUARE - q
    half_sin = s * (w * lax.rsqrt(w))
    half_cos = ROOT - q
    scaled = half_sin * inverse
    return (inverse - scaled * half_sin).astype(BF16), (scaled * half_cos).astype(BF16)


def dot_nt(a, b):
    return lax.dot_general(a, b, (((1,), (1,)), ((), ())), preferred_element_type=F32)


def dot_nn(a, b):
    return lax.dot_general(a, b, (((1,), (0,)), ((), ())), preferred_element_type=F32)


def multiple(x, m):
    return x if isinstance(x, int) else pl.multiple_of(x, m)


def span(index):
    return pl.ds(multiple(index * EDGE, EDGE), EDGE)


def lane_sums(x):
    return jnp.sum(x, axis=0, keepdims=True)


def swapped(v):
    return jnp.concatenate([v[16:32], -v[0:16]], axis=0)


class Tiles:
    def __init__(self, refs):
        self.refs = refs

    def get(self, step_odd, chunk_odd):
        at = (step_odd * 2 + chunk_odd) * 2
        return self.refs[at], self.refs[at + 1]

    def build(self, grid_ref, mics, turns, half, odd, pair, chunk_odd):
        c_ref, s_ref = self.get(odd, chunk_odd)
        for block in range(EDGE // ROWS):
            rows = pl.ds(multiple((half * 2 + odd) * EDGE + block * ROWS, ROWS), ROWS)
            g = [jnp.broadcast_to(grid_ref[rows, d : d + 1], (ROWS, LANES)) for d in range(3)]
            c, s = steering(*g, *mics, turns)
            at = (pl.ds(multiple(half * EDGE + block * ROWS, ROWS), ROWS), span(pair))
            c_ref[at] = c
            s_ref[at] = s

    def adjoint(self, weights, half, odd, pair, chunk_odd):
        c_ref, s_ref = self.get(odd, chunk_odd)
        wc, ws = weights[0], weights[1]
        at = (span(half), span(pair))
        cols = span(pair)
        return dot_nt(wc[chunk_odd, :, cols], c_ref[at]) + dot_nt(ws[chunk_odd, :, cols], s_ref[at])

    def forward(self, image, v, v2, half, odd, pair, chunk_odd):
        c_ref, s_ref = self.get(odd, chunk_odd)
        at = (span(half), span(pair))
        image[chunk_odd, :, span(pair)] += dot_nn(v, c_ref[at]) + dot_nn(v2, s_ref[at])


def prepare_kernel(mic_ref, press_ref, coords_ref, points_ref, g_ref, o1, o2, o3, pad):
    for s, out in ((1, o1), (2, o2), (3, o3)):
        out[0:32] = press_ref[lax.rem(mic_ref[0] + 4 - s, 4)]
        out[32:35] = coords_ref[...]
        out[35:40] = jnp.zeros((5, 1024), F32)
    pad[0:3] = points_ref[...]
    pad[3:8] = jnp.zeros((5, 1024), F32)
    for r in range(8):
        g_ref[r * 128 : r * 128 + 128, :] = pad[:, r * 128 : r * 128 + 128].T


def set_weights(wc, ws, chunk, real, imag, scale):
    odd, cols = chunk % 2, slice((chunk // 2) * EDGE, (chunk // 2) * EDGE + EDGE)
    real, imag = real * scale, imag * scale
    wc[odd, 0:16, cols] = real
    wc[odd, 16:32, cols] = imag
    ws[odd, 0:16, cols] = -imag
    ws[odd, 16:32, cols] = real


def turns_of(mic_ref, wave_ref):
    return wave_ref[mic_ref[0]] * (0.5 / math.pi)


def own_kernel(scale, mic_ref, wave_ref, press_ref, coords_ref, grid_ref, *refs):
    tiles, grad_ref, wc, ws = Tiles(refs[:8]), refs[8], refs[9], refs[10]
    turns = turns_of(mic_ref, wave_ref)
    for chunk in range(4):
        cols = slice(chunk * EDGE, chunk * EDGE + EDGE)
        w = press_ref[mic_ref[0], :, cols].astype(BF16)
        set_weights(wc, ws, chunk, w[0:16], w[16:32], scale)

    def mics(chunk):
        return [coords_ref[d : d + 1, chunk * EDGE : chunk * EDGE + EDGE] for d in range(3)]

    def half_step(half, carry):
        late = None
        for odd in range(2):
            total = jnp.zeros((32, EDGE), F32)
            for pair in range(2):
                for chunk_odd in range(2):
                    if late is not None:
                        value = tiles.adjoint((wc, ws), half, *late)
                        if late[0] == odd:
                            total += value
                        else:
                            grad_ref[:, span(half * 2 + late[0])] = done + value
                    tiles.build(grid_ref, mics(pair * 2 + chunk_odd), turns, half, odd, pair, chunk_odd)
                    late = (odd, pair, chunk_odd)
            done = total
        grad_ref[:, span(half * 2 + 1)] = done + tiles.adjoint((wc, ws), half, *late)
        return carry

    lax.fori_loop(0, 2, half_step, 0)


def store_image(out_ref, image, first):
    for odd in range(2):
        for pair in range(image.shape[2] // EDGE):
            for piece in range(2):
                tile = (pair * 2 + odd) * 2 + piece
                s, c = tile // 8 + first, tile % 8
                lo = pair * EDGE + piece * 128
                for h in range(2):
                    out_ref[c, h, s] = image[odd, h * 16 : h * 16 + 16, lo : lo + 128]


def rest_kernel(scale, mic_ref, wave_ref, grid_ref, p1, p2, p3, head_ref, *refs):
    own, tiles = Tiles(refs[:8]), Tiles(refs[8:16])
    grad_ref, image_ref, wc, ws, near, far, coords = refs[16:]
    turns = turns_of(mic_ref, wave_ref)
    for s, pack in enumerate((p1, p2, p3)):
        for chunk in range(4):
            w = pack[0:32, chunk * EDGE : chunk * EDGE + EDGE].astype(BF16)
            set_weights(wc, ws, s * 4 + chunk, w[0:16], w[16:32], scale)
        coords[:, s * 1024 : s * 1024 + 1024] = pack[32:40]
    near[...] = jnp.zeros_like(near)
    far[...] = jnp.zeros_like(far)

    def mics(pair, chunk_odd):
        lo = pl.ds(multiple((pair * 2 + chunk_odd) * EDGE, EDGE), EDGE)
        return [coords[d : d + 1, lo] for d in range(3)]

    def one_step(half, odd, v, before):
        total = head_ref[:, span(half * 2 + odd)]

        def pair_body(pair, total, first):
            if not first:
                total += tiles.adjoint((wc, ws), half, odd, pair - 1, 1)
            if before is not None:
                tiles.forward(far, *v, *before, pair, 0)
                if first:
                    for p in range(2):
                        for o in range(2):
                            own.forward(near, *v, *before, p, o)
            tiles.build(grid_ref, mics(pair, 0), turns, half, odd, pair, 0)
            total += tiles.adjoint((wc, ws), half, odd, pair, 0)
            if before is not None:
                tiles.forward(far, *v, *before, pair, 1)
            tiles.build(grid_ref, mics(pair, 1), turns, half, odd, pair, 1)
            return total

        total = pair_body(0, total, True)
        total = lax.fori_loop(1, 6, lambda pair, total: pair_body(pair, total, False), total)
        total += tiles.adjoint((wc, ws), half, odd, 5, 1)
        grad_ref[:, span(half * 2 + odd)] = total
        v = total.astype(BF16) * scale
        return v, swapped(v)

    v = one_step(0, 0, None, None)
    v = one_step(0, 1, v, (0, 0))
    v = one_step(1, 0, v, (0, 1))
    v = one_step(1, 1, v, (1, 0))
    for p in range(2):
        for o in range(2):
            own.forward(near, *v, 1, 1, p, o)

    def tail(pair, carry):
        tiles.forward(far, *v, 1, 1, pair, 0)
        tiles.forward(far, *v, 1, 1, pair, 1)
        return carry

    lax.fori_loop(0, 6, tail, 0)
    store_image(image_ref, near, 0)
    store_image(image_ref, far, 1)


def again_kernel(scale, q_ref, grad0_ref, *refs):
    own, tiles = Tiles(refs[:8]), Tiles(refs[8:16])
    both_ref, image_ref, sums_ref, wa, wb, wc, wd, near, far = refs[16:]
    for block in range(4):
        for chunk in range(4):
            real = jnp.concatenate([q_ref[4 * chunk + 2 * p, block] for p in range(2)], axis=1)
            imag = jnp.concatenate([q_ref[4 * chunk + 2 * p + 1, block] for p in range(2)], axis=1)
            if block == 0:
                set_weights(wa, wb, chunk, real, imag, scale)
            else:
                set_weights(wc, wd, (block - 1) * 4 + chunk, real, imag, scale)
    near[...] = jnp.zeros_like(near)
    far[...] = jnp.zeros_like(far)
    sums_ref[...] = jnp.zeros_like(sums_ref)

    def forward(v, half, odd):
        for o in range(2):
            for image, (c_ref, s_ref) in ((near, own.get(odd, o)), (far, tiles.get(odd, o))):
                image[o] += dot_nn(v[0], c_ref[span(half), :]) + dot_nn(v[1], s_ref[span(half), :])

    def adjoint(half, odd):
        total = None
        for o in range(2):
            for w_c, w_s, (c_ref, s_ref) in ((wa, wb, own.get(odd, o)), (wc, wd, tiles.get(odd, o))):
                value = dot_nt(w_c[o], c_ref[span(half), :]) + dot_nt(w_s[o], s_ref[span(half), :])
                total = value if total is None else total + value
        return total

    def finish(half, odd, total):
        cols = span(half * 2 + odd)
        g0 = grad0_ref[:, cols]
        both_ref[0, :, cols] = g0
        both_ref[1, :, cols] = total
        sums_ref[0:1] += lane_sums(g0 * g0)
        sums_ref[1:2] += lane_sums(g0 * total)
        sums_ref[2:3] += lane_sums(total * total)
        v = total.astype(BF16) * scale
        return v, swapped(v)

    v = finish(0, 0, adjoint(0, 0))
    for half, odd, before in ((0, 1, (0, 0)), (1, 0, (0, 1)), (1, 1, (1, 0))):
        total = adjoint(half, odd)
        forward(v, *before)
        v = finish(half, odd, total)
    forward(v, 1, 1)
    store_image(image_ref, near, 0)
    store_image(image_ref, far, 1)


def gather_kernel(parts_ref, shard_ref, copies_ref):
    total = parts_ref[0]
    for j in range(1, 16):
        total += parts_ref[j]
    shard_ref[...] = total
    low = total.astype(BF16)
    for j in range(16):
        copies_ref[j] = low


def spread_kernel(mic_ref, parts_ref, q_ref, sums_ref, out_ref, shard):
    total = parts_ref[0]
    for j in range(1, 16):
        total += parts_ref[j]
    shard[...] = total
    q = q_ref[...]

    def flat(x):
        return lane_sums(x.reshape(64, 128))

    near = sums_ref[0:3, 0:128] + sums_ref[0:3, 128:256]
    sums = jnp.concatenate([near, flat(q * q), flat(q * total), flat(total * total), jnp.zeros((2, 128), F32)], axis=0)
    for t in range(4):
        s = lax.rem(t + 4 - mic_ref[0], 4)
        a, b = q_ref[s], shard[s]
        for k in range(4):
            out_ref[t * 4 + k, 0:16] = a
            out_ref[t * 4 + k, 16:32] = b
            out_ref[t * 4 + k, 32:40] = sums


def relay_kernel(bin_ref, recv_ref, out_ref):
    sums = recv_ref[0, 32:40]
    for j in range(1, 16):
        sums += recv_ref[j, 32:40]
    for m in range(4):
        piece = recv_ref[m * 4 + bin_ref[0], 0:32]
        for j in range(16):
            out_ref[j, m * 32 : m * 32 + 32] = piece
    for j in range(16):
        out_ref[j, 128:136] = sums


def last_kernel(mic_ref, recv_ref, press_ref, h0, h1, h2, h3, x_ref, r_ref):
    total = recv_ref[0, 128:136]
    for j in range(1, 16):
        total += recv_ref[j, 128:136]
    total = jnp.sum(total, axis=1, keepdims=True)
    gg, gh, hh, qq, qp, pp = [total[i : i + 1] for i in range(6)]
    step0 = gg / qq
    norm1 = gg - 2.0 * step0 * gh + step0 * step0 * hh
    ratio = norm1 / gg
    image1 = (1.0 + ratio) * (1.0 + ratio) * qq - 2.0 * (1.0 + ratio) * step0 * qp + step0 * step0 * pp
    step1 = norm1 / image1
    lead = jnp.broadcast_to(step0 + step1 * (1.0 + ratio), (16, 128))
    tail = jnp.broadcast_to(step0 * step1, (16, 128))
    for s, hop in enumerate((h0, h1, h2, h3)):
        bin_at = lax.rem(mic_ref[0] + s, 4)
        for h in range(2):
            for c in range(8):
                rows, cols = slice(h * 16, h * 16 + 16), slice(c * 128, c * 128 + 128)
                x_ref[bin_at, h, :, cols] = lead * hop[0, rows, cols] - tail * hop[1, rows, cols]
    for m in range(4):
        for h in range(2):
            for c in range(8):
                cols = slice(c * 128, c * 128 + 128)
                q = recv_ref[2 * c + h, m * 32 : m * 32 + 16]
                p = recv_ref[2 * c + h, m * 32 + 16 : m * 32 + 32]
                r_ref[m, h, :, cols] = press_ref[m, h, :, cols] - lead * q + tail * p


def call(kernel, name, in_specs, out_shape, scratch=(), limit=16):
    return pl.pallas_call(
        kernel,
        in_specs=in_specs,
        out_specs=jax.tree.map(lambda _: VM, out_shape),
        out_shape=out_shape,
        scratch_shapes=list(scratch),
        compiler_params=pltpu.CompilerParams(vmem_limit_bytes=limit << 20),
        name=name,
    )


def array(*shape, dtype=F32):
    return jax.ShapeDtypeStruct(shape, dtype)


def ahead(x, shift):
    return lax.ppermute(x, "mic", [((t + shift) % 4, t) for t in range(4)])


def body(grid_points, mic_coords, wavenumbers, pressures):
    scale = 1.0 / math.sqrt(grid_points.shape[1] * lax.axis_size("grid"))
    mic = jnp.reshape(lax.axis_index("mic"), (1,)).astype(jnp.int32)
    bin_at = jnp.reshape(lax.axis_index("bin"), (1,)).astype(jnp.int32)
    flat = pressures.reshape(4, 32, 1024)

    points, *packs = call(
        prepare_kernel, "prepare", [SM, VM, VM, VM], [array(1024, 8)] + [array(40, 1024)] * 3, [pltpu.VMEM((8, 1024), F32)]
    )(mic, flat, mic_coords, grid_points)
    packs = [ahead(pack, s) for s, pack in zip((1, 2, 3), packs)]

    def held(width):
        return [pltpu.VMEM((512, width), BF16)] * 8

    weights_near = [pltpu.VMEM((2, 32, 512), BF16)] * 2
    weights_far = [pltpu.VMEM((2, 32, 1536), BF16)] * 2
    images = [pltpu.VMEM((2, 32, 512), F32), pltpu.VMEM((2, 32, 1536), F32)]
    *near, head = call(
        functools.partial(own_kernel, scale), "own", [SM, SM, VM, VM, VM], held(512) + [array(32, 1024)], weights_near
    )(mic, wavenumbers, flat, mic_coords, points)
    near = [pltpu.with_memory_space_constraint(t, pltpu.VMEM) for t in near]
    image_type = array(8, 2, 4, 16, 128)
    *far, grad0, part0 = call(
        functools.partial(rest_kernel, scale),
        "rest",
        [SM, SM] + [VM] * 13,
        held(1536) + [array(32, 1024), image_type],
        weights_far + images + [pltpu.VMEM((8, 3072), F32)],
        limit=32,
    )(mic, wavenumbers, points, *packs, head, *near)
    far = [pltpu.with_memory_space_constraint(t, pltpu.VMEM) for t in far]

    parts = lax.all_to_all(part0.reshape(16, 4, 16, 128), "grid", 0, 0)
    image0, copies = call(
        gather_kernel, "gather", [VM], [array(4, 16, 128), array(16, 4, 16, 128, dtype=BF16)]
    )(parts)
    rounded = lax.all_to_all(copies, "grid", 0, 0)

    both, part1, sums = call(
        functools.partial(again_kernel, scale),
        "again",
        [VM] * 18,
        [array(2, 32, 1024), image_type, array(8, EDGE)],
        weights_near + weights_far + images,
        limit=32,
    )(rounded, grad0, *near, *far)

    hops = [both] + [ahead(both, s) for s in (1, 2, 3)]
    parts = lax.all_to_all(part1.reshape(16, 4, 16, 128), "grid", 0, 0)
    sent = call(spread_kernel, "spread", [SM, VM, VM, VM], array(16, 40, 128), [pltpu.VMEM((4, 16, 128), F32)])(
        mic, parts, image0, sums
    )
    recv = lax.all_to_all(sent, ("mic", "bin"), 0, 0)
    sent = call(relay_kernel, "relay", [SM, VM], array(16, 136, 128))(bin_at, recv)
    recv = lax.all_to_all(sent, "grid", 0, 0)
    out_type = array(4, 2, 16, 1024)
    return call(last_kernel, "last", [SM] + [VM] * 6, [out_type, out_type])(mic, recv, pressures, *hops)


def solution(mesh):
    placed = (P(None, "grid"), P(None, "mic"), P("bin"), P("bin", None, None, "mic"))
    return jax.shard_map(
        body,
        mesh=mesh,
        in_specs=placed,
        out_specs=(P("bin", None, None, "grid"), P("bin", None, None, "mic")),
        check_vma=False,
    )
```

time: 770 us -> 153 us (0.20)
  blocking collectives: 333 us -> 37.5 us
  waiting for transfers between devices: 290 us -> 40.2 us
  other arithmetic: 85.2 us -> 0 us
  Pallas kernels: 0 us -> 35.8 us
  starting transfers between devices: 0.16 us -> 35.2 us
  matrix products: 33.6 us -> 0 us
  between operations: 17.9 us -> 0.69 us
    psum x4 -> x0, blocking collectives: 333 us -> none  [the longest x2 281 us: apply_adjoint(): grad_norm = lax.psum(jnp.sum(summed * summed), ('grid', 'bin'))]
    psum x4 -> x0, waiting for transfers between devices: 290 us -> none  [the longest x2 186 us: body(): apply_summed = lax.psum(apply_partial_terms, 'grid')]
    convert_element_type x4 -> x0, other arithmetic: 70.7 us -> none  [the longest x1 67.4 us: steering_tiles(): cos_list.append((jnp.cos(phase_angle) * amplitude).astype(jnp.bfloat16))]
    all_to_all x0 -> x3, blocking collectives: none -> 37.5 us  [the longest x1 15.8 us: body(): parts = lax.all_to_all(part0.reshape(16, 4, 16, 128), 'grid', 0, 0)]
    pallas_call x0 -> x8, Pallas kernels: none -> 35.8 us  [the longest x1 19.1 us: body(): call(functools.partial(rest_kernel, scale), 'rest', [SM, SM] + [VM] * 13,...]
    dot_general x8 -> x0, matrix products: 33.6 us -> none  [the longest x2 10 us: body(): jnp.einsum('fkg,fgm->fkm', apply_rounded, cos_tiles, preferred_element_ty...]
    ppermute x0 -> x6, waiting for transfers between devices: none -> 27.1 us  [ahead(): return lax.ppermute(x, 'mic', [((t + shift) % 4, t) for t in range(4)])]
    all_to_all x0 -> x2, starting transfers between devices: none -> 20.4 us  [the longest x1 16.7 us: body(): recv = lax.all_to_all(sent, ('mic', 'bin'), 0, 0)]
  transfers between devices with their start and end apart: 4 -> 8, of which waited for: 4 -> 6; matrix products, arithmetic and copies ran while one was open for 0% -> 0% of each run, Pallas kernels for 0% -> 4%
where the time goes in v2:
time: 153 us
  waiting for transfers between devices  40.2 us (26%)
  blocking collectives  37.5 us (25%)
  Pallas kernels  35.8 us (23%)
  starting transfers between devices  35.2 us (23%)
  local copies, waits for them, and re-layouts  3.13 us (2%)
    ppermute x6, waiting for transfers between devices, ahead(): return lax.ppermute(x, 'mic', [((t + shift) % 4, t) for t in range(4)])  27.1 us
    pallas_call x1, Pallas kernels, body(): call(functools.partial(rest_kernel, scale), 'rest', [SM, SM] + [VM] * 13,...  19.1 us
    all_to_all x1, starting transfers between devices, body(): recv = lax.all_to_all(sent, ('mic', 'bin'), 0, 0)  16.7 us
    all_to_all x1, blocking collectives, body(): parts = lax.all_to_all(part0.reshape(16, 4, 16, 128), 'grid', 0, 0)  15.8 us
    ppermute x6, starting transfers between devices, ahead(): return lax.ppermute(x, 'mic', [((t + shift) % 4, t) for t in range(4)])  14.8 us
    all_to_all x1, waiting for transfers between devices, body(): recv = lax.all_to_all(sent, ('mic', 'bin'), 0, 0)  13.1 us
    all_to_all x1, blocking collectives, body(): parts = lax.all_to_all(part1.reshape(16, 4, 16, 128), 'grid', 0, 0)  11.6 us
    all_to_all x1, blocking collectives, body(): rounded = lax.all_to_all(copies, 'grid', 0, 0)  10.1 us
  transfers between devices with their start and end apart: 8, of which 6 were waited for; matrix products, arithmetic and copies ran while one was open for 0% of the time, Pallas kernels for 4%

profile of v2, /device:TPU:1, one launch (start us, length us, event | category | flops | bytes accessed | tf_op | source)
XLA Modules:
  0.0 152.5 jit_solution(14066435965175902785)
XLA Ops:
  0.6 0.0 copy-start
  0.6 1.0 copy-done
  1.7 0.0 copy-start.2
  1.7 0.7 copy-done.2
  2.4 0.0 copy-start.3
  2.4 0.7 copy-done.3
  3.1 0.2 prepare.1
  3.4 6.9 %collective-permute-start = (f32[40,1024]{1,0:T(8,128)S(1)}, f32[40,1024]{1,0:T(8,128)S(1)}, u32[]{:S(2)}, u32[]{:S(2)}) collective-permute-start(f32[40,1024]{1,0:T(8,128)S(1)} %get-tuple-element.31), channel_id=1, source_target_pairs={{4,0},{8,4},{12,8},{0,12},{5,1},{9,5},{13,9},{1,13},{6,2},{10,6},{... | collective-permute-start | bytes 491528 | tf_op jit(solution)/shard_map/ppermute | solution.py:358
  10.3 1.0 collective-permute-start.1
  11.3 2.3 %collective-permute-start.2 = (f32[40,1024]{1,0:T(8,128)S(1)}, f32[40,1024]{1,0:T(8,128)S(1)}, u32[]{:S(2)}, u32[]{:S(2)}) collective-permute-start(f32[40,1024]{1,0:T(8,128)S(1)} %get-tuple-element.33), channel_id=1, source_target_pairs={{12,0},{0,4},{4,8},{8,12},{13,1},{1,5},{5,9},{9,13},{14,2},{2,6},{... | collective-permute-start | bytes 491528 | tf_op jit(solution)/shard_map/ppermute | solution.py:358
  13.5 0.0 copy-start.4
  13.5 0.7 copy-done.4
  14.2 5.6 %own.1 = (bf16[512,512]{1,0:T(8,128)(2,1)S(1)}, bf16[512,512]{1,0:T(8,128)(2,1)S(1)}, bf16[512,512]{1,0:T(8,128)(2,1)S(1)}, bf16[512,512]{1,0:T(8,128)(2,1)S(1)}...) custom-call(s32[1]{0:T(128)} %bitcast.mic_ref, ...), custom_call_target="tpu_custom_call" | custom-call | tf_op jit(solution)/shard_map/own/pallas_call | solution.py:378
  19.8 0.0 collective-permute-done.p1
  19.8 2.8 %collective-permute-done.1.p2 = f32[40,1024]{1,0:T(8,128)S(1)} collective-permute-done((f32[40,1024]{1,0:T(8,128)S(1)}, f32[40,1024]{1,0:T(8,128)S(1)}, u32[]{:S(2)}, u32[]{:S(2)}) %collective-permute-start.1) | collective-permute-done | bytes 163872 | tf_op jit(solution)/shard_map/ppermute | solution.py:358
  22.6 0.3 collective-permute-done.2.p3
  22.9 19.1 %rest.1 = (bf16[512,1536]{1,0:T(8,128)(2,1)S(1)}, bf16[512,1536]{1,0:T(8,128)(2,1)S(1)}, bf16[512,1536]{1,0:T(8,128)(2,1)S(1)}, bf16[512,1536]{1,0:T(8,128)(2,1)...) custom-call(s32[1]{0:T(128)} %bitcast.mic_ref, ...), custom_call_target="tpu_custom_call" | custom-call | tf_op jit(solution)/shard_map/rest/pallas_call | solution.py:383
  42.0 15.8 %all_to_all.25.parts_ref = f32[16,4,16,128]{3,2,1,0:T(8,128)S(1)} all-to-all(f32[16,4,16,128]{3,2,1,0:T(8,128)S(1)} %bitcast.8), channel_id=1, replica_groups=mesh['grid'=16,'mic'=4,'bin'=4] {'grid'}, dimensions={0} | all-to-all | bytes 1048576 | tf_op jit(solution)/shard_map/all_to_all | solution.py:393
  57.9 10.1 %all_to_all.26.q_ref = bf16[16,4,16,128]{3,2,1,0:T(8,128)(2,1)S(1)} all-to-all(bf16[16,4,16,128]{3,2,1,0:T(8,128)(2,1)S(1)} %get-tuple-element.44), channel_id=1, replica_groups=mesh['grid'=16,'mic'=4,'bin'=4] {'grid'}, dimensions={0} | all-to-all | bytes 524288 | tf_op jit(solution)/shard_map/all_to_all | solution.py:397
  68.0 7.8 %again.1 = (f32[2,32,1024]{2,1,0:T(8,128)S(1)}, f32[8,2,4,16,128]{4,3,2,1,0:T(8,128)S(1)}, f32[8,256]{1,0:T(8,128)S(1)}) custom-call(bf16[16,4,16,128]{3,2,1,0:T(8,128)(2,1)S(1)} %all_to_all.26.q_ref, f32[32,1024]{1,0:T(8,128)S(1)} %get-tuple-element.45.grad0_ref, bf16[512,512]{1,0:T(8,128)(2,1)S(1)} %get-tuple-element.35.refs_0_, ...), custom_call_target="tpu_custom_call" | custom-call | tf_op jit(solution)/shard_map/again/pallas_call | solution.py:399
  75.8 11.6 %all_to_all.27.parts_ref = f32[16,4,16,128]{3,2,1,0:T(8,128)S(1)} all-to-all(f32[16,4,16,128]{3,2,1,0:T(8,128)S(1)} %bitcast.7), channel_id=1, replica_groups=mesh['grid'=16,'mic'=4,'bin'=4] {'grid'}, dimensions={0} | all-to-all | bytes 1048576 | tf_op jit(solution)/shard_map/all_to_all | solution.py:409
  87.4 0.8 spread.1
  88.2 16.7 %all-to-all-start.3 = ((f32[16,40,128]{2,1,0:T(8,128)}), f32[16,40,128]{2,1,0:T(8,128)S(1)}, u32[]{:S(2)}, u32[]{:S(2)}) async-start(f32[16,40,128]{2,1,0:T(8,128)} %spread.1), calls=%async_computation.3 | async-start | bytes 655360 | tf_op jit(solution)/shard_map/all_to_all | solution.py:413
  104.9 13.1 %all-to-all-done.3.recv_ref = f32[16,40,128]{2,1,0:T(8,128)S(1)} async-done(((f32[16,40,128]{2,1,0:T(8,128)}), f32[16,40,128]{2,1,0:T(8,128)S(1)}, u32[]{:S(2)}, u32[]{:S(2)}) %all-to-all-start.3) | async-done | bytes 327712 | tf_op jit(solution)/shard_map/all_to_all | solution.py:413
  118.0 0.0 copy-start.1
  118.0 1.1 relay.1
  119.1 3.7 %all-to-all-start.4 = ((f32[16,136,128]{2,1,0:T(8,128)}), f32[16,136,128]{2,1,0:T(8,128)S(1)}, u32[]{:S(2)}, u32[]{:S(2)}) async-start(f32[16,136,128]{2,1,0:T(8,128)} %relay.1), calls=%async_computation.4 | async-start | bytes 2228224 | tf_op jit(solution)/shard_map/all_to_all | solution.py:415
  122.8 0.3 collective-permute-start.5
  123.1 2.3 %collective-permute-start.4 = (f32[2,32,1024]{2,1,0:T(8,128)S(1)}, f32[2,32,1024]{2,1,0:T(8,128)S(1)}, u32[]{:S(2)}, u32[]{:S(2)}) collective-permute-start(f32[2,32,1024]{2,1,0:T(8,128)S(1)} %get-tuple-element.57.h0), channel_id=1, source_target_pairs={{8,0},{12,4},{0,8},{4,12},{9,1},{13,5},{1,9},{5,13},{10,2},{14,6},... | collective-permute-start | bytes 786440 | tf_op jit(solution)/shard_map/ppermute | solution.py:358
  125.4 2.0 %collective-permute-start.3 = (f32[2,32,1024]{2,1,0:T(8,128)S(1)}, f32[2,32,1024]{2,1,0:T(8,128)S(1)}, u32[]{:S(2)}, u32[]{:S(2)}) collective-permute-start(f32[2,32,1024]{2,1,0:T(8,128)S(1)} %get-tuple-element.57.h0), channel_id=1, source_target_pairs={{4,0},{8,4},{12,8},{0,12},{5,1},{9,5},{13,9},{1,13},{6,2},{10,6},{... | collective-permute-start | bytes 786440 | tf_op jit(solution)/shard_map/ppermute | solution.py:358
  127.4 9.9 %collective-permute-done.5.h3 = f32[2,32,1024]{2,1,0:T(8,128)S(1)} collective-permute-done((f32[2,32,1024]{2,1,0:T(8,128)S(1)}, f32[2,32,1024]{2,1,0:T(8,128)S(1)}, u32[]{:S(2)}, u32[]{:S(2)}) %collective-permute-start.5) | collective-permute-done | bytes 262176 | tf_op jit(solution)/shard_map/ppermute | solution.py:358
  137.3 8.0 %collective-permute-done.4.h2 = f32[2,32,1024]{2,1,0:T(8,128)S(1)} collective-permute-done((f32[2,32,1024]{2,1,0:T(8,128)S(1)}, f32[2,32,1024]{2,1,0:T(8,128)S(1)}, u32[]{:S(2)}, u32[]{:S(2)}) %collective-permute-start.4) | collective-permute-done | bytes 262176 | tf_op jit(solution)/shard_map/ppermute | solution.py:358
  145.3 6.0 %collective-permute-done.3.h1 = f32[2,32,1024]{2,1,0:T(8,128)S(1)} collective-permute-done((f32[2,32,1024]{2,1,0:T(8,128)S(1)}, f32[2,32,1024]{2,1,0:T(8,128)S(1)}, u32[]{:S(2)}, u32[]{:S(2)}) %collective-permute-start.3) | collective-permute-done | bytes 262176 | tf_op jit(solution)/shard_map/ppermute | solution.py:358
  151.4 0.0 all-to-all-done.4.recv_ref
  151.4 0.0 copy-done.1
  151.4 1.2 last.1
  (1 shorter events, 0.0 us)
Async XLA Ops:
  0.6 1.0 copy-start
  1.7 0.7 copy-start.2
  2.4 0.7 copy-start.3
  3.4 16.4 %collective-permute-start = (f32[40,1024]{1,0:T(8,128)S(1)}, f32[40,1024]{1,0:T(8,128)S(1)}, u32[]{:S(2)}, u32[]{:S(2)}) collective-permute-start(f32[40,1024]{1,0:T(8,128)S(1)} %get-tuple-element.31), channel_id=1, source_target_pairs={{4,0},{8,4},{12,8},{0,12},{5,1},{9,5},{13,9},{1,13},{6,2},{10,6},{... | collective-permute-start | bytes 491528 | tf_op jit(solution)/shard_map/ppermute | solution.py:358
  10.3 12.4 %collective-permute-start.1 = (f32[40,1024]{1,0:T(8,128)S(1)}, f32[40,1024]{1,0:T(8,128)S(1)}, u32[]{:S(2)}, u32[]{:S(2)}) collective-permute-start(f32[40,1024]{1,0:T(8,128)S(1)} %get-tuple-element.32), channel_id=1, source_target_pairs={{8,0},{12,4},{0,8},{4,12},{9,1},{13,5},{1,9},{5,13},{10,2},{14,6},... | collective-permute-start | bytes 491528 | tf_op jit(solution)/shard_map/ppermute | solution.py:358
  11.3 11.7 %collective-permute-start.2 = (f32[40,1024]{1,0:T(8,128)S(1)}, f32[40,1024]{1,0:T(8,128)S(1)}, u32[]{:S(2)}, u32[]{:S(2)}) collective-permute-start(f32[40,1024]{1,0:T(8,128)S(1)} %get-tuple-element.33), channel_id=1, source_target_pairs={{12,0},{0,4},{4,8},{8,12},{13,1},{1,5},{5,9},{9,13},{14,2},{2,6},{... | collective-permute-start | bytes 491528 | tf_op jit(solution)/shard_map/ppermute | solution.py:358
  13.5 0.7 copy-start.4
  88.2 29.8 %all-to-all-start.3 = ((f32[16,40,128]{2,1,0:T(8,128)}), f32[16,40,128]{2,1,0:T(8,128)S(1)}, u32[]{:S(2)}, u32[]{:S(2)}) async-start(f32[16,40,128]{2,1,0:T(8,128)} %spread.1), calls=%async_computation.3 | async-start | bytes 655360 | tf_op jit(solution)/shard_map/all_to_all | solution.py:413
  118.0 33.4 %copy-start.1 = (f32[4,2,16,1024]{3,2,1,0:T(8,128)S(1)}, f32[4,2,16,1024]{3,2,1,0:T(8,128)}, u32[]{:S(2)}) copy-start(f32[4,2,16,1024]{3,2,1,0:T(8,128)} %press_ref.1) | copy-start | bytes 1572868
  119.1 32.3 %all-to-all-start.4 = ((f32[16,136,128]{2,1,0:T(8,128)}), f32[16,136,128]{2,1,0:T(8,128)S(1)}, u32[]{:S(2)}, u32[]{:S(2)}) async-start(f32[16,136,128]{2,1,0:T(8,128)} %relay.1), calls=%async_computation.4 | async-start | bytes 2228224 | tf_op jit(solution)/shard_map/all_to_all | solution.py:415
  122.8 14.5 %collective-permute-start.5 = (f32[2,32,1024]{2,1,0:T(8,128)S(1)}, f32[2,32,1024]{2,1,0:T(8,128)S(1)}, u32[]{:S(2)}, u32[]{:S(2)}) collective-permute-start(f32[2,32,1024]{2,1,0:T(8,128)S(1)} %get-tuple-element.57.h0), channel_id=1, source_target_pairs={{12,0},{0,4},{4,8},{8,12},{13,1},{1,5},{5,9},{9,13},{14,2},{2,6},{... | collective-permute-start | bytes 786440 | tf_op jit(solution)/shard_map/ppermute | solution.py:358
  123.1 22.2 %collective-permute-start.4 = (f32[2,32,1024]{2,1,0:T(8,128)S(1)}, f32[2,32,1024]{2,1,0:T(8,128)S(1)}, u32[]{:S(2)}, u32[]{:S(2)}) collective-permute-start(f32[2,32,1024]{2,1,0:T(8,128)S(1)} %get-tuple-element.57.h0), channel_id=1, source_target_pairs={{8,0},{12,4},{0,8},{4,12},{9,1},{13,5},{1,9},{5,13},{10,2},{14,6},... | collective-permute-start | bytes 786440 | tf_op jit(solution)/shard_map/ppermute | solution.py:358
  125.4 25.9 %collective-permute-start.3 = (f32[2,32,1024]{2,1,0:T(8,128)S(1)}, f32[2,32,1024]{2,1,0:T(8,128)S(1)}, u32[]{:S(2)}, u32[]{:S(2)}) collective-permute-start(f32[2,32,1024]{2,1,0:T(8,128)S(1)} %get-tuple-element.57.h0), channel_id=1, source_target_pairs={{4,0},{8,4},{12,8},{0,12},{5,1},{9,5},{13,9},{1,13},{6,2},{10,6},{... | collective-permute-start | bytes 786440 | tf_op jit(solution)/shard_map/ppermute | solution.py:358

commit v3 on v2

--- a/solution.py
+++ b/solution.py
@@ -15,6 +15,8 @@
 ROWS, LANES, EDGE = 16, 256, 256
 VM = pl.BlockSpec(memory_space=pltpu.VMEM)
 SM = pl.BlockSpec(memory_space=pltpu.SMEM)
+ANY = pl.BlockSpec(memory_space=pl.ANY)
+HBM = pl.BlockSpec(memory_space=pltpu.HBM)
 
 
 def steering(gx, gy, gz, mx, my, mz, turns):
@@ -91,15 +93,39 @@
         image[chunk_odd, :, span(pair)] += dot_nn(v, c_ref[at]) + dot_nn(v2, s_ref[at])
 
 
-def prepare_kernel(mic_ref, press_ref, coords_ref, points_ref, g_ref, o1, o2, o3, pad):
-    for s, out in ((1, o1), (2, o2), (3, o3)):
-        out[0:32] = press_ref[lax.rem(mic_ref[0] + 4 - s, 4)]
-        out[32:35] = coords_ref[...]
-        out[35:40] = jnp.zeros((5, 1024), F32)
-    pad[0:3] = points_ref[...]
+def three(x):
+    high = x.astype(BF16).astype(F32)
+    left = x - high
+    middle = left.astype(BF16).astype(F32)
+    return high, middle, (left - middle).astype(BF16).astype(F32)
+
+
+def prepare_kernel(mic_ref, wave_hbm, press_hbm, coords_hbm, points_hbm, g_ref, turns_ref, p0, p1, p2, p3, *scratch):
+    wave_ref, press, coords, pad, sems = scratch
+    copies = [
+        pltpu.make_async_copy(press_hbm, press, sems.at[0]),
+        pltpu.make_async_copy(coords_hbm, coords, sems.at[1]),
+        pltpu.make_async_copy(points_hbm, pad.at[0:3], sems.at[2]),
+        pltpu.make_async_copy(wave_hbm, wave_ref, sems.at[3]),
+    ]
+    for copy in copies:
+        copy.start()
+    for copy in copies:
+        copy.wait()
+    turns_ref[...] = jnp.full((8, 128), wave_ref[mic_ref[0]] * (0.5 / math.pi), F32)
+    high, middle, low = [part.astype(BF16) for part in three(coords[...])]
+    for s, out in enumerate((p0, p1, p2, p3)):
+        out[0:32] = press[lax.rem(mic_ref[0] + 4 - s, 4)].astype(BF16)
+        out[32:35], out[35:38], out[38:41] = high, middle, low
+        out[41:48] = jnp.zeros((7, 1024), BF16)
     pad[3:8] = jnp.zeros((5, 1024), F32)
     for r in range(8):
         g_ref[r * 128 : r * 128 + 128, :] = pad[:, r * 128 : r * 128 + 128].T
+
+
+def whole_coords(pack):
+    parts = pack[32:48].astype(F32)
+    return (parts[0:3] + parts[3:6]) + parts[6:9]
 
 
 def set_weights(wc, ws, chunk, real, imag, scale):
@@ -111,20 +137,16 @@
     ws[odd, 16:32, cols] = real
 
 
-def turns_of(mic_ref, wave_ref):
-    return wave_ref[mic_ref[0]] * (0.5 / math.pi)
-
-
-def own_kernel(scale, mic_ref, wave_ref, press_ref, coords_ref, grid_ref, *refs):
-    tiles, grad_ref, wc, ws = Tiles(refs[:8]), refs[8], refs[9], refs[10]
-    turns = turns_of(mic_ref, wave_ref)
+def own_kernel(scale, pack, turns_ref, grid_ref, *refs):
+    tiles, grad_ref, wc, ws, coords = Tiles(refs[:8]), refs[8], refs[9], refs[10], refs[11]
+    turns = turns_ref[0:1, 0:1]
     for chunk in range(4):
-        cols = slice(chunk * EDGE, chunk * EDGE + EDGE)
-        w = press_ref[mic_ref[0], :, cols].astype(BF16)
+        w = pack[0:32, chunk * EDGE : chunk * EDGE + EDGE]
         set_weights(wc, ws, chunk, w[0:16], w[16:32], scale)
+    coords[0:3] = whole_coords(pack)
 
     def mics(chunk):
-        return [coords_ref[d : d + 1, chunk * EDGE : chunk * EDGE + EDGE] for d in range(3)]
+        return [coords[d : d + 1, chunk * EDGE : chunk * EDGE + EDGE] for d in range(3)]
 
     def half_step(half, carry):
         late = None
@@ -158,15 +180,15 @@
                     out_ref[c, h, s] = image[odd, h * 16 : h * 16 + 16, lo : lo + 128]
 
 
-def rest_kernel(scale, mic_ref, wave_ref, grid_ref, p1, p2, p3, head_ref, *refs):
+def rest_kernel(scale, turns_ref, grid_ref, p1, p2, p3, head_ref, *refs):
     own, tiles = Tiles(refs[:8]), Tiles(refs[8:16])
     grad_ref, image_ref, wc, ws, near, far, coords = refs[16:]
-    turns = turns_of(mic_ref, wave_ref)
+    turns = turns_ref[0:1, 0:1]
     for s, pack in enumerate((p1, p2, p3)):
         for chunk in range(4):
-            w = pack[0:32, chunk * EDGE : chunk * EDGE + EDGE].astype(BF16)
+            w = pack[0:32, chunk * EDGE : chunk * EDGE + EDGE]
             set_weights(wc, ws, s * 4 + chunk, w[0:16], w[16:32], scale)
-        coords[:, s * 1024 : s * 1024 + 1024] = pack[32:40]
+        coords[0:3, s * 1024 : s * 1024 + 1024] = whole_coords(pack)
     near[...] = jnp.zeros_like(near)
     far[...] = jnp.zeros_like(far)
 
@@ -220,7 +242,7 @@
 
 def again_kernel(scale, q_ref, grad0_ref, *refs):
     own, tiles = Tiles(refs[:8]), Tiles(refs[8:16])
-    both_ref, image_ref, sums_ref, wa, wb, wc, wd, near, far = refs[16:]
+    packed_ref, image_ref, sums_ref, wa, wb, wc, wd, near, far, grad_ref = refs[16:]
     for block in range(4):
         for chunk in range(4):
             real = jnp.concatenate([q_ref[4 * chunk + 2 * p, block] for p in range(2)], axis=1)
@@ -249,8 +271,7 @@
     def finish(half, odd, total):
         cols = span(half * 2 + odd)
         g0 = grad0_ref[:, cols]
-        both_ref[0, :, cols] = g0
-        both_ref[1, :, cols] = total
+        grad_ref[:, cols] = total
         sums_ref[0:1] += lane_sums(g0 * g0)
         sums_ref[1:2] += lane_sums(g0 * total)
         sums_ref[2:3] += lane_sums(total * total)
@@ -265,6 +286,13 @@
     forward(v, 1, 1)
     store_image(image_ref, near, 0)
     store_image(image_ref, far, 1)
+    gg = jnp.sum(sums_ref[0:1], axis=1, keepdims=True)
+    gh = jnp.sum(sums_ref[1:2], axis=1, keepdims=True)
+    along = jnp.where(gg > 0.0, gh / jnp.where(gg > 0.0, gg, 1.0), 0.0)
+    packed_ref[0:32] = grad0_ref[...].astype(BF16)
+    packed_ref[32:64] = (grad_ref[...] - along * grad0_ref[...]).astype(BF16)
+    high, middle, low = [jnp.broadcast_to(part, (1, 1024)) for part in three(along)]
+    packed_ref[64:80] = jnp.concatenate([high, middle, low, jnp.zeros((13, 1024), F32)], axis=0).astype(BF16)
 
 
 def gather_kernel(parts_ref, shard_ref, copies_ref):
@@ -277,7 +305,8 @@
         copies_ref[j] = low
 
 
-def spread_kernel(mic_ref, parts_ref, q_ref, sums_ref, out_ref, shard):
+def spread_kernel(mic_ref, parts_ref, q_ref, sums_ref, *refs):
+    out_ref, shard = refs[3:]
     total = parts_ref[0]
     for j in range(1, 16):
         total += parts_ref[j]
@@ -310,7 +339,10 @@
         out_ref[j, 128:136] = sums
 
 
-def last_kernel(mic_ref, recv_ref, press_ref, h0, h1, h2, h3, x_ref, r_ref):
+def last_kernel(mic_ref, recv_ref, press_hbm, *refs):
+    packs, (x_ref, r_ref, press_ref, sem) = refs[:4], refs[4:]
+    copy = pltpu.make_async_copy(press_hbm, press_ref, sem)
+    copy.start()
     total = recv_ref[0, 128:136]
     for j in range(1, 16):
         total += recv_ref[j, 128:136]
@@ -323,12 +355,18 @@
     step1 = norm1 / image1
     lead = jnp.broadcast_to(step0 + step1 * (1.0 + ratio), (16, 128))
     tail = jnp.broadcast_to(step0 * step1, (16, 128))
-    for s, hop in enumerate((h0, h1, h2, h3)):
+    for s, pack in enumerate(packs):
         bin_at = lax.rem(mic_ref[0] + s, 4)
+        parts = pack[64:80, 0:128].astype(F32)
+        along = (parts[0:1] + parts[1:2]) + parts[2:3]
+        first = lead - tail * along
         for h in range(2):
             for c in range(8):
-                rows, cols = slice(h * 16, h * 16 + 16), slice(c * 128, c * 128 + 128)
-                x_ref[bin_at, h, :, cols] = lead * hop[0, rows, cols] - tail * hop[1, rows, cols]
+                cols = slice(c * 128, c * 128 + 128)
+                g = pack[h * 16 : h * 16 + 16, cols].astype(F32)
+                y = pack[32 + h * 16 : 48 + h * 16, cols].astype(F32)
+                x_ref[bin_at, h, :, cols] = first * g - tail * y
+    copy.wait()
     for m in range(4):
         for h in range(2):
             for c in range(8):
@@ -338,7 +376,7 @@
                 r_ref[m, h, :, cols] = press_ref[m, h, :, cols] - lead * q + tail * p
 
 
-def call(kernel, name, in_specs, out_shape, scratch=(), limit=16):
+def call(kernel, name, in_specs, out_shape, scratch=(), limit=4, work=0):
     return pl.pallas_call(
         kernel,
         in_specs=in_specs,
@@ -346,6 +384,7 @@
         out_shape=out_shape,
         scratch_shapes=list(scratch),
         compiler_params=pltpu.CompilerParams(vmem_limit_bytes=limit << 20),
+        cost_estimate=pl.CostEstimate(flops=work, bytes_accessed=0, transcendentals=0) if work else None,
         name=name,
     )
 
@@ -360,14 +399,24 @@
 
 def body(grid_points, mic_coords, wavenumbers, pressures):
     scale = 1.0 / math.sqrt(grid_points.shape[1] * lax.axis_size("grid"))
-    mic = jnp.reshape(lax.axis_index("mic"), (1,)).astype(jnp.int32)
-    bin_at = jnp.reshape(lax.axis_index("bin"), (1,)).astype(jnp.int32)
+    mic, bin_at = [jnp.reshape(lax.axis_index(name), (1,)).astype(jnp.int32) for name in ("mic", "bin")]
     flat = pressures.reshape(4, 32, 1024)
 
-    points, *packs = call(
-        prepare_kernel, "prepare", [SM, VM, VM, VM], [array(1024, 8)] + [array(40, 1024)] * 3, [pltpu.VMEM((8, 1024), F32)]
-    )(mic, flat, mic_coords, grid_points)
-    packs = [ahead(pack, s) for s, pack in zip((1, 2, 3), packs)]
+    points, turns, *packs = call(
+        prepare_kernel,
+        "prepare",
+        [SM, HBM, HBM, HBM, HBM],
+        [pltpu.VMEM((1024, 8), F32), pltpu.VMEM((8, 128), F32)] + [pltpu.VMEM((48, 1024), BF16)] * 4,
+        [
+            pltpu.SMEM((4,), F32),
+            pltpu.VMEM((4, 32, 1024), F32),
+            pltpu.VMEM((3, 1024), F32),
+            pltpu.VMEM((8, 1024), F32),
+            pltpu.SemaphoreType.DMA((4,)),
+        ],
+        limit=60,
+    )(mic, wavenumbers, flat, mic_coords, grid_points)
+    packs[1:] = [ahead(pack, s) for s, pack in zip((1, 2, 3), packs[1:])]
 
     def held(width):
         return [pltpu.VMEM((512, width), BF16)] * 8
@@ -376,18 +425,21 @@
     weights_far = [pltpu.VMEM((2, 32, 1536), BF16)] * 2
     images = [pltpu.VMEM((2, 32, 512), F32), pltpu.VMEM((2, 32, 1536), F32)]
     *near, head = call(
-        functools.partial(own_kernel, scale), "own", [SM, SM, VM, VM, VM], held(512) + [array(32, 1024)], weights_near
-    )(mic, wavenumbers, flat, mic_coords, points)
+        functools.partial(own_kernel, scale),
+        "own",
+        [VM] * 3,
+        held(512) + [array(32, 1024)],
+        weights_near + [pltpu.VMEM((8, 1024), F32)],
+    )(packs[0], turns, points)
     near = [pltpu.with_memory_space_constraint(t, pltpu.VMEM) for t in near]
     image_type = array(8, 2, 4, 16, 128)
     *far, grad0, part0 = call(
         functools.partial(rest_kernel, scale),
         "rest",
-        [SM, SM] + [VM] * 13,
+        [VM] * 14,
         held(1536) + [array(32, 1024), image_type],
         weights_far + images + [pltpu.VMEM((8, 3072), F32)],
-        limit=32,
-    )(mic, wavenumbers, points, *packs, head, *near)
+    )(turns, points, *packs[1:], head, *near)
     far = [pltpu.with_memory_space_constraint(t, pltpu.VMEM) for t in far]
 
     parts = lax.all_to_all(part0.reshape(16, 4, 16, 128), "grid", 0, 0)
@@ -396,25 +448,31 @@
     )(parts)
     rounded = lax.all_to_all(copies, "grid", 0, 0)
 
-    both, part1, sums = call(
+    packed, part1, sums = call(
         functools.partial(again_kernel, scale),
         "again",
         [VM] * 18,
-        [array(2, 32, 1024), image_type, array(8, EDGE)],
-        weights_near + weights_far + images,
-        limit=32,
+        [array(80, 1024, dtype=BF16), image_type, array(8, EDGE)],
+        weights_near + weights_far + images + [pltpu.VMEM((32, 1024), F32)],
+        work=8 << 30,
     )(rounded, grad0, *near, *far)
 
-    hops = [both] + [ahead(both, s) for s in (1, 2, 3)]
+    hops = [packed] + [ahead(packed, s) for s in (1, 2, 3)]
     parts = lax.all_to_all(part1.reshape(16, 4, 16, 128), "grid", 0, 0)
-    sent = call(spread_kernel, "spread", [SM, VM, VM, VM], array(16, 40, 128), [pltpu.VMEM((4, 16, 128), F32)])(
-        mic, parts, image0, sums
-    )
+    sent = call(
+        spread_kernel, "spread", [SM, VM, VM, VM] + [ANY] * 3, array(16, 40, 128), [pltpu.VMEM((4, 16, 128), F32)]
+    )(mic, parts, image0, sums, *hops[1:])
     recv = lax.all_to_all(sent, ("mic", "bin"), 0, 0)
     sent = call(relay_kernel, "relay", [SM, VM], array(16, 136, 128))(bin_at, recv)
     recv = lax.all_to_all(sent, "grid", 0, 0)
     out_type = array(4, 2, 16, 1024)
-    return call(last_kernel, "last", [SM] + [VM] * 6, [out_type, out_type])(mic, recv, pressures, *hops)
+    return call(
+        last_kernel,
+        "last",
+        [SM, VM, HBM] + [VM] * 4,
+        [out_type, out_type],
+        [pltpu.VMEM((4, 2, 16, 1024), F32), pltpu.SemaphoreType.DMA],
+    )(mic, recv, pressures, *hops)
 
 
 def solution(mesh):

time: 153 us -> 146 us (0.954)
  blocking collectives: 37.5 us -> 50.8 us
  waiting for transfers between devices: 40.2 us -> 28 us
  starting transfers between devices: 35.2 us -> 30.5 us
  local copies, waits for them, and re-layouts: 3.13 us -> 0.01 us
    all_to_all x1, blocking collectives: 11.6 us -> 24.9 us  [body(): recv = lax.all_to_all(sent, 'grid', 0, 0)]
    ppermute x6, waiting for transfers between devices: 27.1 us -> 14.9 us  [ahead(): return lax.ppermute(x, 'mic', [((t + shift) % 4, t) for t in range(4)])]
    all_to_all x1, starting transfers between devices: 16.7 us -> 7.4 us  [body(): recv = lax.all_to_all(sent, ('mic', 'bin'), 0, 0)]
    ppermute x6, starting transfers between devices: 14.8 us -> 19.5 us  [ahead(): return lax.ppermute(x, 'mic', [((t + shift) % 4, t) for t in range(4)])]
    unnamed x10 -> x2, local copies, waits for them, and re-layouts: 3.13 us -> 0.01 us
  transfers between devices with their start and end apart: 8 -> 8, of which waited for: 6 -> 5; matrix products, arithmetic and copies ran while one was open for 0% -> 0% of each run, Pallas kernels for 4% -> 3%
where the time goes in v3:
time: 146 us
  blocking collectives  50.8 us (35%)
  Pallas kernels  35.7 us (24%)
  starting transfers between devices  30.5 us (21%)
  waiting for transfers between devices  28 us (19%)
    all_to_all x1, blocking collectives, body(): recv = lax.all_to_all(sent, 'grid', 0, 0)  24.9 us
    ppermute x6, starting transfers between devices, ahead(): return lax.ppermute(x, 'mic', [((t + shift) % 4, t) for t in range(4)])  19.5 us
    pallas_call x1, Pallas kernels, body(): call(functools.partial(rest_kernel, scale), 'rest', [VM] * 14, held(1536)...  18.5 us
    all_to_all x1, blocking collectives, body(): parts = lax.all_to_all(part0.reshape(16, 4, 16, 128), 'grid', 0, 0)  15.7 us
    ppermute x6, waiting for transfers between devices, ahead(): return lax.ppermute(x, 'mic', [((t + shift) % 4, t) for t in range(4)])  14.9 us
    all_to_all x1, waiting for transfers between devices, body(): recv = lax.all_to_all(sent, ('mic', 'bin'), 0, 0)  13.1 us
    all_to_all x1, blocking collectives, body(): rounded = lax.all_to_all(copies, 'grid', 0, 0)  10.1 us
    pallas_call x1, Pallas kernels, body(): call(functools.partial(again_kernel, scale), 'again', [VM] * 18, [array(8...  8.57 us
  transfers between devices with their start and end apart: 8, of which 5 were waited for; matrix products, arithmetic and copies ran while one was open for 0% of the time, Pallas kernels for 3%

profile of v3, /device:TPU:1, one launch (start us, length us, event | category | flops | bytes accessed | tf_op | source)
XLA Modules:
  0.0 145.7 jit_solution(8337197723586838028)
XLA Ops:
  0.6 1.3 prepare.1
  2.0 6.9 %collective-permute-start = (bf16[48,1024]{1,0:T(8,128)(2,1)S(1)}, bf16[48,1024]{1,0:T(8,128)(2,1)S(1)}, u32[]{:S(2)}, u32[]{:S(2)}) collective-permute-start(bf16[48,1024]{1,0:T(8,128)(2,1)S(1)} %get-tuple-element.34), channel_id=1, source_target_pairs={{4,0},{8,4},{12,8},{0,12},{5,1},{9,5},{13,9},{1,13},{6,2},{10,6},{... | collective-permute-start | bytes 294920 | tf_op jit(solution)/shard_map/ppermute | solution.py:397
  8.9 1.0 collective-permute-start.1
  9.9 2.3 %collective-permute-start.2 = (bf16[48,1024]{1,0:T(8,128)(2,1)S(1)}, bf16[48,1024]{1,0:T(8,128)(2,1)S(1)}, u32[]{:S(2)}, u32[]{:S(2)}) collective-permute-start(bf16[48,1024]{1,0:T(8,128)(2,1)S(1)} %get-tuple-element.36), channel_id=1, source_target_pairs={{12,0},{0,4},{4,8},{8,12},{13,1},{1,5},{5,9},{9,13},{14,2},{2,6},{... | collective-permute-start | bytes 294920 | tf_op jit(solution)/shard_map/ppermute | solution.py:397
  12.1 5.1 %own.1 = (bf16[512,512]{1,0:T(8,128)(2,1)S(1)}, bf16[512,512]{1,0:T(8,128)(2,1)S(1)}, bf16[512,512]{1,0:T(8,128)(2,1)S(1)}, bf16[512,512]{1,0:T(8,128)(2,1)S(1)}...) custom-call(bf16[48,1024]{1,0:T(8,128)(2,1)S(1)} %get-tuple-element., ...), custom_call_target="tpu_custom_call" | custom-call | tf_op jit(solution)/shard_map/own/pallas_call | solution.py:427
  17.2 0.0 collective-permute-done.p1
  17.2 0.2 collective-permute-done.1.p2
  17.5 0.7 collective-permute-done.2.p3
  18.2 18.5 %rest.1 = (bf16[512,1536]{1,0:T(8,128)(2,1)S(1)}, bf16[512,1536]{1,0:T(8,128)(2,1)S(1)}, bf16[512,1536]{1,0:T(8,128)(2,1)S(1)}, bf16[512,1536]{1,0:T(8,128)(2,1)...) custom-call(f32[8,128]{1,0:T(8,128)S(1)} %get-tuple-element.32.turns, ...), custom_call_target="tpu_custom_call" | custom-call | tf_op jit(solution)/shard_map/rest/pallas_call | solution.py:436
  36.7 15.7 %all_to_all.25.parts_ref = f32[16,4,16,128]{3,2,1,0:T(8,128)S(1)} all-to-all(f32[16,4,16,128]{3,2,1,0:T(8,128)S(1)} %bitcast.6), channel_id=1, replica_groups=mesh['grid'=16,'mic'=4,'bin'=4] {'grid'}, dimensions={0} | all-to-all | bytes 1048576 | tf_op jit(solution)/shard_map/all_to_all | solution.py:445
  52.4 10.1 %all_to_all.26.q_ref = bf16[16,4,16,128]{3,2,1,0:T(8,128)(2,1)S(1)} all-to-all(bf16[16,4,16,128]{3,2,1,0:T(8,128)(2,1)S(1)} %get-tuple-element.48), channel_id=1, replica_groups=mesh['grid'=16,'mic'=4,'bin'=4] {'grid'}, dimensions={0} | all-to-all | bytes 524288 | tf_op jit(solution)/shard_map/all_to_all | solution.py:449
  62.6 8.6 %again.1 = (bf16[80,1024]{1,0:T(8,128)(2,1)S(1)}, f32[8,2,4,16,128]{4,3,2,1,0:T(8,128)}, f32[8,256]{1,0:T(8,128)S(1)}) custom-call(bf16[16,4,16,128]{3,2,1,0:T(8,128)(2,1)S(1)} %all_to_all.26.q_ref, f32[32,1024]{1,0:T(8,128)S(1)} %get-tuple-element.49.grad0_ref, bf16[512,512]{1,0:T(8,128)(2,1)S(1)} %get-tuple-element.39.refs_0_, ...), custom_call_target="tpu_custom_call" | custom-call | flops 8589934592 | tf_op jit(solution)/shard_map/again/pallas_call | solution.py:451
  71.1 3.6 %all-to-all-start.2 = ((f32[16,4,16,128]{3,2,1,0:T(8,128)}), f32[16,4,16,128]{3,2,1,0:T(8,128)S(1)}, u32[]{:S(2)}, u32[]{:S(2)}) async-start(f32[16,4,16,128]{3,2,1,0:T(8,128)} %bitcast.4), calls=%async_computation.2 | async-start | bytes 1048576 | tf_op jit(solution)/shard_map/all_to_all | solution.py:461
  74.7 3.6 %collective-permute-start.5 = (bf16[80,1024]{1,0:T(8,128)(2,1)S(1)}, bf16[80,1024]{1,0:T(8,128)(2,1)S(1)}, u32[]{:S(2)}, u32[]{:S(2)}) collective-permute-start(bf16[80,1024]{1,0:T(8,128)(2,1)S(1)} %get-tuple-element.61.refs_0_), channel_id=1, source_target_pairs={{12,0},{0,4},{4,8},{8,12},{13,1},{1,5},{5,9},{9,13},{14,2},{2,6},{... | collective-permute-start | bytes 491528 | tf_op jit(solution)/shard_map/ppermute | solution.py:397
  78.3 2.2 %collective-permute-start.4 = (bf16[80,1024]{1,0:T(8,128)(2,1)S(1)}, bf16[80,1024]{1,0:T(8,128)(2,1)S(1)}, u32[]{:S(2)}, u32[]{:S(2)}) collective-permute-start(bf16[80,1024]{1,0:T(8,128)(2,1)S(1)} %get-tuple-element.61.refs_0_), channel_id=1, source_target_pairs={{8,0},{12,4},{0,8},{4,12},{9,1},{13,5},{1,9},{5,13},{10,2},{14,6},... | collective-permute-start | bytes 491528 | tf_op jit(solution)/shard_map/ppermute | solution.py:397
  80.6 3.5 %collective-permute-start.3 = (bf16[80,1024]{1,0:T(8,128)(2,1)S(1)}, bf16[80,1024]{1,0:T(8,128)(2,1)S(1)}, u32[]{:S(2)}, u32[]{:S(2)}) collective-permute-start(bf16[80,1024]{1,0:T(8,128)(2,1)S(1)} %get-tuple-element.61.refs_0_), channel_id=1, source_target_pairs={{4,0},{8,4},{12,8},{0,12},{5,1},{9,5},{13,9},{1,13},{6,2},{10,6},{... | collective-permute-start | bytes 491528 | tf_op jit(solution)/shard_map/ppermute | solution.py:397
  84.0 0.0 collective-permute-done.5.refs_2_.refs_3_
  84.0 2.6 %collective-permute-done.4.refs_1_.refs_2_ = bf16[80,1024]{1,0:T(8,128)(2,1)S(1)} collective-permute-done((bf16[80,1024]{1,0:T(8,128)(2,1)S(1)}, bf16[80,1024]{1,0:T(8,128)(2,1)S(1)}, u32[]{:S(2)}, u32[]{:S(2)}) %collective-permute-start.4) | collective-permute-done | bytes 163872 | tf_op jit(solution)/shard_map/ppermute | solution.py:397
  86.7 11.3 %collective-permute-done.3.refs_0_.refs_1_ = bf16[80,1024]{1,0:T(8,128)(2,1)S(1)} collective-permute-done((bf16[80,1024]{1,0:T(8,128)(2,1)S(1)}, bf16[80,1024]{1,0:T(8,128)(2,1)S(1)}, u32[]{:S(2)}, u32[]{:S(2)}) %collective-permute-start.3) | collective-permute-done | bytes 163872 | tf_op jit(solution)/shard_map/ppermute | solution.py:397
  98.0 0.0 all-to-all-done.2.parts_ref
  98.0 0.8 spread.1
  98.8 7.4 %all-to-all-start.3 = ((f32[16,40,128]{2,1,0:T(8,128)}), f32[16,40,128]{2,1,0:T(8,128)S(1)}, u32[]{:S(2)}, u32[]{:S(2)}) async-start(f32[16,40,128]{2,1,0:T(8,128)} %spread.1), calls=%async_computation.3 | async-start | bytes 655360 | tf_op jit(solution)/shard_map/all_to_all | solution.py:465
  106.2 13.1 %all-to-all-done.3.recv_ref = f32[16,40,128]{2,1,0:T(8,128)S(1)} async-done(((f32[16,40,128]{2,1,0:T(8,128)}), f32[16,40,128]{2,1,0:T(8,128)S(1)}, u32[]{:S(2)}, u32[]{:S(2)}) %all-to-all-start.3) | async-done | bytes 327712 | tf_op jit(solution)/shard_map/all_to_all | solution.py:465
  119.2 0.0 copy-start
  119.2 0.1 relay.1
  119.3 24.9 %all_to_all.27.recv_ref = f32[16,136,128]{2,1,0:T(8,128)S(1)} all-to-all(f32[16,136,128]{2,1,0:T(8,128)S(1)} %relay.1), channel_id=1, replica_groups=mesh['grid'=16,'mic'=4,'bin'=4] {'grid'}, dimensions={0} | all-to-all | bytes 2228224 | tf_op jit(solution)/shard_map/all_to_all | solution.py:467
  144.3 0.0 copy-done
  144.3 1.3 last.1
  (1 shorter events, 0.0 us)
Async XLA Ops:
  2.0 15.3 %collective-permute-start = (bf16[48,1024]{1,0:T(8,128)(2,1)S(1)}, bf16[48,1024]{1,0:T(8,128)(2,1)S(1)}, u32[]{:S(2)}, u32[]{:S(2)}) collective-permute-start(bf16[48,1024]{1,0:T(8,128)(2,1)S(1)} %get-tuple-element.34), channel_id=1, source_target_pairs={{4,0},{8,4},{12,8},{0,12},{5,1},{9,5},{13,9},{1,13},{6,2},{10,6},{... | collective-permute-start | bytes 294920 | tf_op jit(solution)/shard_map/ppermute | solution.py:397
  8.9 8.6 %collective-permute-start.1 = (bf16[48,1024]{1,0:T(8,128)(2,1)S(1)}, bf16[48,1024]{1,0:T(8,128)(2,1)S(1)}, u32[]{:S(2)}, u32[]{:S(2)}) collective-permute-start(bf16[48,1024]{1,0:T(8,128)(2,1)S(1)} %get-tuple-element.35), channel_id=1, source_target_pairs={{8,0},{12,4},{0,8},{4,12},{9,1},{13,5},{1,9},{5,13},{10,2},{14,6},... | collective-permute-start | bytes 294920 | tf_op jit(solution)/shard_map/ppermute | solution.py:397
  9.9 8.3 %collective-permute-start.2 = (bf16[48,1024]{1,0:T(8,128)(2,1)S(1)}, bf16[48,1024]{1,0:T(8,128)(2,1)S(1)}, u32[]{:S(2)}, u32[]{:S(2)}) collective-permute-start(bf16[48,1024]{1,0:T(8,128)(2,1)S(1)} %get-tuple-element.36), channel_id=1, source_target_pairs={{12,0},{0,4},{4,8},{8,12},{13,1},{1,5},{5,9},{9,13},{14,2},{2,6},{... | collective-permute-start | bytes 294920 | tf_op jit(solution)/shard_map/ppermute | solution.py:397
  71.1 26.9 %all-to-all-start.2 = ((f32[16,4,16,128]{3,2,1,0:T(8,128)}), f32[16,4,16,128]{3,2,1,0:T(8,128)S(1)}, u32[]{:S(2)}, u32[]{:S(2)}) async-start(f32[16,4,16,128]{3,2,1,0:T(8,128)} %bitcast.4), calls=%async_computation.2 | async-start | bytes 1048576 | tf_op jit(solution)/shard_map/all_to_all | solution.py:461
  74.7 9.3 %collective-permute-start.5 = (bf16[80,1024]{1,0:T(8,128)(2,1)S(1)}, bf16[80,1024]{1,0:T(8,128)(2,1)S(1)}, u32[]{:S(2)}, u32[]{:S(2)}) collective-permute-start(bf16[80,1024]{1,0:T(8,128)(2,1)S(1)} %get-tuple-element.61.refs_0_), channel_id=1, source_target_pairs={{12,0},{0,4},{4,8},{8,12},{13,1},{1,5},{5,9},{9,13},{14,2},{2,6},{... | collective-permute-start | bytes 491528 | tf_op jit(solution)/shard_map/ppermute | solution.py:397
  78.3 8.4 %collective-permute-start.4 = (bf16[80,1024]{1,0:T(8,128)(2,1)S(1)}, bf16[80,1024]{1,0:T(8,128)(2,1)S(1)}, u32[]{:S(2)}, u32[]{:S(2)}) collective-permute-start(bf16[80,1024]{1,0:T(8,128)(2,1)S(1)} %get-tuple-element.61.refs_0_), channel_id=1, source_target_pairs={{8,0},{12,4},{0,8},{4,12},{9,1},{13,5},{1,9},{5,13},{10,2},{14,6},... | collective-permute-start | bytes 491528 | tf_op jit(solution)/shard_map/ppermute | solution.py:397
  80.6 17.4 %collective-permute-start.3 = (bf16[80,1024]{1,0:T(8,128)(2,1)S(1)}, bf16[80,1024]{1,0:T(8,128)(2,1)S(1)}, u32[]{:S(2)}, u32[]{:S(2)}) collective-permute-start(bf16[80,1024]{1,0:T(8,128)(2,1)S(1)} %get-tuple-element.61.refs_0_), channel_id=1, source_target_pairs={{4,0},{8,4},{12,8},{0,12},{5,1},{9,5},{13,9},{1,13},{6,2},{10,6},{... | collective-permute-start | bytes 491528 | tf_op jit(solution)/shard_map/ppermute | solution.py:397
  98.8 20.5 %all-to-all-start.3 = ((f32[16,40,128]{2,1,0:T(8,128)}), f32[16,40,128]{2,1,0:T(8,128)S(1)}, u32[]{:S(2)}, u32[]{:S(2)}) async-start(f32[16,40,128]{2,1,0:T(8,128)} %spread.1), calls=%async_computation.3 | async-start | bytes 655360 | tf_op jit(solution)/shard_map/all_to_all | solution.py:465
  119.2 25.0 %copy-start = (f32[4,2,16,1024]{3,2,1,0:T(8,128)S(1)}, f32[4,2,16,1024]{3,2,1,0:T(8,128)}, u32[]{:S(2)}) copy-start(f32[4,2,16,1024]{3,2,1,0:T(8,128)} %press_hbm.1) | copy-start | bytes 1572868

commit v4 on v3

--- a/solution.py
+++ b/solution.py
@@ -177,7 +177,7 @@
                 s, c = tile // 8 + first, tile % 8
                 lo = pair * EDGE + piece * 128
                 for h in range(2):
-                    out_ref[c, h, s] = image[odd, h * 16 : h * 16 + 16, lo : lo + 128]
+                    out_ref[c, h, s] = image[odd, h * 16 : h * 16 + 16, lo : lo + 128].astype(BF16)
 
 
 def rest_kernel(scale, turns_ref, grid_ref, p1, p2, p3, head_ref, *refs):
@@ -242,7 +242,7 @@
 
 def again_kernel(scale, q_ref, grad0_ref, *refs):
     own, tiles = Tiles(refs[:8]), Tiles(refs[8:16])
-    packed_ref, image_ref, sums_ref, wa, wb, wc, wd, near, far, grad_ref = refs[16:]
+    packed_ref, image_ref, sums_ref, along_ref, wa, wb, wc, wd, near, far, grad_ref = refs[16:]
     for block in range(4):
         for chunk in range(4):
             real = jnp.concatenate([q_ref[4 * chunk + 2 * p, block] for p in range(2)], axis=1)
@@ -288,64 +288,97 @@
     store_image(image_ref, far, 1)
     gg = jnp.sum(sums_ref[0:1], axis=1, keepdims=True)
     gh = jnp.sum(sums_ref[1:2], axis=1, keepdims=True)
-    along = jnp.where(gg > 0.0, gh / jnp.where(gg > 0.0, gg, 1.0), 0.0)
+    along = coefficient(gg, gh)
+    along_ref[...] = jnp.broadcast_to(along, (8, 128))
     packed_ref[0:32] = grad0_ref[...].astype(BF16)
     packed_ref[32:64] = (grad_ref[...] - along * grad0_ref[...]).astype(BF16)
-    high, middle, low = [jnp.broadcast_to(part, (1, 1024)) for part in three(along)]
-    packed_ref[64:80] = jnp.concatenate([high, middle, low, jnp.zeros((13, 1024), F32)], axis=0).astype(BF16)
+
+
+def coefficient(aa, ab):
+    value = jnp.where(aa > 0.0, ab / jnp.where(aa > 0.0, aa, 1.0), 0.0)
+    return value.astype(BF16).astype(F32)
+
+
+def total_of(parts_ref):
+    total = parts_ref[0].astype(F32)
+    for j in range(1, 16):
+        total += parts_ref[j].astype(F32)
+    return total
 
 
 def gather_kernel(parts_ref, shard_ref, copies_ref):
-    total = parts_ref[0]
-    for j in range(1, 16):
-        total += parts_ref[j]
+    total = total_of(parts_ref)
     shard_ref[...] = total
     low = total.astype(BF16)
     for j in range(16):
         copies_ref[j] = low
 
 
-def spread_kernel(mic_ref, parts_ref, q_ref, sums_ref, *refs):
-    out_ref, shard = refs[3:]
-    total = parts_ref[0]
-    for j in range(1, 16):
-        total += parts_ref[j]
-    shard[...] = total
+def pack_sums(sums, rest):
+    high, middle, low = three(sums[:, 0:64] + sums[:, 64:128])
+    left = jnp.concatenate([high, low], axis=0)
+    right = jnp.concatenate([middle, jnp.zeros_like(low)], axis=0)
+    return jnp.concatenate([jnp.concatenate([left, right], axis=1), rest], axis=0).astype(BF16)
+
+
+def unpack_sums(tile):
+    tile = tile.astype(F32)
+    return tile[0:6] + jnp.concatenate([tile[6:12, 0:64], jnp.zeros((6, 64), F32)], axis=1), tile[12:16]
+
+
+def spread_kernel(mic_ref, parts_ref, q_ref, sums_ref, along_ref, out_ref, shard):
+    total = total_of(parts_ref)
     q = q_ref[...]
 
     def flat(x):
         return lane_sums(x.reshape(64, 128))
 
     near = sums_ref[0:3, 0:128] + sums_ref[0:3, 128:256]
-    sums = jnp.concatenate([near, flat(q * q), flat(q * total), flat(total * total), jnp.zeros((2, 128), F32)], axis=0)
+    qq, qp = flat(q * q), flat(q * total)
+    sums = jnp.concatenate([near, qq, qp, flat(total * total)], axis=0)
+    along = coefficient(jnp.sum(qq, axis=1, keepdims=True), jnp.sum(qp, axis=1, keepdims=True))
+    shard[...] = total - along * q
+    rest = jnp.concatenate([jnp.broadcast_to(along, (1, 128)), along_ref[0:1], jnp.zeros((2, 128), F32)], axis=0)
+    tile = pack_sums(sums, rest)
     for t in range(4):
         s = lax.rem(t + 4 - mic_ref[0], 4)
-        a, b = q_ref[s], shard[s]
+        a = q_ref[s]
+        high = a.astype(BF16)
+        middle = (a - high.astype(F32)).astype(BF16)
+        off = shard[s].astype(BF16)
         for k in range(4):
-            out_ref[t * 4 + k, 0:16] = a
-            out_ref[t * 4 + k, 16:32] = b
-            out_ref[t * 4 + k, 32:40] = sums
-
-
-def relay_kernel(bin_ref, recv_ref, out_ref):
-    sums = recv_ref[0, 32:40]
+            out_ref[t * 4 + k, 0:16] = high
+            out_ref[t * 4 + k, 16:32] = middle
+            out_ref[t * 4 + k, 32:48] = off
+            out_ref[t * 4 + k, 48:64] = tile
+
+
+def relay_kernel(bin_ref, recv_ref, out_ref, along_ref):
+    sums = unpack_sums(recv_ref[0, 48:64])[0]
     for j in range(1, 16):
-        sums += recv_ref[j, 32:40]
+        sums += unpack_sums(recv_ref[j, 48:64])[0]
+    rest = []
     for m in range(4):
-        piece = recv_ref[m * 4 + bin_ref[0], 0:32]
+        slot = m * 4 + bin_ref[0]
+        piece = recv_ref[slot, 0:48]
         for j in range(16):
-            out_ref[j, m * 32 : m * 32 + 32] = piece
+            out_ref[j, m * 48 : m * 48 + 48] = piece
+        values = recv_ref[slot, 48:64].astype(F32)
+        rest.append(values[12:13])
+        along_ref[m : m + 1] = values[13:14]
+    along_ref[4:8] = jnp.zeros((4, 128), F32)
+    tile = pack_sums(sums, jnp.concatenate(rest, axis=0))
     for j in range(16):
-        out_ref[j, 128:136] = sums
-
-
-def last_kernel(mic_ref, recv_ref, press_hbm, *refs):
+        out_ref[j, 192:208] = tile
+
+
+def last_kernel(mic_ref, recv_ref, along_ref, press_hbm, *refs):
     packs, (x_ref, r_ref, press_ref, sem) = refs[:4], refs[4:]
     copy = pltpu.make_async_copy(press_hbm, press_ref, sem)
     copy.start()
-    total = recv_ref[0, 128:136]
+    total = unpack_sums(recv_ref[0, 192:208])[0]
     for j in range(1, 16):
-        total += recv_ref[j, 128:136]
+        total += unpack_sums(recv_ref[j, 192:208])[0]
     total = jnp.sum(total, axis=1, keepdims=True)
     gg, gh, hh, qq, qp, pp = [total[i : i + 1] for i in range(6)]
     step0 = gg / qq
@@ -357,9 +390,7 @@
     tail = jnp.broadcast_to(step0 * step1, (16, 128))
     for s, pack in enumerate(packs):
         bin_at = lax.rem(mic_ref[0] + s, 4)
-        parts = pack[64:80, 0:128].astype(F32)
-        along = (parts[0:1] + parts[1:2]) + parts[2:3]
-        first = lead - tail * along
+        first = lead - tail * along_ref[pl.ds(bin_at, 1)]
         for h in range(2):
             for c in range(8):
                 cols = slice(c * 128, c * 128 + 128)
@@ -367,13 +398,14 @@
                 y = pack[32 + h * 16 : 48 + h * 16, cols].astype(F32)
                 x_ref[bin_at, h, :, cols] = first * g - tail * y
     copy.wait()
-    for m in range(4):
-        for h in range(2):
-            for c in range(8):
-                cols = slice(c * 128, c * 128 + 128)
-                q = recv_ref[2 * c + h, m * 32 : m * 32 + 16]
-                p = recv_ref[2 * c + h, m * 32 + 16 : m * 32 + 32]
-                r_ref[m, h, :, cols] = press_ref[m, h, :, cols] - lead * q + tail * p
+    for h in range(2):
+        for c in range(8):
+            j, cols = 2 * c + h, slice(c * 128, c * 128 + 128)
+            rest = unpack_sums(recv_ref[j, 192:208])[1]
+            for m in range(4):
+                q = recv_ref[j, m * 48 : m * 48 + 16].astype(F32) + recv_ref[j, m * 48 + 16 : m * 48 + 32].astype(F32)
+                off = recv_ref[j, m * 48 + 32 : m * 48 + 48].astype(F32)
+                r_ref[m, h, :, cols] = press_ref[m, h, :, cols] - (lead - tail * rest[m : m + 1]) * q + tail * off
 
 
 def call(kernel, name, in_specs, out_shape, scratch=(), limit=4, work=0):
@@ -432,7 +464,7 @@
         weights_near + [pltpu.VMEM((8, 1024), F32)],
     )(packs[0], turns, points)
     near = [pltpu.with_memory_space_constraint(t, pltpu.VMEM) for t in near]
-    image_type = array(8, 2, 4, 16, 128)
+    image_type = array(8, 2, 4, 16, 128, dtype=BF16)
     *far, grad0, part0 = call(
         functools.partial(rest_kernel, scale),
         "rest",
@@ -448,11 +480,11 @@
     )(parts)
     rounded = lax.all_to_all(copies, "grid", 0, 0)
 
-    packed, part1, sums = call(
+    packed, part1, sums, along = call(
         functools.partial(again_kernel, scale),
         "again",
         [VM] * 18,
-        [array(80, 1024, dtype=BF16), image_type, array(8, EDGE)],
+        [array(64, 1024, dtype=BF16), image_type, array(8, EDGE), array(8, 128)],
         weights_near + weights_far + images + [pltpu.VMEM((32, 1024), F32)],
         work=8 << 30,
     )(rounded, grad0, *near, *far)
@@ -460,19 +492,19 @@
     hops = [packed] + [ahead(packed, s) for s in (1, 2, 3)]
     parts = lax.all_to_all(part1.reshape(16, 4, 16, 128), "grid", 0, 0)
     sent = call(
-        spread_kernel, "spread", [SM, VM, VM, VM] + [ANY] * 3, array(16, 40, 128), [pltpu.VMEM((4, 16, 128), F32)]
-    )(mic, parts, image0, sums, *hops[1:])
+        spread_kernel, "spread", [SM] + [VM] * 4, array(16, 64, 128, dtype=BF16), [pltpu.VMEM((4, 16, 128), F32)]
+    )(mic, parts, image0, sums, along)
     recv = lax.all_to_all(sent, ("mic", "bin"), 0, 0)
-    sent = call(relay_kernel, "relay", [SM, VM], array(16, 136, 128))(bin_at, recv)
+    sent, alongs = call(relay_kernel, "relay", [SM, VM], [array(16, 208, 128, dtype=BF16), array(8, 128)])(bin_at, recv)
     recv = lax.all_to_all(sent, "grid", 0, 0)
     out_type = array(4, 2, 16, 1024)
     return call(
         last_kernel,
         "last",
-        [SM, VM, HBM] + [VM] * 4,
+        [SM, VM, VM, HBM] + [VM] * 4,
         [out_type, out_type],
         [pltpu.VMEM((4, 2, 16, 1024), F32), pltpu.SemaphoreType.DMA],
-    )(mic, recv, pressures, *hops)
+    )(mic, recv, alongs, pressures, *hops)
 
 
 def solution(mesh):

time: 146 us -> 129 us (0.88)
  blocking collectives: 50.8 us -> 34.3 us
  waiting for transfers between devices: 28 us -> 25.4 us
  starting transfers between devices: 30.5 us -> 32 us
    all_to_all x1, blocking collectives: 24.9 us -> 10.2 us  [body(): parts = lax.all_to_all(part1.reshape(16, 4, 16, 128), 'grid', 0, 0)]
    all_to_all x1, starting transfers between devices: 7.4 us -> 13.7 us  [body(): recv = lax.all_to_all(sent, ('mic', 'bin'), 0, 0)]
    ppermute x6, starting transfers between devices: 19.5 us -> 14.8 us  [ahead(): return lax.ppermute(x, 'mic', [((t + shift) % 4, t) for t in range(4)])]
    all_to_all x1, blocking collectives: 15.7 us -> 13.9 us  [body(): parts = lax.all_to_all(part0.reshape(16, 4, 16, 128), 'grid', 0, 0)]
  transfers between devices with their start and end apart: 8 -> 8, of which waited for: 5 -> 6; matrix products, arithmetic and copies ran while one was open for 0% -> 0% of each run, Pallas kernels for 3% -> 4%
where the time goes in v4:
time: 129 us
  Pallas kernels  36.1 us (28%)
  blocking collectives  34.3 us (27%)
  starting transfers between devices  32 us (25%)
  waiting for transfers between devices  25.4 us (20%)
    pallas_call x1, Pallas kernels, body(): call(functools.partial(rest_kernel, scale), 'rest', [VM] * 14, held(1536)...  18.6 us
    ppermute x6, starting transfers between devices, ahead(): return lax.ppermute(x, 'mic', [((t + shift) % 4, t) for t in range(4)])  14.8 us
    all_to_all x1, blocking collectives, body(): parts = lax.all_to_all(part0.reshape(16, 4, 16, 128), 'grid', 0, 0)  13.9 us
    ppermute x6, waiting for transfers between devices, ahead(): return lax.ppermute(x, 'mic', [((t + shift) % 4, t) for t in range(4)])  13.7 us
    all_to_all x1, starting transfers between devices, body(): recv = lax.all_to_all(sent, ('mic', 'bin'), 0, 0)  13.7 us
    all_to_all x1, waiting for transfers between devices, body(): recv = lax.all_to_all(sent, ('mic', 'bin'), 0, 0)  11.7 us
    all_to_all x1, blocking collectives, body(): parts = lax.all_to_all(part1.reshape(16, 4, 16, 128), 'grid', 0, 0)  10.2 us
    all_to_all x1, blocking collectives, body(): rounded = lax.all_to_all(copies, 'grid', 0, 0)  10.2 us
  transfers between devices with their start and end apart: 8, of which 6 were waited for; matrix products, arithmetic and copies ran while one was open for 0% of the time, Pallas kernels for 4%

profile of v4, /device:TPU:1, one launch (start us, length us, event | category | flops | bytes accessed | tf_op | source)
XLA Modules:
  0.0 128.7 jit_solution(2698098675172586273)
XLA Ops:
  0.6 1.3 %prepare.1 = (f32[1024,8]{1,0:T(8,128)S(1)}, f32[8,128]{1,0:T(8,128)S(1)}, bf16[48,1024]{1,0:T(8,128)(2,1)S(1)}, bf16[48,1024]{1,0:T(8,128)(2,1)S(1)}, bf16[48,1...) custom-call(s32[1]{0:T(128)} %bitcast.mic_ref, f32[4]{0:T(128)} %wave_hbm.1, f32[4,32,1024]{2,1,0:T(8,128)} %bitcast.5, ...), custom_call_target="tpu_custom_call" | custom-call | tf_op jit(solution)/shard_map/prepare/pallas_call | solution.py:437
  2.0 6.9 %collective-permute-start = (bf16[48,1024]{1,0:T(8,128)(2,1)S(1)}, bf16[48,1024]{1,0:T(8,128)(2,1)S(1)}, u32[]{:S(2)}, u32[]{:S(2)}) collective-permute-start(bf16[48,1024]{1,0:T(8,128)(2,1)S(1)} %get-tuple-element.37), channel_id=1, source_target_pairs={{4,0},{8,4},{12,8},{0,12},{5,1},{9,5},{13,9},{1,13},{6,2},{10,6},{... | collective-permute-start | bytes 294920 | tf_op jit(solution)/shard_map/ppermute | solution.py:429
  8.9 1.0 collective-permute-start.1
  9.9 2.3 %collective-permute-start.2 = (bf16[48,1024]{1,0:T(8,128)(2,1)S(1)}, bf16[48,1024]{1,0:T(8,128)(2,1)S(1)}, u32[]{:S(2)}, u32[]{:S(2)}) collective-permute-start(bf16[48,1024]{1,0:T(8,128)(2,1)S(1)} %get-tuple-element.39), channel_id=1, source_target_pairs={{12,0},{0,4},{4,8},{8,12},{13,1},{1,5},{5,9},{9,13},{14,2},{2,6},{... | collective-permute-start | bytes 294920 | tf_op jit(solution)/shard_map/ppermute | solution.py:429
  12.1 5.1 %own.1 = (bf16[512,512]{1,0:T(8,128)(2,1)S(1)}, bf16[512,512]{1,0:T(8,128)(2,1)S(1)}, bf16[512,512]{1,0:T(8,128)(2,1)S(1)}, bf16[512,512]{1,0:T(8,128)(2,1)S(1)}...) custom-call(bf16[48,1024]{1,0:T(8,128)(2,1)S(1)} %get-tuple-element., ...), custom_call_target="tpu_custom_call" | custom-call | tf_op jit(solution)/shard_map/own/pallas_call | solution.py:459
  17.3 0.0 collective-permute-done.p1
  17.3 0.2 collective-permute-done.1.p2
  17.5 0.7 collective-permute-done.2.p3
  18.2 18.6 %rest.1 = (bf16[512,1536]{1,0:T(8,128)(2,1)S(1)}, bf16[512,1536]{1,0:T(8,128)(2,1)S(1)}, bf16[512,1536]{1,0:T(8,128)(2,1)S(1)}, bf16[512,1536]{1,0:T(8,128)(2,1)...) custom-call(f32[8,128]{1,0:T(8,128)S(1)} %get-tuple-element.35.turns, ...), custom_call_target="tpu_custom_call" | custom-call | tf_op jit(solution)/shard_map/rest/pallas_call | solution.py:468
  36.7 13.9 %all_to_all.25.parts_ref = bf16[16,4,16,128]{3,2,1,0:T(8,128)(2,1)S(1)} all-to-all(bf16[16,4,16,128]{3,2,1,0:T(8,128)(2,1)S(1)} %bitcast.7), channel_id=1, replica_groups=mesh['grid'=16,'mic'=4,'bin'=4] {'grid'}, dimensions={0} | all-to-all | bytes 524288 | tf_op jit(solution)/shard_map/all_to_all | solution.py:477
  50.7 10.2 %all_to_all.26.q_ref = bf16[16,4,16,128]{3,2,1,0:T(8,128)(2,1)S(1)} all-to-all(bf16[16,4,16,128]{3,2,1,0:T(8,128)(2,1)S(1)} %get-tuple-element.51), channel_id=1, replica_groups=mesh['grid'=16,'mic'=4,'bin'=4] {'grid'}, dimensions={0} | all-to-all | bytes 524288 | tf_op jit(solution)/shard_map/all_to_all | solution.py:481
  60.9 7.8 %again.1 = (bf16[64,1024]{1,0:T(8,128)(2,1)S(1)}, bf16[8,2,4,16,128]{4,3,2,1,0:T(8,128)(2,1)S(1)}, f32[8,256]{1,0:T(8,128)S(1)}, f32[8,128]{1,0:T(8,128)S(1)}) custom-call(bf16[16,4,16,128]{3,2,1,0:T(8,128)(2,1)S(1)} %all_to_all.26.q_ref, f32[32,1024]{1,0:T(8,128)S(1)} %get-tuple-element.52.grad0_ref, bf16[512,512]{1,0:T(8,128)(2,1)S(1)} %get-tuple-element.42.refs_0_, ...), custom_call_target="tpu_custom_call" | custom-call | flops 8589934592 | tf_op jit(solution)/shard_map/again/pallas_call | solution.py:483
  68.7 10.2 %all_to_all.27.parts_ref = bf16[16,4,16,128]{3,2,1,0:T(8,128)(2,1)S(1)} all-to-all(bf16[16,4,16,128]{3,2,1,0:T(8,128)(2,1)S(1)} %bitcast.6), channel_id=1, replica_groups=mesh['grid'=16,'mic'=4,'bin'=4] {'grid'}, dimensions={0} | all-to-all | bytes 524288 | tf_op jit(solution)/shard_map/all_to_all | solution.py:493
  78.8 0.0 copy-start
  78.8 0.9 spread.1
  79.7 13.7 %all-to-all-start.3 = ((bf16[16,64,128]{2,1,0:T(8,128)(2,1)}), bf16[16,64,128]{2,1,0:T(8,128)(2,1)S(1)}, u32[]{:S(2)}, u32[]{:S(2)}) async-start(bf16[16,64,128]{2,1,0:T(8,128)(2,1)} %spread.1), calls=%async_computation.3 | async-start | bytes 524288 | tf_op jit(solution)/shard_map/all_to_all | solution.py:497
  93.4 11.7 %all-to-all-done.3.recv_ref = bf16[16,64,128]{2,1,0:T(8,128)(2,1)S(1)} async-done(((bf16[16,64,128]{2,1,0:T(8,128)(2,1)}), bf16[16,64,128]{2,1,0:T(8,128)(2,1)S(1)}, u32[]{:S(2)}, u32[]{:S(2)}) %all-to-all-start.3) | async-done | bytes 262176 | tf_op jit(solution)/shard_map/all_to_all | solution.py:497
  105.1 1.1 relay.1
  106.2 3.6 %all-to-all-start.4 = ((bf16[16,208,128]{2,1,0:T(8,128)(2,1)}), bf16[16,208,128]{2,1,0:T(8,128)(2,1)S(1)}, u32[]{:S(2)}, u32[]{:S(2)}) async-start(bf16[16,208,128]{2,1,0:T(8,128)(2,1)} %get-tuple-element.65), calls=%async_computation.4 | async-start | bytes 1703936 | tf_op jit(solution)/shard_map/all_to_all | solution.py:499
  109.8 0.4 collective-permute-start.5
  110.2 2.2 %collective-permute-start.4 = (bf16[64,1024]{1,0:T(8,128)(2,1)S(1)}, bf16[64,1024]{1,0:T(8,128)(2,1)S(1)}, u32[]{:S(2)}, u32[]{:S(2)}) collective-permute-start(bf16[64,1024]{1,0:T(8,128)(2,1)S(1)} %get-tuple-element.67.refs_0_), channel_id=1, source_target_pairs={{8,0},{12,4},{0,8},{4,12},{9,1},{13,5},{1,9},{5,13},{10,2},{14,6},... | collective-permute-start | bytes 393224 | tf_op jit(solution)/shard_map/ppermute | solution.py:429
  112.5 1.9 %collective-permute-start.3 = (bf16[64,1024]{1,0:T(8,128)(2,1)S(1)}, bf16[64,1024]{1,0:T(8,128)(2,1)S(1)}, u32[]{:S(2)}, u32[]{:S(2)}) collective-permute-start(bf16[64,1024]{1,0:T(8,128)(2,1)S(1)} %get-tuple-element.67.refs_0_), channel_id=1, source_target_pairs={{4,0},{8,4},{12,8},{0,12},{5,1},{9,5},{13,9},{1,13},{6,2},{10,6},{... | collective-permute-start | bytes 393224 | tf_op jit(solution)/shard_map/ppermute | solution.py:429
  114.4 5.2 %collective-permute-done.5.refs_3_ = bf16[64,1024]{1,0:T(8,128)(2,1)S(1)} collective-permute-done((bf16[64,1024]{1,0:T(8,128)(2,1)S(1)}, bf16[64,1024]{1,0:T(8,128)(2,1)S(1)}, u32[]{:S(2)}, u32[]{:S(2)}) %collective-permute-start.5) | collective-permute-done | bytes 131104 | tf_op jit(solution)/shard_map/ppermute | solution.py:429
  119.6 2.7 %collective-permute-done.4.refs_2_ = bf16[64,1024]{1,0:T(8,128)(2,1)S(1)} collective-permute-done((bf16[64,1024]{1,0:T(8,128)(2,1)S(1)}, bf16[64,1024]{1,0:T(8,128)(2,1)S(1)}, u32[]{:S(2)}, u32[]{:S(2)}) %collective-permute-start.4) | collective-permute-done | bytes 131104 | tf_op jit(solution)/shard_map/ppermute | solution.py:429
  122.2 5.0 %collective-permute-done.3.refs_1_ = bf16[64,1024]{1,0:T(8,128)(2,1)S(1)} collective-permute-done((bf16[64,1024]{1,0:T(8,128)(2,1)S(1)}, bf16[64,1024]{1,0:T(8,128)(2,1)S(1)}, u32[]{:S(2)}, u32[]{:S(2)}) %collective-permute-start.3) | collective-permute-done | bytes 131104 | tf_op jit(solution)/shard_map/ppermute | solution.py:429
  127.2 0.0 all-to-all-done.4.recv_ref
  127.3 0.0 copy-done
  127.3 1.3 last.1
  (1 shorter events, 0.0 us)
Async XLA Ops:
  2.0 15.3 %collective-permute-start = (bf16[48,1024]{1,0:T(8,128)(2,1)S(1)}, bf16[48,1024]{1,0:T(8,128)(2,1)S(1)}, u32[]{:S(2)}, u32[]{:S(2)}) collective-permute-start(bf16[48,1024]{1,0:T(8,128)(2,1)S(1)} %get-tuple-element.37), channel_id=1, source_target_pairs={{4,0},{8,4},{12,8},{0,12},{5,1},{9,5},{13,9},{1,13},{6,2},{10,6},{... | collective-permute-start | bytes 294920 | tf_op jit(solution)/shard_map/ppermute | solution.py:429
  8.9 8.6 %collective-permute-start.1 = (bf16[48,1024]{1,0:T(8,128)(2,1)S(1)}, bf16[48,1024]{1,0:T(8,128)(2,1)S(1)}, u32[]{:S(2)}, u32[]{:S(2)}) collective-permute-start(bf16[48,1024]{1,0:T(8,128)(2,1)S(1)} %get-tuple-element.38), channel_id=1, source_target_pairs={{8,0},{12,4},{0,8},{4,12},{9,1},{13,5},{1,9},{5,13},{10,2},{14,6},... | collective-permute-start | bytes 294920 | tf_op jit(solution)/shard_map/ppermute | solution.py:429
  9.9 8.3 %collective-permute-start.2 = (bf16[48,1024]{1,0:T(8,128)(2,1)S(1)}, bf16[48,1024]{1,0:T(8,128)(2,1)S(1)}, u32[]{:S(2)}, u32[]{:S(2)}) collective-permute-start(bf16[48,1024]{1,0:T(8,128)(2,1)S(1)} %get-tuple-element.39), channel_id=1, source_target_pairs={{12,0},{0,4},{4,8},{8,12},{13,1},{1,5},{5,9},{9,13},{14,2},{2,6},{... | collective-permute-start | bytes 294920 | tf_op jit(solution)/shard_map/ppermute | solution.py:429
  78.8 48.4 %copy-start = (f32[4,2,16,1024]{3,2,1,0:T(8,128)S(1)}, f32[4,2,16,1024]{3,2,1,0:T(8,128)}, u32[]{:S(2)}) copy-start(f32[4,2,16,1024]{3,2,1,0:T(8,128)} %press_hbm.1) | copy-start | bytes 1572868
  79.7 25.4 %all-to-all-start.3 = ((bf16[16,64,128]{2,1,0:T(8,128)(2,1)}), bf16[16,64,128]{2,1,0:T(8,128)(2,1)S(1)}, u32[]{:S(2)}, u32[]{:S(2)}) async-start(bf16[16,64,128]{2,1,0:T(8,128)(2,1)} %spread.1), calls=%async_computation.3 | async-start | bytes 524288 | tf_op jit(solution)/shard_map/all_to_all | solution.py:497
  106.2 21.1 %all-to-all-start.4 = ((bf16[16,208,128]{2,1,0:T(8,128)(2,1)}), bf16[16,208,128]{2,1,0:T(8,128)(2,1)S(1)}, u32[]{:S(2)}, u32[]{:S(2)}) async-start(bf16[16,208,128]{2,1,0:T(8,128)(2,1)} %get-tuple-element.65), calls=%async_computation.4 | async-start | bytes 1703936 | tf_op jit(solution)/shard_map/all_to_all | solution.py:499
  109.8 9.7 %collective-permute-start.5 = (bf16[64,1024]{1,0:T(8,128)(2,1)S(1)}, bf16[64,1024]{1,0:T(8,128)(2,1)S(1)}, u32[]{:S(2)}, u32[]{:S(2)}) collective-permute-start(bf16[64,1024]{1,0:T(8,128)(2,1)S(1)} %get-tuple-element.67.refs_0_), channel_id=1, source_target_pairs={{12,0},{0,4},{4,8},{8,12},{13,1},{1,5},{5,9},{9,13},{14,2},{2,6},{... | collective-permute-start | bytes 393224 | tf_op jit(solution)/shard_map/ppermute | solution.py:429
  110.2 12.0 %collective-permute-start.4 = (bf16[64,1024]{1,0:T(8,128)(2,1)S(1)}, bf16[64,1024]{1,0:T(8,128)(2,1)S(1)}, u32[]{:S(2)}, u32[]{:S(2)}) collective-permute-start(bf16[64,1024]{1,0:T(8,128)(2,1)S(1)} %get-tuple-element.67.refs_0_), channel_id=1, source_target_pairs={{8,0},{12,4},{0,8},{4,12},{9,1},{13,5},{1,9},{5,13},{10,2},{14,6},... | collective-permute-start | bytes 393224 | tf_op jit(solution)/shard_map/ppermute | solution.py:429
  112.5 14.8 %collective-permute-start.3 = (bf16[64,1024]{1,0:T(8,128)(2,1)S(1)}, bf16[64,1024]{1,0:T(8,128)(2,1)S(1)}, u32[]{:S(2)}, u32[]{:S(2)}) collective-permute-start(bf16[64,1024]{1,0:T(8,128)(2,1)S(1)} %get-tuple-element.67.refs_0_), channel_id=1, source_target_pairs={{4,0},{8,4},{12,8},{0,12},{5,1},{9,5},{13,9},{1,13},{6,2},{10,6},{... | collective-permute-start | bytes 393224 | tf_op jit(solution)/shard_map/ppermute | solution.py:429

commit v5 on v4

--- a/solution.py
+++ b/solution.py
@@ -100,8 +100,8 @@
     return high, middle, (left - middle).astype(BF16).astype(F32)
 
 
-def prepare_kernel(mic_ref, wave_hbm, press_hbm, coords_hbm, points_hbm, g_ref, turns_ref, p0, p1, p2, p3, *scratch):
-    wave_ref, press, coords, pad, sems = scratch
+def prepare_kernel(mic_ref, bin_ref, grid_ref, wave_hbm, press_hbm, coords_hbm, points_hbm, g_ref, turns_ref, p0, p1, p2, p3, press, *scratch):
+    wave_ref, coords, pad, sems = scratch
     copies = [
         pltpu.make_async_copy(press_hbm, press, sems.at[0]),
         pltpu.make_async_copy(coords_hbm, coords, sems.at[1]),
@@ -326,59 +326,61 @@
     return tile[0:6] + jnp.concatenate([tile[6:12, 0:64], jnp.zeros((6, 64), F32)], axis=1), tile[12:16]
 
 
-def spread_kernel(mic_ref, parts_ref, q_ref, sums_ref, along_ref, out_ref, shard):
+def spread_kernel(mic_ref, grid_ref, parts_ref, q_ref, sums_ref, along_ref, p0, p1, p2, p3, out_ref, off_press, off_image):
     total = total_of(parts_ref)
     q = q_ref[...]
+    rows = pl.ds(pl.multiple_of(lax.rem(grid_ref[0], 2) * 16, 16), 16)
+    cols = pl.ds(pl.multiple_of(lax.div(grid_ref[0], 2) * 128, 128), 128)
+    press = jnp.stack([pack[rows, cols] for pack in (p0, p1, p2, p3)]).astype(F32)
 
     def flat(x):
         return lane_sums(x.reshape(64, 128))
+
+    def part_along(aa, ab):
+        return coefficient(jnp.sum(aa, axis=1, keepdims=True), jnp.sum(ab, axis=1, keepdims=True))
 
     near = sums_ref[0:3, 0:128] + sums_ref[0:3, 128:256]
     qq, qp = flat(q * q), flat(q * total)
     sums = jnp.concatenate([near, qq, qp, flat(total * total)], axis=0)
-    along = coefficient(jnp.sum(qq, axis=1, keepdims=True), jnp.sum(qp, axis=1, keepdims=True))
-    shard[...] = total - along * q
-    rest = jnp.concatenate([jnp.broadcast_to(along, (1, 128)), along_ref[0:1], jnp.zeros((2, 128), F32)], axis=0)
-    tile = pack_sums(sums, rest)
+    on_press = part_along(flat(press * press), flat(press * q))
+    on_image = part_along(qq, qp)
+    off_press[...] = q - on_press * press
+    off_image[...] = total - on_image * q
+    both = jnp.concatenate([jnp.broadcast_to(on_image, (1, 64)), jnp.broadcast_to(on_press, (1, 64))], axis=1)
+    tile = pack_sums(sums, jnp.concatenate([both, along_ref[0:1], jnp.zeros((2, 128), F32)], axis=0))
     for t in range(4):
         s = lax.rem(t + 4 - mic_ref[0], 4)
-        a = q_ref[s]
-        high = a.astype(BF16)
-        middle = (a - high.astype(F32)).astype(BF16)
-        off = shard[s].astype(BF16)
+        first, second = off_press[s].astype(BF16), off_image[s].astype(BF16)
         for k in range(4):
-            out_ref[t * 4 + k, 0:16] = high
-            out_ref[t * 4 + k, 16:32] = middle
-            out_ref[t * 4 + k, 32:48] = off
-            out_ref[t * 4 + k, 48:64] = tile
+            out_ref[t * 4 + k, 0:16] = first
+            out_ref[t * 4 + k, 16:32] = second
+            out_ref[t * 4 + k, 32:48] = tile
 
 
 def relay_kernel(bin_ref, recv_ref, out_ref, along_ref):
-    sums = unpack_sums(recv_ref[0, 48:64])[0]
+    sums = unpack_sums(recv_ref[0, 32:48])[0]
     for j in range(1, 16):
-        sums += unpack_sums(recv_ref[j, 48:64])[0]
+        sums += unpack_sums(recv_ref[j, 32:48])[0]
     rest = []
     for m in range(4):
         slot = m * 4 + bin_ref[0]
-        piece = recv_ref[slot, 0:48]
+        piece = recv_ref[slot, 0:32]
         for j in range(16):
-            out_ref[j, m * 48 : m * 48 + 48] = piece
-        values = recv_ref[slot, 48:64].astype(F32)
+            out_ref[j, m * 32 : m * 32 + 32] = piece
+        values = recv_ref[slot, 32:48].astype(F32)
         rest.append(values[12:13])
         along_ref[m : m + 1] = values[13:14]
     along_ref[4:8] = jnp.zeros((4, 128), F32)
     tile = pack_sums(sums, jnp.concatenate(rest, axis=0))
     for j in range(16):
-        out_ref[j, 192:208] = tile
-
-
-def last_kernel(mic_ref, recv_ref, along_ref, press_hbm, *refs):
-    packs, (x_ref, r_ref, press_ref, sem) = refs[:4], refs[4:]
-    copy = pltpu.make_async_copy(press_hbm, press_ref, sem)
-    copy.start()
-    total = unpack_sums(recv_ref[0, 192:208])[0]
+        out_ref[j, 128:144] = tile
+
+
+def last_kernel(mic_ref, recv_ref, along_ref, press_ref, *refs):
+    packs, (x_ref, r_ref) = refs[:4], refs[4:]
+    total = unpack_sums(recv_ref[0, 128:144])[0]
     for j in range(1, 16):
-        total += unpack_sums(recv_ref[j, 192:208])[0]
+        total += unpack_sums(recv_ref[j, 128:144])[0]
     total = jnp.sum(total, axis=1, keepdims=True)
     gg, gh, hh, qq, qp, pp = [total[i : i + 1] for i in range(6)]
     step0 = gg / qq
@@ -397,15 +399,16 @@
                 g = pack[h * 16 : h * 16 + 16, cols].astype(F32)
                 y = pack[32 + h * 16 : 48 + h * 16, cols].astype(F32)
                 x_ref[bin_at, h, :, cols] = first * g - tail * y
-    copy.wait()
     for h in range(2):
         for c in range(8):
             j, cols = 2 * c + h, slice(c * 128, c * 128 + 128)
-            rest = unpack_sums(recv_ref[j, 192:208])[1]
+            rest = unpack_sums(recv_ref[j, 128:144])[1]
             for m in range(4):
-                q = recv_ref[j, m * 48 : m * 48 + 16].astype(F32) + recv_ref[j, m * 48 + 16 : m * 48 + 32].astype(F32)
-                off = recv_ref[j, m * 48 + 32 : m * 48 + 48].astype(F32)
-                r_ref[m, h, :, cols] = press_ref[m, h, :, cols] - (lead - tail * rest[m : m + 1]) * q + tail * off
+                press = press_ref[m, h * 16 : h * 16 + 16, cols]
+                q = recv_ref[j, m * 32 : m * 32 + 16].astype(F32)
+                q += rest[m : m + 1, 64:65] * press.astype(BF16).astype(F32)
+                off = recv_ref[j, m * 32 + 16 : m * 32 + 32].astype(F32)
+                r_ref[m, h, :, cols] = press - (lead - tail * rest[m : m + 1, 0:1]) * q + tail * off
 
 
 def call(kernel, name, in_specs, out_shape, scratch=(), limit=4, work=0):
@@ -431,23 +434,23 @@
 
 def body(grid_points, mic_coords, wavenumbers, pressures):
     scale = 1.0 / math.sqrt(grid_points.shape[1] * lax.axis_size("grid"))
-    mic, bin_at = [jnp.reshape(lax.axis_index(name), (1,)).astype(jnp.int32) for name in ("mic", "bin")]
+    mic, bin_at, grid_at = [jnp.reshape(lax.axis_index(name), (1,)).astype(jnp.int32) for name in ("mic", "bin", "grid")]
     flat = pressures.reshape(4, 32, 1024)
 
-    points, turns, *packs = call(
+    points, turns, *packs, press = call(
         prepare_kernel,
         "prepare",
-        [SM, HBM, HBM, HBM, HBM],
-        [pltpu.VMEM((1024, 8), F32), pltpu.VMEM((8, 128), F32)] + [pltpu.VMEM((48, 1024), BF16)] * 4,
+        [SM, SM, SM, HBM, HBM, HBM, HBM],
+        [pltpu.VMEM((1024, 8), F32), pltpu.VMEM((8, 128), F32)] + [pltpu.VMEM((48, 1024), BF16)] * 4
+        + [pltpu.VMEM((4, 32, 1024), F32)],
         [
             pltpu.SMEM((4,), F32),
-            pltpu.VMEM((4, 32, 1024), F32),
             pltpu.VMEM((3, 1024), F32),
             pltpu.VMEM((8, 1024), F32),
             pltpu.SemaphoreType.DMA((4,)),
         ],
         limit=60,
-    )(mic, wavenumbers, flat, mic_coords, grid_points)
+    )(mic, bin_at, grid_at, wavenumbers, flat, mic_coords, grid_points)
     packs[1:] = [ahead(pack, s) for s, pack in zip((1, 2, 3), packs[1:])]
 
     def held(width):
@@ -489,22 +492,26 @@
         work=8 << 30,
     )(rounded, grad0, *near, *far)
 
-    hops = [packed] + [ahead(packed, s) for s in (1, 2, 3)]
+    near_hop = ahead(packed, 1)
+    hops = [packed, near_hop, ahead(near_hop, 1), ahead(packed, 3)]
     parts = lax.all_to_all(part1.reshape(16, 4, 16, 128), "grid", 0, 0)
     sent = call(
-        spread_kernel, "spread", [SM] + [VM] * 4, array(16, 64, 128, dtype=BF16), [pltpu.VMEM((4, 16, 128), F32)]
-    )(mic, parts, image0, sums, along)
+        spread_kernel,
+        "spread",
+        [SM, SM] + [VM] * 8,
+        array(16, 48, 128, dtype=BF16),
+        [pltpu.VMEM((4, 16, 128), F32)] * 2,
+    )(mic, grid_at, parts, image0, sums, along, *packs)
     recv = lax.all_to_all(sent, ("mic", "bin"), 0, 0)
-    sent, alongs = call(relay_kernel, "relay", [SM, VM], [array(16, 208, 128, dtype=BF16), array(8, 128)])(bin_at, recv)
+    sent, alongs = call(relay_kernel, "relay", [SM, VM], [array(16, 144, 128, dtype=BF16), array(8, 128)])(bin_at, recv)
     recv = lax.all_to_all(sent, "grid", 0, 0)
     out_type = array(4, 2, 16, 1024)
     return call(
         last_kernel,
         "last",
-        [SM, VM, VM, HBM] + [VM] * 4,
+        [SM] + [VM] * 7,
         [out_type, out_type],
-        [pltpu.VMEM((4, 2, 16, 1024), F32), pltpu.SemaphoreType.DMA],
-    )(mic, recv, alongs, pressures, *hops)
+    )(mic, recv, alongs, press, *hops)
 
 
 def solution(mesh):

time: 129 us -> 125 us (0.969)
  blocking collectives: 34.3 us -> 58 us
  starting transfers between devices: 32 us -> 18.2 us
  waiting for transfers between devices: 25.4 us -> 12.7 us
    all_to_all x0 -> x1, blocking collectives: none -> 23.8 us  [body(): recv = lax.all_to_all(sent, ('mic', 'bin'), 0, 0)]
    all_to_all x1 -> x0, starting transfers between devices: 13.7 us -> none  [body(): recv = lax.all_to_all(sent, ('mic', 'bin'), 0, 0)]
    all_to_all x1 -> x0, waiting for transfers between devices: 11.7 us -> none  [body(): recv = lax.all_to_all(sent, ('mic', 'bin'), 0, 0)]
  transfers between devices with their start and end apart: 8 -> 7, of which waited for: 6 -> 4; matrix products, arithmetic and copies ran while one was open for 0% -> 0% of each run, Pallas kernels for 4% -> 4%
where the time goes in v5:
time: 125 us
  blocking collectives  58 us (46%)
  Pallas kernels  35.4 us (28%)
  starting transfers between devices  18.2 us (15%)
  waiting for transfers between devices  12.7 us (10%)
    all_to_all x1, blocking collectives, body(): recv = lax.all_to_all(sent, ('mic', 'bin'), 0, 0)  23.8 us
    pallas_call x1, Pallas kernels, body(): call(functools.partial(rest_kernel, scale), 'rest', [VM] * 14, held(1536)...  18.6 us
    ppermute x6, starting transfers between devices, ahead(): return lax.ppermute(x, 'mic', [((t + shift) % 4, t) for t in range(4)])  14.6 us
    all_to_all x1, blocking collectives, body(): parts = lax.all_to_all(part0.reshape(16, 4, 16, 128), 'grid', 0, 0)  13.9 us
    ppermute x6, waiting for transfers between devices, ahead(): return lax.ppermute(x, 'mic', [((t + shift) % 4, t) for t in range(4)])  12.7 us
    all_to_all x1, blocking collectives, body(): rounded = lax.all_to_all(copies, 'grid', 0, 0)  10.2 us
    all_to_all x1, blocking collectives, body(): parts = lax.all_to_all(part1.reshape(16, 4, 16, 128), 'grid', 0, 0)  10.2 us
    pallas_call x1, Pallas kernels, body(): call(functools.partial(again_kernel, scale), 'again', [VM] * 18, [array(6...  7.8 us
  transfers between devices with their start and end apart: 7, of which 4 were waited for; matrix products, arithmetic and copies ran while one was open for 0% of the time, Pallas kernels for 4%

profile of v5, /device:TPU:1, one launch (start us, length us, event | category | flops | bytes accessed | tf_op | source)
XLA Modules:
  0.0 125.0 jit_solution(2290960870807841894)
XLA Ops:
  0.6 1.3 %prepare.1 = (f32[1024,8]{1,0:T(8,128)S(1)}, f32[8,128]{1,0:T(8,128)S(1)}, bf16[48,1024]{1,0:T(8,128)(2,1)S(1)}, bf16[48,1024]{1,0:T(8,128)(2,1)S(1)}, bf16[48,1...) custom-call(s32[1]{0:T(128)} %bitcast.mic_ref, s32[1]{0:T(128)} %bitcast.1.bin_ref, ...), custom_call_target="tpu_custom_call" | custom-call | tf_op jit(solution)/shard_map/prepare/pallas_call | solution.py:440
  2.0 6.9 %collective-permute-start = (bf16[48,1024]{1,0:T(8,128)(2,1)S(1)}, bf16[48,1024]{1,0:T(8,128)(2,1)S(1)}, u32[]{:S(2)}, u32[]{:S(2)}) collective-permute-start(bf16[48,1024]{1,0:T(8,128)(2,1)S(1)} %get-tuple-element.38), channel_id=1, source_target_pairs={{4,0},{8,4},{12,8},{0,12},{5,1},{9,5},{13,9},{1,13},{6,2},{10,6},{... | collective-permute-start | bytes 294920 | tf_op jit(solution)/shard_map/ppermute | solution.py:432
  8.9 1.0 collective-permute-start.1
  9.9 2.3 %collective-permute-start.2 = (bf16[48,1024]{1,0:T(8,128)(2,1)S(1)}, bf16[48,1024]{1,0:T(8,128)(2,1)S(1)}, u32[]{:S(2)}, u32[]{:S(2)}) collective-permute-start(bf16[48,1024]{1,0:T(8,128)(2,1)S(1)} %get-tuple-element.40), channel_id=1, source_target_pairs={{12,0},{0,4},{4,8},{8,12},{13,1},{1,5},{5,9},{9,13},{14,2},{2,6},{... | collective-permute-start | bytes 294920 | tf_op jit(solution)/shard_map/ppermute | solution.py:432
  12.1 5.1 %own.1 = (bf16[512,512]{1,0:T(8,128)(2,1)S(1)}, bf16[512,512]{1,0:T(8,128)(2,1)S(1)}, bf16[512,512]{1,0:T(8,128)(2,1)S(1)}, bf16[512,512]{1,0:T(8,128)(2,1)S(1)}...) custom-call(bf16[48,1024]{1,0:T(8,128)(2,1)S(1)} %get-tuple-element., ...), custom_call_target="tpu_custom_call" | custom-call | tf_op jit(solution)/shard_map/own/pallas_call | solution.py:462
  17.3 0.0 collective-permute-done.p1
  17.3 0.2 collective-permute-done.1.p2
  17.5 0.7 collective-permute-done.2.p3
  18.2 18.6 %rest.1 = (bf16[512,1536]{1,0:T(8,128)(2,1)S(1)}, bf16[512,1536]{1,0:T(8,128)(2,1)S(1)}, bf16[512,1536]{1,0:T(8,128)(2,1)S(1)}, bf16[512,1536]{1,0:T(8,128)(2,1)...) custom-call(f32[8,128]{1,0:T(8,128)S(1)} %get-tuple-element.36.turns, ...), custom_call_target="tpu_custom_call" | custom-call | tf_op jit(solution)/shard_map/rest/pallas_call | solution.py:471
  36.7 13.9 %all_to_all.25.parts_ref = bf16[16,4,16,128]{3,2,1,0:T(8,128)(2,1)S(1)} all-to-all(bf16[16,4,16,128]{3,2,1,0:T(8,128)(2,1)S(1)} %bitcast.7), channel_id=1, replica_groups=mesh['grid'=16,'mic'=4,'bin'=4] {'grid'}, dimensions={0} | all-to-all | bytes 524288 | tf_op jit(solution)/shard_map/all_to_all | solution.py:480
  50.7 10.2 %all_to_all.26.q_ref = bf16[16,4,16,128]{3,2,1,0:T(8,128)(2,1)S(1)} all-to-all(bf16[16,4,16,128]{3,2,1,0:T(8,128)(2,1)S(1)} %get-tuple-element.52), channel_id=1, replica_groups=mesh['grid'=16,'mic'=4,'bin'=4] {'grid'}, dimensions={0} | all-to-all | bytes 524288 | tf_op jit(solution)/shard_map/all_to_all | solution.py:484
  60.9 7.8 %again.1 = (bf16[64,1024]{1,0:T(8,128)(2,1)S(1)}, bf16[8,2,4,16,128]{4,3,2,1,0:T(8,128)(2,1)S(1)}, f32[8,256]{1,0:T(8,128)S(1)}, f32[8,128]{1,0:T(8,128)S(1)}) custom-call(bf16[16,4,16,128]{3,2,1,0:T(8,128)(2,1)S(1)} %all_to_all.26.q_ref, f32[32,1024]{1,0:T(8,128)S(1)} %get-tuple-element.53.grad0_ref, bf16[512,512]{1,0:T(8,128)(2,1)S(1)} %get-tuple-element.43.refs_0_, ...), custom_call_target="tpu_custom_call" | custom-call | flops 8589934592 | tf_op jit(solution)/shard_map/again/pallas_call | solution.py:486
  68.7 10.2 %all_to_all.27.parts_ref = bf16[16,4,16,128]{3,2,1,0:T(8,128)(2,1)S(1)} all-to-all(bf16[16,4,16,128]{3,2,1,0:T(8,128)(2,1)S(1)} %bitcast.6), channel_id=1, replica_groups=mesh['grid'=16,'mic'=4,'bin'=4] {'grid'}, dimensions={0} | all-to-all | bytes 524288 | tf_op jit(solution)/shard_map/all_to_all | solution.py:497
  78.8 0.2 spread.1
  79.0 23.8 %all_to_all.28.recv_ref = bf16[16,48,128]{2,1,0:T(8,128)(2,1)S(1)} all-to-all(bf16[16,48,128]{2,1,0:T(8,128)(2,1)S(1)} %spread.1), channel_id=1, replica_groups=mesh['grid'=16,'mic'=4,'bin'=4] {'mic','bin'}, dimensions={0} | all-to-all | bytes 393216 | tf_op jit(solution)/shard_map/all_to_all | solution.py:505
  102.8 1.0 relay.1
  103.8 3.6 %all-to-all-start.4 = ((bf16[16,144,128]{2,1,0:T(8,128)(2,1)}), bf16[16,144,128]{2,1,0:T(8,128)(2,1)S(1)}, u32[]{:S(2)}, u32[]{:S(2)}) async-start(bf16[16,144,128]{2,1,0:T(8,128)(2,1)} %get-tuple-element.66), calls=%async_computation.4 | async-start | bytes 1179648 | tf_op jit(solution)/shard_map/all_to_all | solution.py:507
  107.4 0.6 collective-permute-start.3
  108.0 1.9 %collective-permute-start.5 = (bf16[64,1024]{1,0:T(8,128)(2,1)S(1)}, bf16[64,1024]{1,0:T(8,128)(2,1)S(1)}, u32[]{:S(2)}, u32[]{:S(2)}) collective-permute-start(bf16[64,1024]{1,0:T(8,128)(2,1)S(1)} %get-tuple-element.69.refs_0_), channel_id=1, source_target_pairs={{12,0},{0,4},{4,8},{8,12},{13,1},{1,5},{5,9},{9,13},{14,2},{2,6},{... | collective-permute-start | bytes 393224 | tf_op jit(solution)/shard_map/ppermute | solution.py:432
  109.8 6.4 %collective-permute-done.3.refs_1_ = bf16[64,1024]{1,0:T(8,128)(2,1)S(1)} collective-permute-done((bf16[64,1024]{1,0:T(8,128)(2,1)S(1)}, bf16[64,1024]{1,0:T(8,128)(2,1)S(1)}, u32[]{:S(2)}, u32[]{:S(2)}) %collective-permute-start.3) | collective-permute-done | bytes 131104 | tf_op jit(solution)/shard_map/ppermute | solution.py:432
  116.3 2.0 %collective-permute-start.4 = (bf16[64,1024]{1,0:T(8,128)(2,1)S(1)}, bf16[64,1024]{1,0:T(8,128)(2,1)S(1)}, u32[]{:S(2)}, u32[]{:S(2)}) collective-permute-start(bf16[64,1024]{1,0:T(8,128)(2,1)S(1)} %collective-permute-done.3.refs_1_), channel_id=1, source_target_pairs={{4,0},{8,4},{12,8},{0,12},{5,1},{9,5},{13,9},{1,13},{6,2},{10,6},{... | collective-permute-start | bytes 393224 | tf_op jit(solution)/shard_map/ppermute | solution.py:432
  118.2 0.0 collective-permute-done.5.refs_3_
  118.2 5.4 %collective-permute-done.4.refs_2_ = bf16[64,1024]{1,0:T(8,128)(2,1)S(1)} collective-permute-done((bf16[64,1024]{1,0:T(8,128)(2,1)S(1)}, bf16[64,1024]{1,0:T(8,128)(2,1)S(1)}, u32[]{:S(2)}, u32[]{:S(2)}) %collective-permute-start.4) | collective-permute-done | bytes 131104 | tf_op jit(solution)/shard_map/ppermute | solution.py:432
  123.6 0.0 all-to-all-done.4.recv_ref
  123.6 1.3 %last.1 = (f32[4,2,16,1024]{3,2,1,0:T(8,128)}, f32[4,2,16,1024]{3,2,1,0:T(8,128)}) custom-call(s32[1]{0:T(128)} %bitcast.mic_ref, bf16[16,144,128]{2,1,0:T(8,128)(2,1)S(1)} %all-to-all-done.4.recv_ref, f32[8,128]{1,0:T(8,128)S(1)} %get-tuple-element.67.along_ref, f32[4,32,1024]{2,1,0:T(8,128)S(1)} %get-tuple-element.68.press_ref, ...), custom_call_target="tpu_custom_call" | custom-call | tf_op jit(solution)/shard_map/last/pallas_call | solution.py:509
  (1 shorter events, 0.0 us)
Async XLA Ops:
  2.0 15.3 %collective-permute-start = (bf16[48,1024]{1,0:T(8,128)(2,1)S(1)}, bf16[48,1024]{1,0:T(8,128)(2,1)S(1)}, u32[]{:S(2)}, u32[]{:S(2)}) collective-permute-start(bf16[48,1024]{1,0:T(8,128)(2,1)S(1)} %get-tuple-element.38), channel_id=1, source_target_pairs={{4,0},{8,4},{12,8},{0,12},{5,1},{9,5},{13,9},{1,13},{6,2},{10,6},{... | collective-permute-start | bytes 294920 | tf_op jit(solution)/shard_map/ppermute | solution.py:432
  8.9 8.6 %collective-permute-start.1 = (bf16[48,1024]{1,0:T(8,128)(2,1)S(1)}, bf16[48,1024]{1,0:T(8,128)(2,1)S(1)}, u32[]{:S(2)}, u32[]{:S(2)}) collective-permute-start(bf16[48,1024]{1,0:T(8,128)(2,1)S(1)} %get-tuple-element.39), channel_id=1, source_target_pairs={{8,0},{12,4},{0,8},{4,12},{9,1},{13,5},{1,9},{5,13},{10,2},{14,6},... | collective-permute-start | bytes 294920 | tf_op jit(solution)/shard_map/ppermute | solution.py:432
  9.9 8.3 %collective-permute-start.2 = (bf16[48,1024]{1,0:T(8,128)(2,1)S(1)}, bf16[48,1024]{1,0:T(8,128)(2,1)S(1)}, u32[]{:S(2)}, u32[]{:S(2)}) collective-permute-start(bf16[48,1024]{1,0:T(8,128)(2,1)S(1)} %get-tuple-element.40), channel_id=1, source_target_pairs={{12,0},{0,4},{4,8},{8,12},{13,1},{1,5},{5,9},{9,13},{14,2},{2,6},{... | collective-permute-start | bytes 294920 | tf_op jit(solution)/shard_map/ppermute | solution.py:432
  103.8 19.9 %all-to-all-start.4 = ((bf16[16,144,128]{2,1,0:T(8,128)(2,1)}), bf16[16,144,128]{2,1,0:T(8,128)(2,1)S(1)}, u32[]{:S(2)}, u32[]{:S(2)}) async-start(bf16[16,144,128]{2,1,0:T(8,128)(2,1)} %get-tuple-element.66), calls=%async_computation.4 | async-start | bytes 1179648 | tf_op jit(solution)/shard_map/all_to_all | solution.py:507
  107.4 8.9 %collective-permute-start.3 = (bf16[64,1024]{1,0:T(8,128)(2,1)S(1)}, bf16[64,1024]{1,0:T(8,128)(2,1)S(1)}, u32[]{:S(2)}, u32[]{:S(2)}) collective-permute-start(bf16[64,1024]{1,0:T(8,128)(2,1)S(1)} %get-tuple-element.69.refs_0_), channel_id=1, source_target_pairs={{4,0},{8,4},{12,8},{0,12},{5,1},{9,5},{13,9},{1,13},{6,2},{10,6},{... | collective-permute-start | bytes 393224 | tf_op jit(solution)/shard_map/ppermute | solution.py:432
  108.0 10.3 %collective-permute-start.5 = (bf16[64,1024]{1,0:T(8,128)(2,1)S(1)}, bf16[64,1024]{1,0:T(8,128)(2,1)S(1)}, u32[]{:S(2)}, u32[]{:S(2)}) collective-permute-start(bf16[64,1024]{1,0:T(8,128)(2,1)S(1)} %get-tuple-element.69.refs_0_), channel_id=1, source_target_pairs={{12,0},{0,4},{4,8},{8,12},{13,1},{1,5},{5,9},{9,13},{14,2},{2,6},{... | collective-permute-start | bytes 393224 | tf_op jit(solution)/shard_map/ppermute | solution.py:432
  116.3 7.4 %collective-permute-start.4 = (bf16[64,1024]{1,0:T(8,128)(2,1)S(1)}, bf16[64,1024]{1,0:T(8,128)(2,1)S(1)}, u32[]{:S(2)}, u32[]{:S(2)}) collective-permute-start(bf16[64,1024]{1,0:T(8,128)(2,1)S(1)} %collective-permute-done.3.refs_1_), channel_id=1, source_target_pairs={{4,0},{8,4},{12,8},{0,12},{5,1},{9,5},{13,9},{1,13},{6,2},{10,6},{... | collective-permute-start | bytes 393224 | tf_op jit(solution)/shard_map/ppermute | solution.py:432

commit v6 on v5

--- a/solution.py
+++ b/solution.py
@@ -137,22 +137,26 @@
     ws[odd, 16:32, cols] = real
 
 
-def own_kernel(scale, pack, turns_ref, grid_ref, *refs):
-    tiles, grad_ref, wc, ws, coords = Tiles(refs[:8]), refs[8], refs[9], refs[10], refs[11]
+def head_kernel(scale, count, turns_ref, grid_ref, *refs):
+    packs, refs = refs[:count], refs[count:]
+    if count > 1:
+        before, refs = refs[0], refs[1:]
+    tiles, (grad_ref, wc, ws, coords) = Tiles(refs[:8]), refs[8:]
     turns = turns_ref[0:1, 0:1]
-    for chunk in range(4):
-        w = pack[0:32, chunk * EDGE : chunk * EDGE + EDGE]
-        set_weights(wc, ws, chunk, w[0:16], w[16:32], scale)
-    coords[0:3] = whole_coords(pack)
+    for s, pack in enumerate(packs):
+        for chunk in range(4):
+            w = pack[0:32, chunk * EDGE : chunk * EDGE + EDGE]
+            set_weights(wc, ws, s * 4 + chunk, w[0:16], w[16:32], scale)
+        coords[0:3, s * 1024 : s * 1024 + 1024] = whole_coords(pack)
 
     def mics(chunk):
         return [coords[d : d + 1, chunk * EDGE : chunk * EDGE + EDGE] for d in range(3)]
 
     def half_step(half, carry):
-        late = None
+        late = done = None
         for odd in range(2):
-            total = jnp.zeros((32, EDGE), F32)
-            for pair in range(2):
+            total = jnp.zeros((32, EDGE), F32) if count == 1 else before[:, span(half * 2 + odd)]
+            for pair in range(2 * count):
                 for chunk_odd in range(2):
                     if late is not None:
                         value = tiles.adjoint((wc, ws), half, *late)
@@ -169,101 +173,83 @@
     lax.fori_loop(0, 2, half_step, 0)
 
 
-def store_image(out_ref, image, first):
+def store_image(out_ref, image, blocks):
     for odd in range(2):
         for pair in range(image.shape[2] // EDGE):
             for piece in range(2):
                 tile = (pair * 2 + odd) * 2 + piece
-                s, c = tile // 8 + first, tile % 8
+                s, c = blocks[tile // 8], tile % 8
                 lo = pair * EDGE + piece * 128
                 for h in range(2):
                     out_ref[c, h, s] = image[odd, h * 16 : h * 16 + 16, lo : lo + 128].astype(BF16)
 
 
-def rest_kernel(scale, turns_ref, grid_ref, p1, p2, p3, head_ref, *refs):
-    own, tiles = Tiles(refs[:8]), Tiles(refs[8:16])
-    grad_ref, image_ref, wc, ws, near, far, coords = refs[16:]
+BLOCKS = ((0,), (1, 3), (2,))
+
+
+def rest_kernel(scale, turns_ref, grid_ref, pack, before, *refs):
+    near, middle, tiles = Tiles(refs[:8]), Tiles(refs[8:16]), Tiles(refs[16:24])
+    grad_ref, image_ref, wc, ws, coords = refs[24:29]
+    images = refs[29:]
     turns = turns_ref[0:1, 0:1]
-    for s, pack in enumerate((p1, p2, p3)):
-        for chunk in range(4):
-            w = pack[0:32, chunk * EDGE : chunk * EDGE + EDGE]
-            set_weights(wc, ws, s * 4 + chunk, w[0:16], w[16:32], scale)
-        coords[0:3, s * 1024 : s * 1024 + 1024] = whole_coords(pack)
-    near[...] = jnp.zeros_like(near)
-    far[...] = jnp.zeros_like(far)
-
-    def mics(pair, chunk_odd):
-        lo = pl.ds(multiple((pair * 2 + chunk_odd) * EDGE, EDGE), EDGE)
-        return [coords[d : d + 1, lo] for d in range(3)]
-
-    def one_step(half, odd, v, before):
-        total = head_ref[:, span(half * 2 + odd)]
-
-        def pair_body(pair, total, first):
-            if not first:
-                total += tiles.adjoint((wc, ws), half, odd, pair - 1, 1)
-            if before is not None:
-                tiles.forward(far, *v, *before, pair, 0)
-                if first:
-                    for p in range(2):
-                        for o in range(2):
-                            own.forward(near, *v, *before, p, o)
-            tiles.build(grid_ref, mics(pair, 0), turns, half, odd, pair, 0)
-            total += tiles.adjoint((wc, ws), half, odd, pair, 0)
-            if before is not None:
-                tiles.forward(far, *v, *before, pair, 1)
-            tiles.build(grid_ref, mics(pair, 1), turns, half, odd, pair, 1)
-            return total
-
-        total = pair_body(0, total, True)
-        total = lax.fori_loop(1, 6, lambda pair, total: pair_body(pair, total, False), total)
-        total += tiles.adjoint((wc, ws), half, odd, 5, 1)
+    for chunk in range(4):
+        w = pack[0:32, chunk * EDGE : chunk * EDGE + EDGE]
+        set_weights(wc, ws, chunk, w[0:16], w[16:32], scale)
+    coords[0:3] = whole_coords(pack)
+    for image in images:
+        image[...] = jnp.zeros_like(image)
+    tasks = []
+    for group, image, blocks in zip((near, middle, tiles), images, BLOCKS):
+        tasks += [(group, image, pair, odd) for pair in range(2 * len(blocks)) for odd in range(2)]
+
+    def forward(some, v, half, odd):
+        for group, image, pair, chunk_odd in some:
+            group.forward(image, *v, half, odd, pair, chunk_odd)
+
+    v = last = None
+    for half, odd in ((0, 0), (0, 1), (1, 0), (1, 1)):
+        total = before[:, span(half * 2 + odd)]
+        for n in range(4):
+            if n:
+                total += tiles.adjoint((wc, ws), half, odd, *divmod(n - 1, 2))
+            if last is not None:
+                forward(tasks[4 * n : 4 * n + 4], v, *last)
+            cols = slice(n * EDGE, n * EDGE + EDGE)
+            tiles.build(grid_ref, [coords[d : d + 1, cols] for d in range(3)], turns, half, odd, *divmod(n, 2))
+        total += tiles.adjoint((wc, ws), half, odd, 1, 1)
         grad_ref[:, span(half * 2 + odd)] = total
         v = total.astype(BF16) * scale
-        return v, swapped(v)
-
-    v = one_step(0, 0, None, None)
-    v = one_step(0, 1, v, (0, 0))
-    v = one_step(1, 0, v, (0, 1))
-    v = one_step(1, 1, v, (1, 0))
-    for p in range(2):
-        for o in range(2):
-            own.forward(near, *v, 1, 1, p, o)
-
-    def tail(pair, carry):
-        tiles.forward(far, *v, 1, 1, pair, 0)
-        tiles.forward(far, *v, 1, 1, pair, 1)
-        return carry
-
-    lax.fori_loop(0, 6, tail, 0)
-    store_image(image_ref, near, 0)
-    store_image(image_ref, far, 1)
+        v, last = (v, swapped(v)), (half, odd)
+    forward(tasks, v, *last)
+    for image, blocks in zip(images, BLOCKS):
+        store_image(image_ref, image, blocks)
 
 
 def again_kernel(scale, q_ref, grad0_ref, *refs):
-    own, tiles = Tiles(refs[:8]), Tiles(refs[8:16])
-    packed_ref, image_ref, sums_ref, along_ref, wa, wb, wc, wd, near, far, grad_ref = refs[16:]
-    for block in range(4):
-        for chunk in range(4):
-            real = jnp.concatenate([q_ref[4 * chunk + 2 * p, block] for p in range(2)], axis=1)
-            imag = jnp.concatenate([q_ref[4 * chunk + 2 * p + 1, block] for p in range(2)], axis=1)
-            if block == 0:
-                set_weights(wa, wb, chunk, real, imag, scale)
-            else:
-                set_weights(wc, wd, (block - 1) * 4 + chunk, real, imag, scale)
-    near[...] = jnp.zeros_like(near)
-    far[...] = jnp.zeros_like(far)
+    groups = Tiles(refs[:8]), Tiles(refs[8:16]), Tiles(refs[16:24])
+    packed_ref, image_ref, sums_ref, along_ref, *refs = refs[24:]
+    weights, images, grad_ref = (refs[0:2], refs[2:4], refs[4:6]), refs[6:9], refs[9]
+    for pair, blocks in zip(weights, BLOCKS):
+        for at, block in enumerate(blocks):
+            for chunk in range(4):
+                real = jnp.concatenate([q_ref[4 * chunk + 2 * p, block] for p in range(2)], axis=1)
+                imag = jnp.concatenate([q_ref[4 * chunk + 2 * p + 1, block] for p in range(2)], axis=1)
+                set_weights(*pair, at * 4 + chunk, real, imag, scale)
+    for image in images:
+        image[...] = jnp.zeros_like(image)
     sums_ref[...] = jnp.zeros_like(sums_ref)
 
     def forward(v, half, odd):
         for o in range(2):
-            for image, (c_ref, s_ref) in ((near, own.get(odd, o)), (far, tiles.get(odd, o))):
+            for image, group in zip(images, groups):
+                c_ref, s_ref = group.get(odd, o)
                 image[o] += dot_nn(v[0], c_ref[span(half), :]) + dot_nn(v[1], s_ref[span(half), :])
 
     def adjoint(half, odd):
         total = None
         for o in range(2):
-            for w_c, w_s, (c_ref, s_ref) in ((wa, wb, own.get(odd, o)), (wc, wd, tiles.get(odd, o))):
+            for (w_c, w_s), group in zip(weights, groups):
+                c_ref, s_ref = group.get(odd, o)
                 value = dot_nt(w_c[o], c_ref[span(half), :]) + dot_nt(w_s[o], s_ref[span(half), :])
                 total = value if total is None else total + value
         return total
@@ -284,8 +270,8 @@
         forward(v, *before)
         v = finish(half, odd, total)
     forward(v, 1, 1)
-    store_image(image_ref, near, 0)
-    store_image(image_ref, far, 1)
+    for image, blocks in zip(images, BLOCKS):
+        store_image(image_ref, image, blocks)
     gg = jnp.sum(sums_ref[0:1], axis=1, keepdims=True)
     gh = jnp.sum(sums_ref[1:2], axis=1, keepdims=True)
     along = coefficient(gg, gh)
@@ -456,26 +442,42 @@
     def held(width):
         return [pltpu.VMEM((512, width), BF16)] * 8
 
-    weights_near = [pltpu.VMEM((2, 32, 512), BF16)] * 2
-    weights_far = [pltpu.VMEM((2, 32, 1536), BF16)] * 2
-    images = [pltpu.VMEM((2, 32, 512), F32), pltpu.VMEM((2, 32, 1536), F32)]
+    def weights(count):
+        return [pltpu.VMEM((2, 32, 512 * count), BF16)] * 2
+
+    def coords(count):
+        return [pltpu.VMEM((8, 1024 * count), F32)]
+
+    images = [pltpu.VMEM((2, 32, 512 * len(blocks)), F32) for blocks in BLOCKS]
+    image_type = array(8, 2, 4, 16, 128, dtype=BF16)
+
+    def stay(tiles):
+        return [pltpu.with_memory_space_constraint(t, pltpu.VMEM) for t in tiles]
+
     *near, head = call(
-        functools.partial(own_kernel, scale),
+        functools.partial(head_kernel, scale, 1),
         "own",
         [VM] * 3,
         held(512) + [array(32, 1024)],
-        weights_near + [pltpu.VMEM((8, 1024), F32)],
-    )(packs[0], turns, points)
-    near = [pltpu.with_memory_space_constraint(t, pltpu.VMEM) for t in near]
-    image_type = array(8, 2, 4, 16, 128, dtype=BF16)
+        weights(1) + coords(1),
+    )(turns, points, packs[0])
+    near = stay(near)
+    *middle, head = call(
+        functools.partial(head_kernel, scale, 2),
+        "middle",
+        [VM] * 5,
+        held(1024) + [array(32, 1024)],
+        weights(2) + coords(2),
+    )(turns, points, packs[1], packs[3], head)
+    middle = stay(middle)
     *far, grad0, part0 = call(
         functools.partial(rest_kernel, scale),
         "rest",
-        [VM] * 14,
-        held(1536) + [array(32, 1024), image_type],
-        weights_far + images + [pltpu.VMEM((8, 3072), F32)],
-    )(turns, points, *packs[1:], head, *near)
-    far = [pltpu.with_memory_space_constraint(t, pltpu.VMEM) for t in far]
+        [VM] * 20,
+        held(512) + [array(32, 1024), image_type],
+        weights(1) + coords(1) + images,
+    )(turns, points, packs[2], head, *near, *middle)
+    tiles = near + middle + stay(far)
 
     parts = lax.all_to_all(part0.reshape(16, 4, 16, 128), "grid", 0, 0)
     image0, copies = call(
@@ -486,11 +488,11 @@
     packed, part1, sums, along = call(
         functools.partial(again_kernel, scale),
         "again",
-        [VM] * 18,
+        [VM] * 26,
         [array(64, 1024, dtype=BF16), image_type, array(8, EDGE), array(8, 128)],
-        weights_near + weights_far + images + [pltpu.VMEM((32, 1024), F32)],
+        weights(1) + weights(2) + weights(1) + images + [pltpu.VMEM((32, 1024), F32)],
         work=8 << 30,
-    )(rounded, grad0, *near, *far)
+    )(rounded, grad0, *tiles)
 
     near_hop = ahead(packed, 1)
     hops = [packed, near_hop, ahead(near_hop, 1), ahead(packed, 3)]

time: 125 us -> 121 us (0.968)
  blocking collectives: 58 us -> 56.4 us
  Pallas kernels: 35.4 us -> 34 us
    all_to_all x1, blocking collectives: 23.8 us -> 21.9 us  [body(): recv = lax.all_to_all(sent, ('mic', 'bin'), 0, 0)]
    pallas_call x3 -> x4, Pallas kernels: 31.5 us -> 30.1 us  [the longest x1 10 us: body(): call(functools.partial(head_kernel, scale, 2), 'middle', [VM] * 5, held(1...]
  transfers between devices with their start and end apart: 7 -> 7, of which waited for: 4 -> 2; matrix products, arithmetic and copies ran while one was open for 0% -> 0% of each run, Pallas kernels for 4% -> 12%
where the time goes in v6:
time: 121 us
  blocking collectives  56.4 us (47%)
  Pallas kernels  34 us (28%)
  starting transfers between devices  18.2 us (15%)
  waiting for transfers between devices  11.9 us (10%)
    all_to_all x1, blocking collectives, body(): recv = lax.all_to_all(sent, ('mic', 'bin'), 0, 0)  21.9 us
    ppermute x6, starting transfers between devices, ahead(): return lax.ppermute(x, 'mic', [((t + shift) % 4, t) for t in range(4)])  14.6 us
    all_to_all x1, blocking collectives, body(): parts = lax.all_to_all(part0.reshape(16, 4, 16, 128), 'grid', 0, 0)  14.1 us
    ppermute x6, waiting for transfers between devices, ahead(): return lax.ppermute(x, 'mic', [((t + shift) % 4, t) for t in range(4)])  11.9 us
    all_to_all x1, blocking collectives, body(): rounded = lax.all_to_all(copies, 'grid', 0, 0)  10.2 us
    all_to_all x1, blocking collectives, body(): parts = lax.all_to_all(part1.reshape(16, 4, 16, 128), 'grid', 0, 0)  10.2 us
    pallas_call x1, Pallas kernels, body(): call(functools.partial(head_kernel, scale, 2), 'middle', [VM] * 5, held(1...  10 us
    pallas_call x1, Pallas kernels, body(): call(functools.partial(again_kernel, scale), 'again', [VM] * 26, [array(6...  7.84 us
  transfers between devices with their start and end apart: 7, of which 2 were waited for; matrix products, arithmetic and copies ran while one was open for 0% of the time, Pallas kernels for 12%

profile of v6, /device:TPU:1, one launch (start us, length us, event | category | flops | bytes accessed | tf_op | source)
XLA Modules:
  0.0 121.1 jit_solution(11887942932817876086)
XLA Ops:
  0.6 1.3 %prepare.1 = (f32[1024,8]{1,0:T(8,128)S(1)}, f32[8,128]{1,0:T(8,128)S(1)}, bf16[48,1024]{1,0:T(8,128)(2,1)S(1)}, bf16[48,1024]{1,0:T(8,128)(2,1)S(1)}, bf16[48,1...) custom-call(s32[1]{0:T(128)} %bitcast.mic_ref, s32[1]{0:T(128)} %bitcast.1.bin_ref, ...), custom_call_target="tpu_custom_call" | custom-call | tf_op jit(solution)/shard_map/prepare/pallas_call | solution.py:426
  2.0 6.9 %collective-permute-start.1 = (bf16[48,1024]{1,0:T(8,128)(2,1)S(1)}, bf16[48,1024]{1,0:T(8,128)(2,1)S(1)}, u32[]{:S(2)}, u32[]{:S(2)}) collective-permute-start(bf16[48,1024]{1,0:T(8,128)(2,1)S(1)} %get-tuple-element.48), channel_id=1, source_target_pairs={{4,0},{8,4},{12,8},{0,12},{5,1},{9,5},{13,9},{1,13},{6,2},{10,6},{... | collective-permute-start | bytes 294920 | tf_op jit(solution)/shard_map/ppermute | solution.py:418
  8.9 0.0 collective-permute-start.2
  8.9 3.3 %collective-permute-start = (bf16[48,1024]{1,0:T(8,128)(2,1)S(1)}, bf16[48,1024]{1,0:T(8,128)(2,1)S(1)}, u32[]{:S(2)}, u32[]{:S(2)}) collective-permute-start(bf16[48,1024]{1,0:T(8,128)(2,1)S(1)} %get-tuple-element.47), channel_id=1, source_target_pairs={{8,0},{12,4},{0,8},{4,12},{9,1},{13,5},{1,9},{5,13},{10,2},{14,6},... | collective-permute-start | bytes 294920 | tf_op jit(solution)/shard_map/ppermute | solution.py:418
  12.1 5.1 %own.1 = (bf16[512,512]{1,0:T(8,128)(2,1)S(1)}, bf16[512,512]{1,0:T(8,128)(2,1)S(1)}, bf16[512,512]{1,0:T(8,128)(2,1)S(1)}, bf16[512,512]{1,0:T(8,128)(2,1)S(1)}...) custom-call(f32[8,128]{1,0:T(8,128)S(1)} %get-tuple-element.45.turns, ...), custom_call_target="tpu_custom_call" | custom-call | tf_op jit(solution)/shard_map/own/pallas_call | solution.py:457
  17.3 0.0 collective-permute-done.1.refs_0_.p1
  17.3 0.0 collective-permute-done.2.refs_1_.p3
  17.3 10.0 %middle.1 = (bf16[512,1024]{1,0:T(8,128)(2,1)S(1)}, bf16[512,1024]{1,0:T(8,128)(2,1)S(1)}, bf16[512,1024]{1,0:T(8,128)(2,1)S(1)}, bf16[512,1024]{1,0:T(8,128)(2,...) custom-call(f32[8,128]{1,0:T(8,128)S(1)} %get-tuple-element.45.turns, ...), custom_call_target="tpu_custom_call" | custom-call | tf_op jit(solution)/shard_map/middle/pallas_call | solution.py:465
  27.3 0.0 collective-permute-done.pack.p2
  27.3 7.2 %rest.1 = (bf16[512,512]{1,0:T(8,128)(2,1)S(1)}, bf16[512,512]{1,0:T(8,128)(2,1)S(1)}, bf16[512,512]{1,0:T(8,128)(2,1)S(1)}, bf16[512,512]{1,0:T(8,128)(2,1)S(1)...) custom-call(f32[8,128]{1,0:T(8,128)S(1)} %get-tuple-element.45.turns, ...), custom_call_target="tpu_custom_call" | custom-call | tf_op jit(solution)/shard_map/rest/pallas_call | solution.py:473
  34.5 14.1 %all_to_all.25.parts_ref = bf16[16,4,16,128]{3,2,1,0:T(8,128)(2,1)S(1)} all-to-all(bf16[16,4,16,128]{3,2,1,0:T(8,128)(2,1)S(1)} %bitcast.7), channel_id=1, replica_groups=mesh['grid'=16,'mic'=4,'bin'=4] {'grid'}, dimensions={0} | all-to-all | bytes 524288 | tf_op jit(solution)/shard_map/all_to_all | solution.py:482
  48.6 10.2 %all_to_all.26.q_ref = bf16[16,4,16,128]{3,2,1,0:T(8,128)(2,1)S(1)} all-to-all(bf16[16,4,16,128]{3,2,1,0:T(8,128)(2,1)S(1)} %get-tuple-element.70), channel_id=1, replica_groups=mesh['grid'=16,'mic'=4,'bin'=4] {'grid'}, dimensions={0} | all-to-all | bytes 524288 | tf_op jit(solution)/shard_map/all_to_all | solution.py:486
  58.8 7.8 %again.1 = (bf16[64,1024]{1,0:T(8,128)(2,1)S(1)}, bf16[8,2,4,16,128]{4,3,2,1,0:T(8,128)(2,1)S(1)}, f32[8,256]{1,0:T(8,128)S(1)}, f32[8,128]{1,0:T(8,128)S(1)}) custom-call(bf16[16,4,16,128]{3,2,1,0:T(8,128)(2,1)S(1)} %all_to_all.26.q_ref, f32[32,1024]{1,0:T(8,128)S(1)} %get-tuple-element.71.grad0_ref, bf16[512,512]{1,0:T(8,128)(2,1)S(1)} %get-tuple-element.53.refs_0_, ...), custom_call_target="tpu_custom_call" | custom-call | flops 8589934592 | tf_op jit(solution)/shard_map/again/pallas_call | solution.py:488
  66.6 10.2 %all_to_all.27.parts_ref = bf16[16,4,16,128]{3,2,1,0:T(8,128)(2,1)S(1)} all-to-all(bf16[16,4,16,128]{3,2,1,0:T(8,128)(2,1)S(1)} %bitcast.6), channel_id=1, replica_groups=mesh['grid'=16,'mic'=4,'bin'=4] {'grid'}, dimensions={0} | all-to-all | bytes 524288 | tf_op jit(solution)/shard_map/all_to_all | solution.py:499
  76.8 0.2 spread.1
  77.0 21.9 %all_to_all.28.recv_ref = bf16[16,48,128]{2,1,0:T(8,128)(2,1)S(1)} all-to-all(bf16[16,48,128]{2,1,0:T(8,128)(2,1)S(1)} %spread.1), channel_id=1, replica_groups=mesh['grid'=16,'mic'=4,'bin'=4] {'mic','bin'}, dimensions={0} | all-to-all | bytes 393216 | tf_op jit(solution)/shard_map/all_to_all | solution.py:507
  98.9 1.0 relay.1
  99.9 3.6 %all-to-all-start.4 = ((bf16[16,144,128]{2,1,0:T(8,128)(2,1)}), bf16[16,144,128]{2,1,0:T(8,128)(2,1)S(1)}, u32[]{:S(2)}, u32[]{:S(2)}) async-start(bf16[16,144,128]{2,1,0:T(8,128)(2,1)} %get-tuple-element.84), calls=%async_computation.4 | async-start | bytes 1179648 | tf_op jit(solution)/shard_map/all_to_all | solution.py:509
  103.5 0.6 collective-permute-start.3
  104.1 1.9 %collective-permute-start.5 = (bf16[64,1024]{1,0:T(8,128)(2,1)S(1)}, bf16[64,1024]{1,0:T(8,128)(2,1)S(1)}, u32[]{:S(2)}, u32[]{:S(2)}) collective-permute-start(bf16[64,1024]{1,0:T(8,128)(2,1)S(1)} %get-tuple-element.87.refs_0_), channel_id=1, source_target_pairs={{12,0},{0,4},{4,8},{8,12},{13,1},{1,5},{5,9},{9,13},{14,2},{2,6},{... | collective-permute-start | bytes 393224 | tf_op jit(solution)/shard_map/ppermute | solution.py:418
  106.0 6.5 %collective-permute-done.3.refs_1_ = bf16[64,1024]{1,0:T(8,128)(2,1)S(1)} collective-permute-done((bf16[64,1024]{1,0:T(8,128)(2,1)S(1)}, bf16[64,1024]{1,0:T(8,128)(2,1)S(1)}, u32[]{:S(2)}, u32[]{:S(2)}) %collective-permute-start.3) | collective-permute-done | bytes 131104 | tf_op jit(solution)/shard_map/ppermute | solution.py:418
  112.4 1.9 %collective-permute-start.4 = (bf16[64,1024]{1,0:T(8,128)(2,1)S(1)}, bf16[64,1024]{1,0:T(8,128)(2,1)S(1)}, u32[]{:S(2)}, u32[]{:S(2)}) collective-permute-start(bf16[64,1024]{1,0:T(8,128)(2,1)S(1)} %collective-permute-done.3.refs_1_), channel_id=1, source_target_pairs={{4,0},{8,4},{12,8},{0,12},{5,1},{9,5},{13,9},{1,13},{6,2},{10,6},{... | collective-permute-start | bytes 393224 | tf_op jit(solution)/shard_map/ppermute | solution.py:418
  114.4 0.0 collective-permute-done.5.refs_3_
  114.4 5.4 %collective-permute-done.4.refs_2_ = bf16[64,1024]{1,0:T(8,128)(2,1)S(1)} collective-permute-done((bf16[64,1024]{1,0:T(8,128)(2,1)S(1)}, bf16[64,1024]{1,0:T(8,128)(2,1)S(1)}, u32[]{:S(2)}, u32[]{:S(2)}) %collective-permute-start.4) | collective-permute-done | bytes 131104 | tf_op jit(solution)/shard_map/ppermute | solution.py:418
  119.8 0.0 all-to-all-done.4.recv_ref
  119.8 1.3 %last.1 = (f32[4,2,16,1024]{3,2,1,0:T(8,128)}, f32[4,2,16,1024]{3,2,1,0:T(8,128)}) custom-call(s32[1]{0:T(128)} %bitcast.mic_ref, bf16[16,144,128]{2,1,0:T(8,128)(2,1)S(1)} %all-to-all-done.4.recv_ref, f32[8,128]{1,0:T(8,128)S(1)} %get-tuple-element.85.along_ref, f32[4,32,1024]{2,1,0:T(8,128)S(1)} %get-tuple-element.86.press_ref, ...), custom_call_target="tpu_custom_call" | custom-call | tf_op jit(solution)/shard_map/last/pallas_call | solution.py:511
  (1 shorter events, 0.0 us)
Async XLA Ops:
  2.0 15.3 %collective-permute-start.1 = (bf16[48,1024]{1,0:T(8,128)(2,1)S(1)}, bf16[48,1024]{1,0:T(8,128)(2,1)S(1)}, u32[]{:S(2)}, u32[]{:S(2)}) collective-permute-start(bf16[48,1024]{1,0:T(8,128)(2,1)S(1)} %get-tuple-element.48), channel_id=1, source_target_pairs={{4,0},{8,4},{12,8},{0,12},{5,1},{9,5},{13,9},{1,13},{6,2},{10,6},{... | collective-permute-start | bytes 294920 | tf_op jit(solution)/shard_map/ppermute | solution.py:418
  8.9 8.4 %collective-permute-start.2 = (bf16[48,1024]{1,0:T(8,128)(2,1)S(1)}, bf16[48,1024]{1,0:T(8,128)(2,1)S(1)}, u32[]{:S(2)}, u32[]{:S(2)}) collective-permute-start(bf16[48,1024]{1,0:T(8,128)(2,1)S(1)} %get-tuple-element.49), channel_id=1, source_target_pairs={{12,0},{0,4},{4,8},{8,12},{13,1},{1,5},{5,9},{9,13},{14,2},{2,6},{... | collective-permute-start | bytes 294920 | tf_op jit(solution)/shard_map/ppermute | solution.py:418
  8.9 18.4 %collective-permute-start = (bf16[48,1024]{1,0:T(8,128)(2,1)S(1)}, bf16[48,1024]{1,0:T(8,128)(2,1)S(1)}, u32[]{:S(2)}, u32[]{:S(2)}) collective-permute-start(bf16[48,1024]{1,0:T(8,128)(2,1)S(1)} %get-tuple-element.47), channel_id=1, source_target_pairs={{8,0},{12,4},{0,8},{4,12},{9,1},{13,5},{1,9},{5,13},{10,2},{14,6},... | collective-permute-start | bytes 294920 | tf_op jit(solution)/shard_map/ppermute | solution.py:418
  99.9 19.8 %all-to-all-start.4 = ((bf16[16,144,128]{2,1,0:T(8,128)(2,1)}), bf16[16,144,128]{2,1,0:T(8,128)(2,1)S(1)}, u32[]{:S(2)}, u32[]{:S(2)}) async-start(bf16[16,144,128]{2,1,0:T(8,128)(2,1)} %get-tuple-element.84), calls=%async_computation.4 | async-start | bytes 1179648 | tf_op jit(solution)/shard_map/all_to_all | solution.py:509
  103.5 8.9 %collective-permute-start.3 = (bf16[64,1024]{1,0:T(8,128)(2,1)S(1)}, bf16[64,1024]{1,0:T(8,128)(2,1)S(1)}, u32[]{:S(2)}, u32[]{:S(2)}) collective-permute-start(bf16[64,1024]{1,0:T(8,128)(2,1)S(1)} %get-tuple-element.87.refs_0_), channel_id=1, source_target_pairs={{4,0},{8,4},{12,8},{0,12},{5,1},{9,5},{13,9},{1,13},{6,2},{10,6},{... | collective-permute-start | bytes 393224 | tf_op jit(solution)/shard_map/ppermute | solution.py:418
  104.1 10.3 %collective-permute-start.5 = (bf16[64,1024]{1,0:T(8,128)(2,1)S(1)}, bf16[64,1024]{1,0:T(8,128)(2,1)S(1)}, u32[]{:S(2)}, u32[]{:S(2)}) collective-permute-start(bf16[64,1024]{1,0:T(8,128)(2,1)S(1)} %get-tuple-element.87.refs_0_), channel_id=1, source_target_pairs={{12,0},{0,4},{4,8},{8,12},{13,1},{1,5},{5,9},{9,13},{14,2},{2,6},{... | collective-permute-start | bytes 393224 | tf_op jit(solution)/shard_map/ppermute | solution.py:418
  112.4 7.3 %collective-permute-start.4 = (bf16[64,1024]{1,0:T(8,128)(2,1)S(1)}, bf16[64,1024]{1,0:T(8,128)(2,1)S(1)}, u32[]{:S(2)}, u32[]{:S(2)}) collective-permute-start(bf16[64,1024]{1,0:T(8,128)(2,1)S(1)} %collective-permute-done.3.refs_1_), channel_id=1, source_target_pairs={{4,0},{8,4},{12,8},{0,12},{5,1},{9,5},{13,9},{1,13},{6,2},{10,6},{... | collective-permute-start | bytes 393224 | tf_op jit(solution)/shard_map/ppermute | solution.py:418

commit v7 on v6

--- a/solution.py
+++ b/solution.py
@@ -250,9 +250,9 @@
         for o in range(2):
             for (w_c, w_s), group in zip(weights, groups):
                 c_ref, s_ref = group.get(odd, o)
-                value = dot_nt(w_c[o], c_ref[span(half), :]) + dot_nt(w_s[o], s_ref[span(half), :])
+                value = dot_nt(c_ref[span(half), :], w_c[o]) + dot_nt(s_ref[span(half), :], w_s[o])
                 total = value if total is None else total + value
-        return total
+        return total.T
 
     def finish(half, odd, total):
         cols = span(half * 2 + odd)
@@ -310,6 +310,13 @@
 def unpack_sums(tile):
     tile = tile.astype(F32)
     return tile[0:6] + jnp.concatenate([tile[6:12, 0:64], jnp.zeros((6, 64), F32)], axis=1), tile[12:16]
+
+
+def sums_of(recv_ref, at):
+    total = recv_ref[0, at : at + 16].astype(F32)
+    for j in range(1, 16):
+        total += recv_ref[j, at : at + 16].astype(F32)
+    return unpack_sums(total)[0]
 
 
 def spread_kernel(mic_ref, grid_ref, parts_ref, q_ref, sums_ref, along_ref, p0, p1, p2, p3, out_ref, off_press, off_image):
@@ -344,9 +351,7 @@
 
 
 def relay_kernel(bin_ref, recv_ref, out_ref, along_ref):
-    sums = unpack_sums(recv_ref[0, 32:48])[0]
-    for j in range(1, 16):
-        sums += unpack_sums(recv_ref[j, 32:48])[0]
+    sums = sums_of(recv_ref, 32)
     rest = []
     for m in range(4):
         slot = m * 4 + bin_ref[0]
@@ -364,10 +369,7 @@
 
 def last_kernel(mic_ref, recv_ref, along_ref, press_ref, *refs):
     packs, (x_ref, r_ref) = refs[:4], refs[4:]
-    total = unpack_sums(recv_ref[0, 128:144])[0]
-    for j in range(1, 16):
-        total += unpack_sums(recv_ref[j, 128:144])[0]
-    total = jnp.sum(total, axis=1, keepdims=True)
+    total = jnp.sum(sums_of(recv_ref, 128), axis=1, keepdims=True)
     gg, gh, hh, qq, qp, pp = [total[i : i + 1] for i in range(6)]
     step0 = gg / qq
     norm1 = gg - 2.0 * step0 * gh + step0 * step0 * hh

time: 121 us -> 121 us (level)
  transfers between devices with their start and end apart: 7 -> 7, of which waited for: 2 -> 2; matrix products, arithmetic and copies ran while one was open for 0% -> 0% of each run, Pallas kernels for 12% -> 13%
where the time goes in v7:
time: 121 us
  blocking collectives  56.4 us (47%)
  Pallas kernels  33.4 us (28%)
  starting transfers between devices  18.4 us (15%)
  waiting for transfers between devices  11.9 us (10%)
    all_to_all x1, blocking collectives, body(): recv = lax.all_to_all(sent, ('mic', 'bin'), 0, 0)  21.9 us
    ppermute x6, starting transfers between devices, ahead(): return lax.ppermute(x, 'mic', [((t + shift) % 4, t) for t in range(4)])  14.6 us
    all_to_all x1, blocking collectives, body(): parts = lax.all_to_all(part0.reshape(16, 4, 16, 128), 'grid', 0, 0)  14.1 us
    ppermute x6, waiting for transfers between devices, ahead(): return lax.ppermute(x, 'mic', [((t + shift) % 4, t) for t in range(4)])  11.9 us
    all_to_all x1, blocking collectives, body(): rounded = lax.all_to_all(copies, 'grid', 0, 0)  10.2 us
    all_to_all x1, blocking collectives, body(): parts = lax.all_to_all(part1.reshape(16, 4, 16, 128), 'grid', 0, 0)  10.2 us
    pallas_call x1, Pallas kernels, body(): call(functools.partial(head_kernel, scale, 2), 'middle', [VM] * 5, held(1...  10 us
    pallas_call x1, Pallas kernels, body(): call(functools.partial(again_kernel, scale), 'again', [VM] * 26, [array(6...  7.22 us
  transfers between devices with their start and end apart: 7, of which 2 were waited for; matrix products, arithmetic and copies ran while one was open for 0% of the time, Pallas kernels for 13%

profile of v7, /device:TPU:1, one launch (start us, length us, event | category | flops | bytes accessed | tf_op | source)
XLA Modules:
  0.0 120.7 jit_solution(10042763214605793341)
XLA Ops:
  0.6 1.3 %prepare.1 = (f32[1024,8]{1,0:T(8,128)S(1)}, f32[8,128]{1,0:T(8,128)S(1)}, bf16[48,1024]{1,0:T(8,128)(2,1)S(1)}, bf16[48,1024]{1,0:T(8,128)(2,1)S(1)}, bf16[48,1...) custom-call(s32[1]{0:T(128)} %bitcast.mic_ref, s32[1]{0:T(128)} %bitcast.1.bin_ref, ...), custom_call_target="tpu_custom_call" | custom-call | tf_op jit(solution)/shard_map/prepare/pallas_call | solution.py:428
  2.0 6.9 %collective-permute-start.1 = (bf16[48,1024]{1,0:T(8,128)(2,1)S(1)}, bf16[48,1024]{1,0:T(8,128)(2,1)S(1)}, u32[]{:S(2)}, u32[]{:S(2)}) collective-permute-start(bf16[48,1024]{1,0:T(8,128)(2,1)S(1)} %get-tuple-element.48), channel_id=1, source_target_pairs={{4,0},{8,4},{12,8},{0,12},{5,1},{9,5},{13,9},{1,13},{6,2},{10,6},{... | collective-permute-start | bytes 294920 | tf_op jit(solution)/shard_map/ppermute | solution.py:420
  8.9 0.0 collective-permute-start.2
  8.9 3.3 %collective-permute-start = (bf16[48,1024]{1,0:T(8,128)(2,1)S(1)}, bf16[48,1024]{1,0:T(8,128)(2,1)S(1)}, u32[]{:S(2)}, u32[]{:S(2)}) collective-permute-start(bf16[48,1024]{1,0:T(8,128)(2,1)S(1)} %get-tuple-element.47), channel_id=1, source_target_pairs={{8,0},{12,4},{0,8},{4,12},{9,1},{13,5},{1,9},{5,13},{10,2},{14,6},... | collective-permute-start | bytes 294920 | tf_op jit(solution)/shard_map/ppermute | solution.py:420
  12.1 5.1 %own.1 = (bf16[512,512]{1,0:T(8,128)(2,1)S(1)}, bf16[512,512]{1,0:T(8,128)(2,1)S(1)}, bf16[512,512]{1,0:T(8,128)(2,1)S(1)}, bf16[512,512]{1,0:T(8,128)(2,1)S(1)}...) custom-call(f32[8,128]{1,0:T(8,128)S(1)} %get-tuple-element.45.turns, ...), custom_call_target="tpu_custom_call" | custom-call | tf_op jit(solution)/shard_map/own/pallas_call | solution.py:459
  17.3 0.0 collective-permute-done.1.refs_0_.p1
  17.3 0.0 collective-permute-done.2.refs_1_.p3
  17.3 10.0 %middle.1 = (bf16[512,1024]{1,0:T(8,128)(2,1)S(1)}, bf16[512,1024]{1,0:T(8,128)(2,1)S(1)}, bf16[512,1024]{1,0:T(8,128)(2,1)S(1)}, bf16[512,1024]{1,0:T(8,128)(2,...) custom-call(f32[8,128]{1,0:T(8,128)S(1)} %get-tuple-element.45.turns, ...), custom_call_target="tpu_custom_call" | custom-call | tf_op jit(solution)/shard_map/middle/pallas_call | solution.py:467
  27.3 0.0 collective-permute-done.pack.p2
  27.3 7.2 %rest.1 = (bf16[512,512]{1,0:T(8,128)(2,1)S(1)}, bf16[512,512]{1,0:T(8,128)(2,1)S(1)}, bf16[512,512]{1,0:T(8,128)(2,1)S(1)}, bf16[512,512]{1,0:T(8,128)(2,1)S(1)...) custom-call(f32[8,128]{1,0:T(8,128)S(1)} %get-tuple-element.45.turns, ...), custom_call_target="tpu_custom_call" | custom-call | tf_op jit(solution)/shard_map/rest/pallas_call | solution.py:475
  34.5 14.1 %all_to_all.25.parts_ref = bf16[16,4,16,128]{3,2,1,0:T(8,128)(2,1)S(1)} all-to-all(bf16[16,4,16,128]{3,2,1,0:T(8,128)(2,1)S(1)} %bitcast.7), channel_id=1, replica_groups=mesh['grid'=16,'mic'=4,'bin'=4] {'grid'}, dimensions={0} | all-to-all | bytes 524288 | tf_op jit(solution)/shard_map/all_to_all | solution.py:484
  48.6 10.2 %all_to_all.26.q_ref = bf16[16,4,16,128]{3,2,1,0:T(8,128)(2,1)S(1)} all-to-all(bf16[16,4,16,128]{3,2,1,0:T(8,128)(2,1)S(1)} %get-tuple-element.70), channel_id=1, replica_groups=mesh['grid'=16,'mic'=4,'bin'=4] {'grid'}, dimensions={0} | all-to-all | bytes 524288 | tf_op jit(solution)/shard_map/all_to_all | solution.py:488
  58.8 7.2 %again.1 = (bf16[64,1024]{1,0:T(8,128)(2,1)S(1)}, bf16[8,2,4,16,128]{4,3,2,1,0:T(8,128)(2,1)S(1)}, f32[8,256]{1,0:T(8,128)S(1)}, f32[8,128]{1,0:T(8,128)S(1)}) custom-call(bf16[16,4,16,128]{3,2,1,0:T(8,128)(2,1)S(1)} %all_to_all.26.q_ref, f32[32,1024]{1,0:T(8,128)S(1)} %get-tuple-element.71.grad0_ref, bf16[512,512]{1,0:T(8,128)(2,1)S(1)} %get-tuple-element.53.refs_0_, ...), custom_call_target="tpu_custom_call" | custom-call | flops 8589934592 | tf_op jit(solution)/shard_map/again/pallas_call | solution.py:490
  66.0 10.2 %all_to_all.27.parts_ref = bf16[16,4,16,128]{3,2,1,0:T(8,128)(2,1)S(1)} all-to-all(bf16[16,4,16,128]{3,2,1,0:T(8,128)(2,1)S(1)} %bitcast.6), channel_id=1, replica_groups=mesh['grid'=16,'mic'=4,'bin'=4] {'grid'}, dimensions={0} | all-to-all | bytes 524288 | tf_op jit(solution)/shard_map/all_to_all | solution.py:501
  76.2 0.2 spread.1
  76.4 21.9 %all_to_all.28.recv_ref = bf16[16,48,128]{2,1,0:T(8,128)(2,1)S(1)} all-to-all(bf16[16,48,128]{2,1,0:T(8,128)(2,1)S(1)} %spread.1), channel_id=1, replica_groups=mesh['grid'=16,'mic'=4,'bin'=4] {'mic','bin'}, dimensions={0} | all-to-all | bytes 393216 | tf_op jit(solution)/shard_map/all_to_all | solution.py:509
  98.3 1.0 relay.1
  99.3 3.8 %all-to-all-start.4 = ((bf16[16,144,128]{2,1,0:T(8,128)(2,1)}), bf16[16,144,128]{2,1,0:T(8,128)(2,1)S(1)}, u32[]{:S(2)}, u32[]{:S(2)}) async-start(bf16[16,144,128]{2,1,0:T(8,128)(2,1)} %get-tuple-element.84), calls=%async_computation.4 | async-start | bytes 1179648 | tf_op jit(solution)/shard_map/all_to_all | solution.py:511
  103.1 0.6 collective-permute-start.3
  103.7 1.9 %collective-permute-start.5 = (bf16[64,1024]{1,0:T(8,128)(2,1)S(1)}, bf16[64,1024]{1,0:T(8,128)(2,1)S(1)}, u32[]{:S(2)}, u32[]{:S(2)}) collective-permute-start(bf16[64,1024]{1,0:T(8,128)(2,1)S(1)} %get-tuple-element.87.refs_0_), channel_id=1, source_target_pairs={{12,0},{0,4},{4,8},{8,12},{13,1},{1,5},{5,9},{9,13},{14,2},{2,6},{... | collective-permute-start | bytes 393224 | tf_op jit(solution)/shard_map/ppermute | solution.py:420
  105.6 6.4 %collective-permute-done.3.refs_1_ = bf16[64,1024]{1,0:T(8,128)(2,1)S(1)} collective-permute-done((bf16[64,1024]{1,0:T(8,128)(2,1)S(1)}, bf16[64,1024]{1,0:T(8,128)(2,1)S(1)}, u32[]{:S(2)}, u32[]{:S(2)}) %collective-permute-start.3) | collective-permute-done | bytes 131104 | tf_op jit(solution)/shard_map/ppermute | solution.py:420
  112.0 2.0 %collective-permute-start.4 = (bf16[64,1024]{1,0:T(8,128)(2,1)S(1)}, bf16[64,1024]{1,0:T(8,128)(2,1)S(1)}, u32[]{:S(2)}, u32[]{:S(2)}) collective-permute-start(bf16[64,1024]{1,0:T(8,128)(2,1)S(1)} %collective-permute-done.3.refs_1_), channel_id=1, source_target_pairs={{4,0},{8,4},{12,8},{0,12},{5,1},{9,5},{13,9},{1,13},{6,2},{10,6},{... | collective-permute-start | bytes 393224 | tf_op jit(solution)/shard_map/ppermute | solution.py:420
  114.0 0.0 collective-permute-done.5.refs_3_
  114.0 5.4 %collective-permute-done.4.refs_2_ = bf16[64,1024]{1,0:T(8,128)(2,1)S(1)} collective-permute-done((bf16[64,1024]{1,0:T(8,128)(2,1)S(1)}, bf16[64,1024]{1,0:T(8,128)(2,1)S(1)}, u32[]{:S(2)}, u32[]{:S(2)}) %collective-permute-start.4) | collective-permute-done | bytes 131104 | tf_op jit(solution)/shard_map/ppermute | solution.py:420
  119.4 0.0 all-to-all-done.4.recv_ref
  119.4 1.3 %last.1 = (f32[4,2,16,1024]{3,2,1,0:T(8,128)}, f32[4,2,16,1024]{3,2,1,0:T(8,128)}) custom-call(s32[1]{0:T(128)} %bitcast.mic_ref, bf16[16,144,128]{2,1,0:T(8,128)(2,1)S(1)} %all-to-all-done.4.recv_ref, f32[8,128]{1,0:T(8,128)S(1)} %get-tuple-element.85.along_ref, f32[4,32,1024]{2,1,0:T(8,128)S(1)} %get-tuple-element.86.press_ref, ...), custom_call_target="tpu_custom_call" | custom-call | tf_op jit(solution)/shard_map/last/pallas_call | solution.py:513
  (1 shorter events, 0.0 us)
Async XLA Ops:
  2.0 15.3 %collective-permute-start.1 = (bf16[48,1024]{1,0:T(8,128)(2,1)S(1)}, bf16[48,1024]{1,0:T(8,128)(2,1)S(1)}, u32[]{:S(2)}, u32[]{:S(2)}) collective-permute-start(bf16[48,1024]{1,0:T(8,128)(2,1)S(1)} %get-tuple-element.48), channel_id=1, source_target_pairs={{4,0},{8,4},{12,8},{0,12},{5,1},{9,5},{13,9},{1,13},{6,2},{10,6},{... | collective-permute-start | bytes 294920 | tf_op jit(solution)/shard_map/ppermute | solution.py:420
  8.9 8.4 %collective-permute-start.2 = (bf16[48,1024]{1,0:T(8,128)(2,1)S(1)}, bf16[48,1024]{1,0:T(8,128)(2,1)S(1)}, u32[]{:S(2)}, u32[]{:S(2)}) collective-permute-start(bf16[48,1024]{1,0:T(8,128)(2,1)S(1)} %get-tuple-element.49), channel_id=1, source_target_pairs={{12,0},{0,4},{4,8},{8,12},{13,1},{1,5},{5,9},{9,13},{14,2},{2,6},{... | collective-permute-start | bytes 294920 | tf_op jit(solution)/shard_map/ppermute | solution.py:420
  8.9 18.4 %collective-permute-start = (bf16[48,1024]{1,0:T(8,128)(2,1)S(1)}, bf16[48,1024]{1,0:T(8,128)(2,1)S(1)}, u32[]{:S(2)}, u32[]{:S(2)}) collective-permute-start(bf16[48,1024]{1,0:T(8,128)(2,1)S(1)} %get-tuple-element.47), channel_id=1, source_target_pairs={{8,0},{12,4},{0,8},{4,12},{9,1},{13,5},{1,9},{5,13},{10,2},{14,6},... | collective-permute-start | bytes 294920 | tf_op jit(solution)/shard_map/ppermute | solution.py:420
  99.3 20.1 %all-to-all-start.4 = ((bf16[16,144,128]{2,1,0:T(8,128)(2,1)}), bf16[16,144,128]{2,1,0:T(8,128)(2,1)S(1)}, u32[]{:S(2)}, u32[]{:S(2)}) async-start(bf16[16,144,128]{2,1,0:T(8,128)(2,1)} %get-tuple-element.84), calls=%async_computation.4 | async-start | bytes 1179648 | tf_op jit(solution)/shard_map/all_to_all | solution.py:511
  103.1 8.9 %collective-permute-start.3 = (bf16[64,1024]{1,0:T(8,128)(2,1)S(1)}, bf16[64,1024]{1,0:T(8,128)(2,1)S(1)}, u32[]{:S(2)}, u32[]{:S(2)}) collective-permute-start(bf16[64,1024]{1,0:T(8,128)(2,1)S(1)} %get-tuple-element.87.refs_0_), channel_id=1, source_target_pairs={{4,0},{8,4},{12,8},{0,12},{5,1},{9,5},{13,9},{1,13},{6,2},{10,6},{... | collective-permute-start | bytes 393224 | tf_op jit(solution)/shard_map/ppermute | solution.py:420
  103.7 10.3 %collective-permute-start.5 = (bf16[64,1024]{1,0:T(8,128)(2,1)S(1)}, bf16[64,1024]{1,0:T(8,128)(2,1)S(1)}, u32[]{:S(2)}, u32[]{:S(2)}) collective-permute-start(bf16[64,1024]{1,0:T(8,128)(2,1)S(1)} %get-tuple-element.87.refs_0_), channel_id=1, source_target_pairs={{12,0},{0,4},{4,8},{8,12},{13,1},{1,5},{5,9},{9,13},{14,2},{2,6},{... | collective-permute-start | bytes 393224 | tf_op jit(solution)/shard_map/ppermute | solution.py:420
  112.0 7.4 %collective-permute-start.4 = (bf16[64,1024]{1,0:T(8,128)(2,1)S(1)}, bf16[64,1024]{1,0:T(8,128)(2,1)S(1)}, u32[]{:S(2)}, u32[]{:S(2)}) collective-permute-start(bf16[64,1024]{1,0:T(8,128)(2,1)S(1)} %collective-permute-done.3.refs_1_), channel_id=1, source_target_pairs={{4,0},{8,4},{12,8},{0,12},{5,1},{9,5},{13,9},{1,13},{6,2},{10,6},{... | collective-permute-start | bytes 393224 | tf_op jit(solution)/shard_map/ppermute | solution.py:420
